TPU v7x, 32 devices: a whole 2x2x4 slice. The times are simulated.
32 devices in a mesh: fsdp: 16 (over z, y, core), rep: 2 (over x).
Axes of the slice: x: 2, y: 2, z: 4, core: 2. Of those that a mesh axis runs over, the one named last changes fastest.
Arguments:
- tokens: bfloat16 [32768, 768], P(('fsdp', 'rep')), may hold values from -6 to 6
- segment: int32 [32, 4], P(('fsdp', 'rep')), may hold values from 0 to 3, as said below
- live: int32 [32, 4], P(('fsdp', 'rep')), may hold values from 0 to 1, as said below
- cotangent: bfloat16 [32768, 768], P(('fsdp', 'rep')), may hold values from -6 to 6
- ln1_gain: bfloat16 [2, 768], P(None, 'fsdp'), may hold values from 0.5 to 1.5
- ln1_bias: bfloat16 [2, 768], P(None, 'fsdp'), may hold values from -1.25 to 1.25
- q_weight: bfloat16 [2, 768, 768], P(None, 'fsdp'), may hold values from -0.21875 to 0.21875
- q_bias: bfloat16 [2, 768], P(None, 'fsdp'), may hold values from -1.25 to 1.25
- k_weight: bfloat16 [2, 768, 768], P(None, 'fsdp'), may hold values from -0.21875 to 0.21875
- v_weight: bfloat16 [2, 768, 768], P(None, 'fsdp'), may hold values from -0.21875 to 0.21875
- v_bias: bfloat16 [2, 768], P(None, 'fsdp'), may hold values from -1.25 to 1.25
- o_weight: bfloat16 [2, 768, 768], P(None, 'fsdp'), may hold values from -1.75 to 1.75
- o_bias: bfloat16 [2, 768], P(None, 'fsdp'), may hold values from -1.25 to 1.25
- ln2_gain: bfloat16 [2, 768], P(None, 'fsdp'), may hold values from 0.5 to 1.5
- ln2_bias: bfloat16 [2, 768], P(None, 'fsdp'), may hold values from -1.25 to 1.25
- up_weight: bfloat16 [2, 768, 3072], P(None, 'fsdp'), may hold values from -0.21875 to 0.21875
- up_bias: bfloat16 [2, 3072], P(None, 'fsdp'), may hold values from -1.25 to 1.25
- down_weight: bfloat16 [2, 3072, 768], P(None, 'fsdp'), may hold values from -0.109375 to 0.109375
- down_bias: bfloat16 [2, 768], P(None, 'fsdp'), may hold values from -1.25 to 1.25
Outputs:
- block_out: bfloat16 [32768, 768], P(('fsdp', 'rep'))
- input_grad: float32 [32768, 768], P(('fsdp', 'rep'))
- grad_ln1_gain: float32 [2, 768], P(None, 'fsdp')
- grad_ln1_bias: float32 [2, 768], P(None, 'fsdp')
- grad_q_weight: float32 [2, 768, 768], P(None, 'fsdp')
- grad_q_bias: float32 [2, 768], P(None, 'fsdp')
- grad_k_weight: float32 [2, 768, 768], P(None, 'fsdp')
- grad_v_weight: float32 [2, 768, 768], P(None, 'fsdp')
- grad_v_bias: float32 [2, 768], P(None, 'fsdp')
- grad_o_weight: float32 [2, 768, 768], P(None, 'fsdp')
- grad_o_bias: float32 [2, 768], P(None, 'fsdp')
- grad_ln2_gain: float32 [2, 768], P(None, 'fsdp')
- grad_ln2_bias: float32 [2, 768], P(None, 'fsdp')
- grad_up_weight: float32 [2, 768, 3072], P(None, 'fsdp')
- grad_up_bias: float32 [2, 3072], P(None, 'fsdp')
- grad_down_weight: float32 [2, 3072, 768], P(None, 'fsdp')
- grad_down_bias: float32 [2, 768], P(None, 'fsdp')
Inputs may be any that keep to these rules, and one draw needn't show every extreme that they name: `segment`: in each buffer either every slot has 0 (one image of 1024 tokens) or each slot has its own index (one image of 256 tokens a slot); exactly 12 buffers hold one image of 1024 tokens. Every slot of a buffer of one image is live, and the first slot of every buffer is live.
All inputs are finite; a program needn't handle non-finite values.
Results may differ from a plain program's by a relative error of at most 0.015.
Values may be sent and summed in bfloat16 or wider, within the bound.
A program may use at most 448 MiB of HBM per device.

v0:
```python
import jax
import jax.numpy as jnp
from jax import lax
from jax.sharding import PartitionSpec as P

HEADS = 16


EPSILON = 1e-06


def norm_apply(source, gain_vec, offset):
    mean_val = jnp.mean(source, axis=-1, keepdims=True)
    centered = source - mean_val
    variance = jnp.mean(centered * centered, axis=-1, keepdims=True)
    return centered * lax.rsqrt(variance + EPSILON) * gain_vec + offset


def gelu_tanh(source):
    return jax.nn.gelu(source, approximate=True)


def product(first, second):
    return jnp.dot(first, second, preferred_element_type=jnp.float32)


def left_inner(first, second):
    return lax.dot_general(
        first, second, (((0,), (0,)), ((), ())), preferred_element_type=jnp.float32
    )


def right_inner(first, second):
    return lax.dot_general(
        first, second, (((1,), (1,)), ((), ())), preferred_element_type=jnp.float32
    )


def column_sums(source):
    return jnp.sum(source.astype(jnp.float32), axis=0)


def masked_scores(query_heads, key_heads, seg_rows, seg_tok):
    factor = query_heads.shape[-1] ** (-0.5)
    scores = (
        jnp.einsum("qhd,khd->hqk", query_heads, key_heads, preferred_element_type=jnp.float32)
        * factor
    )
    same_image = seg_rows[:, None] == seg_tok[None, :]
    return jnp.where(same_image[None], scores, -1e30)


def attention_forward(queries, key_rows, value_rows, seg_tok):
    length, width = queries.shape
    head_dim = width // HEADS
    row_block = min(512, length)
    block_count = length // row_block
    key_heads = key_rows.reshape(length, HEADS, head_dim)
    value_heads = value_rows.reshape(length, HEADS, head_dim)
    query_blocks = queries.reshape(block_count, row_block, HEADS, head_dim)
    seg_blocks = seg_tok.reshape(block_count, row_block)

    def one_block(pair):
        query_heads, seg_rows = pair
        scores = masked_scores(query_heads, key_heads, seg_rows, seg_tok)
        row_peak = jnp.max(scores, axis=-1, keepdims=True)
        exponent = jnp.exp(scores - row_peak)
        row_total = jnp.sum(exponent, axis=-1, keepdims=True)
        probs_low = (exponent / row_total).astype(jnp.bfloat16)
        mixture = jnp.einsum(
            "hqk,khd->qhd", probs_low, value_heads, preferred_element_type=jnp.float32
        )
        return (mixture, row_peak + jnp.log(row_total))

    mixture, log_total = lax.map(one_block, (query_blocks, seg_blocks))
    return (mixture.reshape(length, width), log_total)


def attention_backward(queries, key_rows, value_rows, grad_mix, log_total, seg_tok):
    length, width = queries.shape
    head_dim = width // HEADS
    factor = head_dim ** (-0.5)
    row_block = min(512, length)
    block_count = length // row_block
    key_heads = key_rows.reshape(length, HEADS, head_dim)
    value_heads = value_rows.reshape(length, HEADS, head_dim)
    query_blocks = queries.reshape(block_count, row_block, HEADS, head_dim)
    grad_blocks = grad_mix.reshape(block_count, row_block, HEADS, head_dim)
    seg_blocks = seg_tok.reshape(block_count, row_block)

    def one_block(carry, items):
        key_grad, value_grad = carry
        query_heads, grad_heads, seg_rows, log_rows = items
        scores = masked_scores(query_heads, key_heads, seg_rows, seg_tok)
        attn_probs = jnp.exp(scores - log_rows)
        probs_low = attn_probs.astype(jnp.bfloat16)
        grad_probs = jnp.einsum(
            "qhd,khd->hqk", grad_heads, value_heads, preferred_element_type=jnp.float32
        )
        value_grad = value_grad + jnp.einsum(
            "hqk,qhd->khd", probs_low, grad_heads, preferred_element_type=jnp.float32
        )
        row_dot = jnp.sum(attn_probs * grad_probs, axis=-1, keepdims=True)
        grad_scores = (attn_probs * (grad_probs - row_dot)).astype(jnp.bfloat16)
        query_grad = (
            jnp.einsum("hqk,khd->qhd", grad_scores, key_heads, preferred_element_type=jnp.float32)
            * factor
        )
        key_grad = (
            key_grad
            + jnp.einsum(
                "hqk,qhd->khd", grad_scores, query_heads, preferred_element_type=jnp.float32
            )
            * factor
        )
        return ((key_grad, value_grad), query_grad)

    zeros_heads = jnp.zeros((length, HEADS, head_dim), jnp.float32)
    (key_grad, value_grad), query_grad = lax.scan(
        one_block, (zeros_heads, zeros_heads), (query_blocks, grad_blocks, seg_blocks, log_total)
    )
    return (
        query_grad.reshape(length, width),
        key_grad.reshape(length, width),
        value_grad.reshape(length, width),
    )


def block_forward(hidden, weights, seg_tok):
    (
        ln1_gain,
        ln1_bias,
        q_weight,
        q_bias,
        k_weight,
        v_weight,
        v_bias,
        o_weight,
        o_bias,
        ln2_gain,
        ln2_bias,
        up_weight,
        up_bias,
        down_weight,
        down_bias,
    ) = weights
    normed, norm_first = jax.vjp(
        norm_apply, hidden, ln1_gain.astype(jnp.float32), ln1_bias.astype(jnp.float32)
    )
    normed_low = normed.astype(jnp.bfloat16)
    queries = (product(normed_low, q_weight) + q_bias).astype(jnp.bfloat16)
    key_rows = product(normed_low, k_weight).astype(jnp.bfloat16)
    value_rows = (product(normed_low, v_weight) + v_bias).astype(jnp.bfloat16)
    mixture, log_total = attention_forward(queries, key_rows, value_rows, seg_tok)
    mixture_low = mixture.astype(jnp.bfloat16)
    midway = hidden + (product(mixture_low, o_weight) + o_bias)
    normed_mid, norm_second = jax.vjp(
        norm_apply, midway, ln2_gain.astype(jnp.float32), ln2_bias.astype(jnp.float32)
    )
    normed_mid_low = normed_mid.astype(jnp.bfloat16)
    upper_pre = product(normed_mid_low, up_weight) + up_bias
    active, gelu_back = jax.vjp(gelu_tanh, upper_pre)
    active_low = active.astype(jnp.bfloat16)
    result = midway + (product(active_low, down_weight) + down_bias)
    stored = (
        norm_first,
        normed_low,
        queries,
        key_rows,
        value_rows,
        log_total,
        mixture_low,
        norm_second,
        normed_mid_low,
        gelu_back,
        active_low,
    )
    return (result, stored)


def block_backward(hidden, weights, seg_tok, grad_out):
    (
        ln1_gain,
        ln1_bias,
        q_weight,
        q_bias,
        k_weight,
        v_weight,
        v_bias,
        o_weight,
        o_bias,
        ln2_gain,
        ln2_bias,
        up_weight,
        up_bias,
        down_weight,
        down_bias,
    ) = weights
    stored = block_forward(hidden, weights, seg_tok)[1]
    (
        norm_first,
        normed_low,
        queries,
        key_rows,
        value_rows,
        log_total,
        mixture_low,
        norm_second,
        normed_mid_low,
        gelu_back,
        active_low,
    ) = stored
    grad_low = grad_out.astype(jnp.bfloat16)
    grad_down = left_inner(active_low, grad_low)
    grad_down_bias = column_sums(grad_low)
    (grad_upper,) = gelu_back(right_inner(grad_low, down_weight))
    grad_upper_low = grad_upper.astype(jnp.bfloat16)
    grad_up = left_inner(normed_mid_low, grad_upper_low)
    grad_up_bias = column_sums(grad_upper_low)
    grad_mid_norm, grad_ln2_gain, grad_ln2_bias = norm_second(
        right_inner(grad_upper_low, up_weight)
    )
    grad_midway = grad_out + grad_mid_norm
    grad_attn_low = grad_midway.astype(jnp.bfloat16)
    grad_output_proj = left_inner(mixture_low, grad_attn_low)
    grad_output_bias = column_sums(grad_attn_low)
    grad_mix_low = right_inner(grad_attn_low, o_weight).astype(jnp.bfloat16)
    grad_queries, grad_keys, grad_values = attention_backward(
        queries, key_rows, value_rows, grad_mix_low, log_total, seg_tok
    )
    grad_q_low = grad_queries.astype(jnp.bfloat16)
    grad_k_low = grad_keys.astype(jnp.bfloat16)
    grad_v_low = grad_values.astype(jnp.bfloat16)
    grad_query_proj = left_inner(normed_low, grad_q_low)
    grad_query_bias = column_sums(grad_q_low)
    grad_key_proj = left_inner(normed_low, grad_k_low)
    grad_value_proj = left_inner(normed_low, grad_v_low)
    grad_value_bias = column_sums(grad_v_low)
    grad_normed = (
        right_inner(grad_q_low, q_weight)
        + right_inner(grad_k_low, k_weight)
        + right_inner(grad_v_low, v_weight)
    )
    grad_hidden_norm, grad_ln1_gain, grad_ln1_bias = norm_first(grad_normed)
    grad_hidden = grad_midway + grad_hidden_norm
    grad_terms = (
        grad_ln1_gain,
        grad_ln1_bias,
        grad_query_proj,
        grad_query_bias,
        grad_key_proj,
        grad_value_proj,
        grad_value_bias,
        grad_output_proj,
        grad_output_bias,
        grad_ln2_gain,
        grad_ln2_bias,
        grad_up,
        grad_up_bias,
        grad_down,
        grad_down_bias,
    )
    return (grad_hidden, grad_terms)


def on_device(
    tokens,
    segment,
    live,
    cotangent,
    ln1_gain,
    ln1_bias,
    q_weight,
    q_bias,
    k_weight,
    v_weight,
    v_bias,
    o_weight,
    o_bias,
    ln2_gain,
    ln2_bias,
    up_weight,
    up_bias,
    down_weight,
    down_bias,
):
    length = tokens.shape[0]
    slot_tokens = length // segment.shape[1]
    seg_tok = jnp.repeat(segment[0], slot_tokens)
    live_tok = jnp.repeat(live[0], slot_tokens).astype(jnp.float32)
    layers = ln1_gain.shape[0]
    hidden = tokens.astype(jnp.float32)
    saved = []
    fetched = []
    for layer_index in range(layers):
        weights = (
            lax.all_gather(ln1_gain[layer_index], "fsdp", axis=0, tiled=True),
            lax.all_gather(ln1_bias[layer_index], "fsdp", axis=0, tiled=True),
            lax.all_gather(q_weight[layer_index], "fsdp", axis=0, tiled=True),
            lax.all_gather(q_bias[layer_index], "fsdp", axis=0, tiled=True),
            lax.all_gather(k_weight[layer_index], "fsdp", axis=0, tiled=True),
            lax.all_gather(v_weight[layer_index], "fsdp", axis=0, tiled=True),
            lax.all_gather(v_bias[layer_index], "fsdp", axis=0, tiled=True),
            lax.all_gather(o_weight[layer_index], "fsdp", axis=0, tiled=True),
            lax.all_gather(o_bias[layer_index], "fsdp", axis=0, tiled=True),
            lax.all_gather(ln2_gain[layer_index], "fsdp", axis=0, tiled=True),
            lax.all_gather(ln2_bias[layer_index], "fsdp", axis=0, tiled=True),
            lax.all_gather(up_weight[layer_index], "fsdp", axis=0, tiled=True),
            lax.all_gather(up_bias[layer_index], "fsdp", axis=0, tiled=True),
            lax.all_gather(down_weight[layer_index], "fsdp", axis=0, tiled=True),
            lax.all_gather(down_bias[layer_index], "fsdp", axis=0, tiled=True),
        )
        saved.append(hidden)
        fetched.append(weights)
        hidden = block_forward(hidden, weights, seg_tok)[0]
    gradient = cotangent.astype(jnp.float32) * live_tok[:, None]
    summed_layers = [None] * layers
    for layer_index in reversed(range(layers)):
        weights = (
            lax.all_gather(ln1_gain[layer_index], "fsdp", axis=0, tiled=True),
            lax.all_gather(ln1_bias[layer_index], "fsdp", axis=0, tiled=True),
            lax.all_gather(q_weight[layer_index], "fsdp", axis=0, tiled=True),
            lax.all_gather(q_bias[layer_index], "fsdp", axis=0, tiled=True),
            lax.all_gather(k_weight[layer_index], "fsdp", axis=0, tiled=True),
            lax.all_gather(v_weight[layer_index], "fsdp", axis=0, tiled=True),
            lax.all_gather(v_bias[layer_index], "fsdp", axis=0, tiled=True),
            lax.all_gather(o_weight[layer_index], "fsdp", axis=0, tiled=True),
            lax.all_gather(o_bias[layer_index], "fsdp", axis=0, tiled=True),
            lax.all_gather(ln2_gain[layer_index], "fsdp", axis=0, tiled=True),
            lax.all_gather(ln2_bias[layer_index], "fsdp", axis=0, tiled=True),
            lax.all_gather(up_weight[layer_index], "fsdp", axis=0, tiled=True),
            lax.all_gather(up_bias[layer_index], "fsdp", axis=0, tiled=True),
            lax.all_gather(down_weight[layer_index], "fsdp", axis=0, tiled=True),
            lax.all_gather(down_bias[layer_index], "fsdp", axis=0, tiled=True),
        )
        gradient, grad_terms = block_backward(saved[layer_index], weights, seg_tok, gradient)
        sharded = (
            lax.psum_scatter(grad_terms[0], "fsdp", scatter_dimension=0, tiled=True),
            lax.psum_scatter(grad_terms[1], "fsdp", scatter_dimension=0, tiled=True),
            lax.psum_scatter(grad_terms[2], "fsdp", scatter_dimension=0, tiled=True),
            lax.psum_scatter(grad_terms[3], "fsdp", scatter_dimension=0, tiled=True),
            lax.psum_scatter(grad_terms[4], "fsdp", scatter_dimension=0, tiled=True),
            lax.psum_scatter(grad_terms[5], "fsdp", scatter_dimension=0, tiled=True),
            lax.psum_scatter(grad_terms[6], "fsdp", scatter_dimension=0, tiled=True),
            lax.psum_scatter(grad_terms[7], "fsdp", scatter_dimension=0, tiled=True),
            lax.psum_scatter(grad_terms[8], "fsdp", scatter_dimension=0, tiled=True),
            lax.psum_scatter(grad_terms[9], "fsdp", scatter_dimension=0, tiled=True),
            lax.psum_scatter(grad_terms[10], "fsdp", scatter_dimension=0, tiled=True),
            lax.psum_scatter(grad_terms[11], "fsdp", scatter_dimension=0, tiled=True),
            lax.psum_scatter(grad_terms[12], "fsdp", scatter_dimension=0, tiled=True),
            lax.psum_scatter(grad_terms[13], "fsdp", scatter_dimension=0, tiled=True),
            lax.psum_scatter(grad_terms[14], "fsdp", scatter_dimension=0, tiled=True),
        )
        halves = (
            lax.psum_scatter(
                sharded[0].astype(jnp.bfloat16), "rep", scatter_dimension=0, tiled=True
            ).astype(jnp.float32),
            lax.psum_scatter(
                sharded[1].astype(jnp.bfloat16), "rep", scatter_dimension=0, tiled=True
            ).astype(jnp.float32),
            lax.psum_scatter(
                sharded[2].astype(jnp.bfloat16), "rep", scatter_dimension=0, tiled=True
            ).astype(jnp.float32),
            lax.psum_scatter(
                sharded[3].astype(jnp.bfloat16), "rep", scatter_dimension=0, tiled=True
            ).astype(jnp.float32),
            lax.psum_scatter(
                sharded[4].astype(jnp.bfloat16), "rep", scatter_dimension=0, tiled=True
            ).astype(jnp.float32),
            lax.psum_scatter(
                sharded[5].astype(jnp.bfloat16), "rep", scatter_dimension=0, tiled=True
            ).astype(jnp.float32),
            lax.psum_scatter(
                sharded[6].astype(jnp.bfloat16), "rep", scatter_dimension=0, tiled=True
            ).astype(jnp.float32),
            lax.psum_scatter(
                sharded[7].astype(jnp.bfloat16), "rep", scatter_dimension=0, tiled=True
            ).astype(jnp.float32),
            lax.psum_scatter(
                sharded[8].astype(jnp.bfloat16), "rep", scatter_dimension=0, tiled=True
            ).astype(jnp.float32),
            lax.psum_scatter(
                sharded[9].astype(jnp.bfloat16), "rep", scatter_dimension=0, tiled=True
            ).astype(jnp.float32),
            lax.psum_scatter(
                sharded[10].astype(jnp.bfloat16), "rep", scatter_dimension=0, tiled=True
            ).astype(jnp.float32),
            lax.psum_scatter(
                sharded[11].astype(jnp.bfloat16), "rep", scatter_dimension=0, tiled=True
            ).astype(jnp.float32),
            lax.psum_scatter(
                sharded[12].astype(jnp.bfloat16), "rep", scatter_dimension=0, tiled=True
            ).astype(jnp.float32),
            lax.psum_scatter(
                sharded[13].astype(jnp.bfloat16), "rep", scatter_dimension=0, tiled=True
            ).astype(jnp.float32),
            lax.psum_scatter(
                sharded[14].astype(jnp.bfloat16), "rep", scatter_dimension=0, tiled=True
            ).astype(jnp.float32),
        )
        summed = (
            lax.all_gather(halves[0].astype(jnp.bfloat16), "rep", axis=0, tiled=True).astype(
                jnp.float32
            ),
            lax.all_gather(halves[1].astype(jnp.bfloat16), "rep", axis=0, tiled=True).astype(
                jnp.float32
            ),
            lax.all_gather(halves[2].astype(jnp.bfloat16), "rep", axis=0, tiled=True).astype(
                jnp.float32
            ),
            lax.all_gather(halves[3].astype(jnp.bfloat16), "rep", axis=0, tiled=True).astype(
                jnp.float32
            ),
            lax.all_gather(halves[4].astype(jnp.bfloat16), "rep", axis=0, tiled=True).astype(
                jnp.float32
            ),
            lax.all_gather(halves[5].astype(jnp.bfloat16), "rep", axis=0, tiled=True).astype(
                jnp.float32
            ),
            lax.all_gather(halves[6].astype(jnp.bfloat16), "rep", axis=0, tiled=True).astype(
                jnp.float32
            ),
            lax.all_gather(halves[7].astype(jnp.bfloat16), "rep", axis=0, tiled=True).astype(
                jnp.float32
            ),
            lax.all_gather(halves[8].astype(jnp.bfloat16), "rep", axis=0, tiled=True).astype(
                jnp.float32
            ),
            lax.all_gather(halves[9].astype(jnp.bfloat16), "rep", axis=0, tiled=True).astype(
                jnp.float32
            ),
            lax.all_gather(halves[10].astype(jnp.bfloat16), "rep", axis=0, tiled=True).astype(
                jnp.float32
            ),
            lax.all_gather(halves[11].astype(jnp.bfloat16), "rep", axis=0, tiled=True).astype(
                jnp.float32
            ),
            lax.all_gather(halves[12].astype(jnp.bfloat16), "rep", axis=0, tiled=True).astype(
                jnp.float32
            ),
            lax.all_gather(halves[13].astype(jnp.bfloat16), "rep", axis=0, tiled=True).astype(
                jnp.float32
            ),
            lax.all_gather(halves[14].astype(jnp.bfloat16), "rep", axis=0, tiled=True).astype(
                jnp.float32
            ),
        )
        summed_layers[layer_index] = summed
    stacked = tuple(
        (
            jnp.stack([summed_layers[depth_index][number] for depth_index in range(layers)])
            for number in range(15)
        )
    )
    return (hidden.astype(jnp.bfloat16), gradient) + stacked


def solution(mesh):
    return jax.shard_map(
        on_device,
        mesh=mesh,
        in_specs=(
            P(("fsdp", "rep"), None),
            P(("fsdp", "rep"), None),
            P(("fsdp", "rep"), None),
            P(("fsdp", "rep"), None),
            P(None, "fsdp"),
            P(None, "fsdp"),
            P(None, "fsdp", None),
            P(None, "fsdp"),
            P(None, "fsdp", None),
            P(None, "fsdp", None),
            P(None, "fsdp"),
            P(None, "fsdp", None),
            P(None, "fsdp"),
            P(None, "fsdp"),
            P(None, "fsdp"),
            P(None, "fsdp", None),
            P(None, "fsdp"),
            P(None, "fsdp", None),
            P(None, "fsdp"),
        ),
        out_specs=(
            P(("fsdp", "rep"), None),
            P(("fsdp", "rep"), None),
            P(None, "fsdp"),
            P(None, "fsdp"),
            P(None, "fsdp", None),
            P(None, "fsdp"),
            P(None, "fsdp", None),
            P(None, "fsdp", None),
            P(None, "fsdp"),
            P(None, "fsdp", None),
            P(None, "fsdp"),
            P(None, "fsdp"),
            P(None, "fsdp"),
            P(None, "fsdp", None),
            P(None, "fsdp"),
            P(None, "fsdp", None),
            P(None, "fsdp"),
        ),
        check_vma=False,
    )
```

profile of v0, /device:TPU:0, one launch (start us, length us, event | category | flops | bytes accessed | tf_op | source)
XLA Modules:
  0.0 2065.4 jit_solution(11418018425222577919)
XLA Ops:
  29.2 64.2 %all-reduce.73 = (bf16[768]{0:T(1024)(128)(2,1)S(1)}, bf16[768]{0:T(1024)(128)(2,1)S(1)}, bf16[768]{0:T(1024)(128)(2,1)S(1)}, bf16[768]{0:T(1024)(128)(2,1)S(1)}...) all-reduce(bf16[768]{0:T(1024)(128)(2,1)S(1)} %dynamic-update-slice, ...), channel_id=5, replica_groups=mesh['fsdp'=16,'rep'=2] {'fsdp'}, use_global_device_ids=true, to_apply=%add.2 | all-reduce | flops 18432 | bytes 73728
  116.7 15.5 all-gather.47.cloned.1.call-done
  138.0 138.4 %while.78 = (s32[]{:T(128)}, bf16[2,512,16,48]{1,3,2,0:T(8,128)(2,1)}, s32[2,512]{1,0:T(2,128)S(1)}, bf16[2,512,16,48]{1,3,2,0:T(8,128)(2,1)S(1)}, bf16[1024,16,...) while((s32[]{:T(128)}, ...), condition=%wide.region_5.6_spmd.clone, body=%wide.region_2.5_spmd.clone.sunk | while | flops 1678246912 | bytes 140859520 | solution.py:75
  139.5 13.2 fusion.384
  152.7 39.6 %fusion.385 = (f32[16,512]{1,0:T(8,128)S(1)}, f32[16,512,1024]{2,1,0:T(8,128)}) fusion(f32[16,512,1024]{2,1,0:T(8,128)} %fusion.384, pred[512,1024]{1,0:T(8,128)(4,1)} %broadcast_compare_fusion.12), kind=kOutput, calls=%fused_computation.400.clone.1 | output fusion | flops 50332672 | bytes 67665920 | tf_op jit(solution)/shard_map/while/body/eval_jaxpr/sub | solution.py:67
  192.3 15.2 bitcast_dynamic-update-slice_fusion.16
  208.7 13.4 fusion.384
  222.1 39.0 %fusion.385 = (f32[16,512]{1,0:T(8,128)S(1)}, f32[16,512,1024]{2,1,0:T(8,128)}) fusion(f32[16,512,1024]{2,1,0:T(8,128)} %fusion.384, pred[512,1024]{1,0:T(8,128)(4,1)} %broadcast_compare_fusion.12), kind=kOutput, calls=%fused_computation.400.clone.1 | output fusion | flops 50332672 | bytes 67665920 | tf_op jit(solution)/shard_map/while/body/eval_jaxpr/sub | solution.py:67
  261.0 14.9 bitcast_dynamic-update-slice_fusion.16
  288.2 18.4 fusion.280
  309.3 11.9 all-gather.55.cloned.1.call-done
  327.9 33.0 %all-gather.57.cloned.1.call-done = bf16[1,768,768]{2,1,0:T(8,128)(2,1)} async-done(((bf16[1,48,768]{2,1,0:T(8,128)(2,1)}), bf16[1,768,768]{2,1,0:T(8,128)(2,1)}) %all-gather.57.cloned.1.call-update) | async-done | bytes 1179664 | tf_op jit(solution)/shard_map/all_gather | solution.py:301
  364.0 36.5 %all-gather.59.cloned.1.call-done = bf16[1,768,768]{2,1,0:T(8,128)(2,1)} async-done(((bf16[1,48,768]{2,1,0:T(8,128)(2,1)}), bf16[1,768,768]{2,1,0:T(8,128)(2,1)}) %all-gather.59.cloned.1.call-update) | async-done | bytes 1179664 | tf_op jit(solution)/shard_map/all_gather | solution.py:302
  406.1 94.1 %while.80 = (s32[]{:T(128)}, bf16[2,512,16,48]{1,3,2,0:T(8,128)(2,1)}, f32[2,16,512,1]{2,1,3,0:T(8,128)S(1)}, s32[2,512]{1,0:T(2,128)S(1)}, bf16[2,512,16,48]{1,...) while((s32[]{:T(128)}, ...), condition=%wide.region_19.20_spmd.clone, body=%wide.region_16.19_spmd.clone.sunk | while | flops 1711792128 | bytes 127424720 | solution.py:75
  406.8 15.4 fusion.393
  422.2 15.2 fusion.394
  437.5 14.3 bitcast_dynamic-update-slice_fusion.18
  453.4 15.4 fusion.393
  468.8 15.6 fusion.394
  484.4 14.7 bitcast_dynamic-update-slice_fusion.18
  511.3 11.6 fusion.143
  523.0 27.0 %all-gather.65.cloned.1.call-done = bf16[1,3072,768]{2,1,0:T(8,128)(2,1)} async-done(((bf16[1,192,768]{2,1,0:T(8,128)(2,1)}), bf16[1,3072,768]{2,1,0:T(8,128)(2,1)}) %all-gather.65.cloned.1.call-update) | async-done | bytes 4718608 | tf_op jit(solution)/shard_map/all_gather | solution.py:310
  550.0 17.4 convert_reduce_fusion
  605.0 207.8 %while.82 = (s32[]{:T(128)}, f32[1024,16,48]{0,2,1:T(8,128)}, f32[1024,16,48]{0,2,1:T(8,128)}, bf16[2,512,16,48]{1,3,2,0:T(8,128)(2,1)}, bf16[2,512,16,48]{1,3,2...) while((s32[]{:T(128)}, f32[1024,16,48]{0,2,1:T(8,128)}, ...), condition=%wide.region_26.27_spmd.clone, body=%wide.region_24.26_spmd.clone.sunk | while | flops 4157202432 | bytes 343136448 | solution.py:119
  605.7 15.2 fusion.408
  620.9 17.2 bitcast_add_fusion.9
  638.1 25.9 %multiply_reduce_fusion.15 = (f32[16,512]{1,0:T(8,128)S(1)}, f32[16,512,1024]{2,1,0:T(8,128)}) fusion(f32[16,512,1024]{2,1,0:T(8,128)} %fusion.408, f32[16,512]{1,0:T(8,128)S(1)} %dynamic-slice_bitcast_fusion.4, pred[512,1024]{1,0:T(8,128)(4,1)S(1)} %broadcast_compare_fusion.16, bf16[1024,16,48]{0,2,1:T(8,128)(2,1)} %get-tuple-element.1414, ...), kind=kOutput, calls=%fused_computation.79.clone.1 | convolution fusion | flops 847241216 | bytes 70057984 | tf_op jit(solution)/shard_map/while/body/eval_jaxpr/qhd,khd->hqk/dot_general | solution.py:97
  664.0 27.8 %multiply_convert_fusion.8 = bf16[16,512,1024]{2,1,0:T(8,128)(2,1)} fusion(f32[16,512,1024]{2,1,0:T(8,128)} %get-tuple-element.1262, f32[16,512,1024]{2,1,0:T(8,128)} %fusion.408, f32[16,512]{1,0:T(8,128)S(1)} %get-tuple-element.1263, f32[16,512]{1,0:T(8,128)S(1)} %dynamic-slice_bitcast_fusion.4, pred[512,1024]{1,0:T(8,128)(4,1)S(1)} %broadcast_compare_fusion.16), kind=kLoop, calls=%fused_computation.78.clone.1 | loop fusion | flops 50331648 | bytes 84475904 | tf_op jit(solution)/shard_map/while/body/eval_jaxpr/convert_element_type | solution.py:104
  709.0 14.3 fusion.408
  723.3 17.8 bitcast_add_fusion.9
  741.1 25.8 %multiply_reduce_fusion.15 = (f32[16,512]{1,0:T(8,128)S(1)}, f32[16,512,1024]{2,1,0:T(8,128)}) fusion(f32[16,512,1024]{2,1,0:T(8,128)} %fusion.408, f32[16,512]{1,0:T(8,128)S(1)} %dynamic-slice_bitcast_fusion.4, pred[512,1024]{1,0:T(8,128)(4,1)S(1)} %broadcast_compare_fusion.16, bf16[1024,16,48]{0,2,1:T(8,128)(2,1)} %get-tuple-element.1414, ...), kind=kOutput, calls=%fused_computation.79.clone.1 | convolution fusion | flops 847241216 | bytes 70057984 | tf_op jit(solution)/shard_map/while/body/eval_jaxpr/qhd,khd->hqk/dot_general | solution.py:97
  766.9 27.8 %multiply_convert_fusion.8 = bf16[16,512,1024]{2,1,0:T(8,128)(2,1)} fusion(f32[16,512,1024]{2,1,0:T(8,128)} %get-tuple-element.1262, f32[16,512,1024]{2,1,0:T(8,128)} %fusion.408, f32[16,512]{1,0:T(8,128)S(1)} %get-tuple-element.1263, f32[16,512]{1,0:T(8,128)S(1)} %dynamic-slice_bitcast_fusion.4, pred[512,1024]{1,0:T(8,128)(4,1)S(1)} %broadcast_compare_fusion.16), kind=kLoop, calls=%fused_computation.78.clone.1 | loop fusion | flops 50331648 | bytes 84475904 | tf_op jit(solution)/shard_map/while/body/eval_jaxpr/convert_element_type | solution.py:104
  822.8 94.1 %while.81 = (s32[]{:T(128)}, bf16[2,512,16,48]{1,3,2,0:T(8,128)(2,1)}, f32[2,16,512,1]{2,1,3,0:T(8,128)S(1)}, s32[2,512]{1,0:T(2,128)S(1)}, bf16[2,512,16,48]{1,...) while((s32[]{:T(128)}, ...), condition=%wide.region_32.33_spmd.clone, body=%wide.region_29.32_spmd.clone.sunk | while | flops 1711792128 | bytes 127424720 | solution.py:75
  823.2 16.2 fusion.397
  839.4 15.3 fusion.398
  854.7 14.4 bitcast_dynamic-update-slice_fusion.20
  870.7 15.4 fusion.397
  886.2 15.1 fusion.398
  901.3 14.2 bitcast_dynamic-update-slice_fusion.20
  966.5 16.4 convert_reduce_fusion.1
  1021.2 207.6 %while.83 = (s32[]{:T(128)}, f32[1024,16,48]{0,2,1:T(8,128)}, f32[1024,16,48]{0,2,1:T(8,128)}, bf16[2,512,16,48]{1,3,2,0:T(8,128)(2,1)}, bf16[2,512,16,48]{1,3,2...) while((s32[]{:T(128)}, f32[1024,16,48]{0,2,1:T(8,128)}, ...), condition=%wide.region_39.40_spmd.clone, body=%wide.region_37.39_spmd.clone.sunk | while | flops 4157202432 | bytes 343136448 | solution.py:119
  1021.9 14.5 fusion.418
  1036.4 17.3 bitcast_add_fusion.11
  1053.6 25.9 %multiply_reduce_fusion.16 = (f32[16,512]{1,0:T(8,128)S(1)}, f32[16,512,1024]{2,1,0:T(8,128)}) fusion(f32[16,512,1024]{2,1,0:T(8,128)} %fusion.418, f32[16,512]{1,0:T(8,128)S(1)} %dynamic-slice_bitcast_fusion.5, pred[512,1024]{1,0:T(8,128)(4,1)S(1)} %broadcast_compare_fusion.17, bf16[1024,16,48]{0,2,1:T(8,128)(2,1)} %get-tuple-element.1453, ...), kind=kOutput, calls=%fused_computation.108.clone.1 | convolution fusion | flops 847241216 | bytes 70057984 | tf_op jit(solution)/shard_map/while/body/eval_jaxpr/qhd,khd->hqk/dot_general | solution.py:97
  1079.6 28.1 %multiply_convert_fusion.9 = bf16[16,512,1024]{2,1,0:T(8,128)(2,1)} fusion(f32[16,512,1024]{2,1,0:T(8,128)} %get-tuple-element.1275, f32[16,512,1024]{2,1,0:T(8,128)} %fusion.418, f32[16,512]{1,0:T(8,128)S(1)} %get-tuple-element.1276, f32[16,512]{1,0:T(8,128)S(1)} %dynamic-slice_bitcast_fusion.5, pred[512,1024]{1,0:T(8,128)(4,1)S(1)} %broadcast_compare_fusion.17), kind=kLoop, calls=%fused_computation.107.clone.1 | loop fusion | flops 50331648 | bytes 84475904 | tf_op jit(solution)/shard_map/while/body/eval_jaxpr/convert_element_type | solution.py:104
  1125.1 14.3 fusion.418
  1139.4 17.9 bitcast_add_fusion.11
  1157.3 25.8 %multiply_reduce_fusion.16 = (f32[16,512]{1,0:T(8,128)S(1)}, f32[16,512,1024]{2,1,0:T(8,128)}) fusion(f32[16,512,1024]{2,1,0:T(8,128)} %fusion.418, f32[16,512]{1,0:T(8,128)S(1)} %dynamic-slice_bitcast_fusion.5, pred[512,1024]{1,0:T(8,128)(4,1)S(1)} %broadcast_compare_fusion.17, bf16[1024,16,48]{0,2,1:T(8,128)(2,1)} %get-tuple-element.1453, ...), kind=kOutput, calls=%fused_computation.108.clone.1 | convolution fusion | flops 847241216 | bytes 70057984 | tf_op jit(solution)/shard_map/while/body/eval_jaxpr/qhd,khd->hqk/dot_general | solution.py:97
  1183.1 27.8 %multiply_convert_fusion.9 = bf16[16,512,1024]{2,1,0:T(8,128)(2,1)} fusion(f32[16,512,1024]{2,1,0:T(8,128)} %get-tuple-element.1275, f32[16,512,1024]{2,1,0:T(8,128)} %fusion.418, f32[16,512]{1,0:T(8,128)S(1)} %get-tuple-element.1276, f32[16,512]{1,0:T(8,128)S(1)} %dynamic-slice_bitcast_fusion.5, pred[512,1024]{1,0:T(8,128)(4,1)S(1)} %broadcast_compare_fusion.17), kind=kLoop, calls=%fused_computation.107.clone.1 | loop fusion | flops 50331648 | bytes 84475904 | tf_op jit(solution)/shard_map/while/body/eval_jaxpr/convert_element_type | solution.py:104
  1248.9 14.1 fusion.129
  1278.0 13.7 fusion.128
  1301.9 62.7 %reduce-scatter.41.cloned.1.call-done = f32[48,768]{1,0:T(8,128)} async-done(((f32[768,768]{1,0:T(8,128)}), f32[48,768]{1,0:T(8,128)}) %reduce-scatter.41.cloned.1.call-update) | async-done | bytes 147472 | tf_op jit(solution)/shard_map/reduce_scatter | solution.py:343
  1370.7 60.0 %reduce-scatter.33.cloned.1.call-done = f32[48,768]{1,0:T(8,128)} async-done(((f32[768,768]{1,0:T(8,128)}), f32[48,768]{1,0:T(8,128)}) %reduce-scatter.33.cloned.1.call-update) | async-done | bytes 147472 | tf_op jit(solution)/shard_map/reduce_scatter | solution.py:342
  1445.7 145.3 %while.79 = (s32[]{:T(128)}, bf16[2,512,16,48]{1,3,2,0:T(8,128)(2,1)}, s32[2,512]{1,0:T(2,128)S(1)}, bf16[2,512,16,48]{1,3,2,0:T(8,128)(2,1)S(1)}, bf16[1024,16,...) while((s32[]{:T(128)}, ...), condition=%wide.region_13.14_spmd.clone, body=%wide.region_10.13_spmd.clone.sunk | while | flops 1678246912 | bytes 140859520 | solution.py:75
  1447.2 14.8 fusion.389
  1462.0 39.4 %fusion.390 = (f32[16,512]{1,0:T(8,128)S(1)}, f32[16,512,1024]{2,1,0:T(8,128)}) fusion(f32[16,512,1024]{2,1,0:T(8,128)} %fusion.389, pred[512,1024]{1,0:T(8,128)(4,1)} %broadcast_compare_fusion.13), kind=kOutput, calls=%fused_computation.401.clone.1 | output fusion | flops 50332672 | bytes 67665920 | tf_op jit(solution)/shard_map/while/body/eval_jaxpr/sub | solution.py:67
  1501.3 15.1 bitcast_dynamic-update-slice_fusion.17
  1517.7 13.4 fusion.389
  1531.1 44.3 %fusion.390 = (f32[16,512]{1,0:T(8,128)S(1)}, f32[16,512,1024]{2,1,0:T(8,128)}) fusion(f32[16,512,1024]{2,1,0:T(8,128)} %fusion.389, pred[512,1024]{1,0:T(8,128)(4,1)} %broadcast_compare_fusion.13), kind=kOutput, calls=%fused_computation.401.clone.1 | output fusion | flops 50332672 | bytes 67665920 | tf_op jit(solution)/shard_map/while/body/eval_jaxpr/sub | solution.py:67
  1575.4 15.4 bitcast_dynamic-update-slice_fusion.17
  1605.5 62.4 %all-reduce.72 = (bf16[768]{0:T(1024)(128)(2,1)S(1)}, bf16[768]{0:T(1024)(128)(2,1)S(1)}, bf16[768]{0:T(1024)(128)(2,1)S(1)}, bf16[768]{0:T(1024)(128)(2,1)S(1)}...) all-reduce(f32[768]{0:T(1024)S(1)} %copy-done.121, ...), channel_id=34, replica_groups=mesh['fsdp'=16,'rep'=2] {'fsdp'}, use_global_device_ids=true, to_apply=%region_46.47.clone | all-reduce | flops 18432 | bytes 110592
  1691.0 19.8 add_convert_fusion.2
  1730.2 47.3 %reduce-scatter.65.cloned.1.call-done = f32[192,768]{1,0:T(8,128)} async-done(((f32[3072,768]{1,0:T(8,128)}), f32[192,768]{1,0:T(8,128)}) %reduce-scatter.65.cloned.1.call-update) | async-done | bytes 589840 | tf_op jit(solution)/shard_map/reduce_scatter | solution.py:351
  1883.6 109.7 %reduce-scatter.57.cloned.1.call-done = f32[48,3072]{1,0:T(8,128)} async-done(((f32[768,3072]{1,0:T(8,128)}), f32[48,3072]{1,0:T(8,128)}) %reduce-scatter.57.cloned.1.call-update) | async-done | bytes 589840 | tf_op jit(solution)/shard_map/reduce_scatter | solution.py:349
  (835 shorter events, 597.0 us)
Async XLA Ops:
  7.3 17.3 copy-start.157
  7.3 17.3 copy-start.147
  7.3 17.3 copy-start.158
  7.3 93.8 %copy-start.52 = (bf16[1024,768]{1,0:T(8,128)(2,1)S(1)}, bf16[1024,768]{1,0:T(8,128)(2,1)}, u32[]{:S(2)}) copy-start(bf16[1024,768]{1,0:T(8,128)(2,1)} %param.31) | copy-start | bytes 4718596
  7.3 98.1 %all-gather.43.cloned.1.call-start = ((), (), s32[]{:S(2)}) async-start(), calls=%async_computation.48 | async-start | bytes 1253376 | tf_op jit(solution)/shard_map/all_gather | solution.py:299
  9.1 104.2 %all-gather.45.cloned.1.call-start = ((), (), s32[]{:S(2)}) async-start(), calls=%async_computation.49 | async-start | bytes 1253376 | tf_op jit(solution)/shard_map/all_gather | solution.py:301
  10.8 121.4 %all-gather.47.cloned.1.call-start = ((), (), s32[]{:S(2)}) async-start(), calls=%async_computation.50 | async-start | bytes 1253376 | tf_op jit(solution)/shard_map/all_gather | solution.py:302
  12.5 269.7 %all-gather.49.cloned.1.call-start = ((), (), s32[]{:S(2)}) async-start(), calls=%async_computation.51 | async-start | bytes 1253376 | tf_op jit(solution)/shard_map/all_gather | solution.py:304
  14.1 274.0 %all-gather.51.cloned.1.call-start = ((), (), s32[]{:S(2)}) async-start(), calls=%async_computation.52 | async-start | bytes 5013504 | tf_op jit(solution)/shard_map/all_gather | solution.py:308
  16.1 272.0 %all-gather.53.cloned.1.call-start = ((), (), s32[]{:S(2)}) async-start(), calls=%async_computation.53 | async-start | bytes 5013504 | tf_op jit(solution)/shard_map/all_gather | solution.py:310
  17.1 304.2 %all-gather.55.cloned.1.call-start = ((), (), s32[]{:S(2)}) async-start(), calls=%async_computation.54 | async-start | bytes 1253376 | tf_op jit(solution)/shard_map/all_gather | solution.py:299
  17.8 343.0 %all-gather.57.cloned.1.call-start = ((), (), s32[]{:S(2)}) async-start(), calls=%async_computation.55 | async-start | bytes 1253376 | tf_op jit(solution)/shard_map/all_gather | solution.py:301
  18.6 381.9 %all-gather.59.cloned.1.call-start = ((), (), s32[]{:S(2)}) async-start(), calls=%async_computation.56 | async-start | bytes 1253376 | tf_op jit(solution)/shard_map/all_gather | solution.py:302
  19.3 485.6 %all-gather.61.cloned.1.call-start = ((), (), s32[]{:S(2)}) async-start(), calls=%async_computation.57 | async-start | bytes 1253376 | tf_op jit(solution)/shard_map/all_gather | solution.py:304
  19.9 491.4 %all-gather.63.cloned.1.call-start = ((), (), s32[]{:S(2)}) async-start(), calls=%async_computation.58 | async-start | bytes 5013504 | tf_op jit(solution)/shard_map/all_gather | solution.py:308
  20.6 529.4 %all-gather.65.cloned.1.call-start = ((), (), s32[]{:S(2)}) async-start(), calls=%async_computation.59 | async-start | bytes 5013504 | tf_op jit(solution)/shard_map/all_gather | solution.py:310
  21.2 1270.7 %reduce-scatter.53.cloned.1.call-start = ((), (), s32[]{:S(2)}) async-start(), calls=%async_computation.38 | async-start | bytes 2506752 | tf_op jit(solution)/shard_map/reduce_scatter | solution.py:345
  93.4 38.8 %copy-start.99 = (f32[768]{0:T(1024)}, f32[768]{0:T(1024)S(1)}, u32[]{:S(2)}) copy-start(f32[768]{0:T(1024)S(1)} %convert_element_type.601) | copy-start | bytes 9220
  93.4 38.8 %copy-start.139 = (f32[768]{0:T(1024)}, f32[768]{0:T(1024)S(1)}, u32[]{:S(2)}) copy-start(f32[768]{0:T(1024)S(1)} %convert_element_type.602) | copy-start | bytes 9220
  102.2 30.0 %copy-start.94 = (f32[1024]{0:T(1024)}, f32[1024]{0:T(1024)S(1)}, u32[]{:S(2)}) copy-start(f32[1024]{0:T(1024)S(1)} %broadcast_multiply_fusion.5) | copy-start | bytes 12292
  103.8 28.4 %copy-start.111 = (f32[1024]{0:T(1024)}, f32[1024]{0:T(1024)S(1)}, u32[]{:S(2)}) copy-start(f32[1024]{0:T(1024)S(1)} %fusion.227) | copy-start | bytes 12292
  327.9 72.6 %copy-start.144 = (f32[768]{0:T(1024)S(1)}, f32[768]{0:T(1024)}, u32[]{:S(2)}) copy-start(f32[768]{0:T(1024)} %convert_element_type.613) | copy-start | bytes 9220
  509.2 73.5 %copy-start.69 = (f32[1024]{0:T(1024)}, f32[1024]{0:T(1024)S(1)}, u32[]{:S(2)}) copy-start(f32[1024]{0:T(1024)S(1)} %broadcast_multiply_fusion.1) | copy-start | bytes 12292
  511.2 71.6 %copy-start.79 = (f32[1024]{0:T(1024)}, f32[1024]{0:T(1024)S(1)}, u32[]{:S(2)}) copy-start(f32[1024]{0:T(1024)S(1)} %fusion.229) | copy-start | bytes 12292
  511.2 38.7 %copy-start.102 = (f32[1,2,4,128]{3,1,2,0:T(2,128)S(1)}, f32[1,2,4,128]{3,1,2,0:T(2,128)}, u32[]{:S(2)}) copy-start(f32[1,2,4,128]{3,1,2,0:T(2,128)} %copy.145) | copy-start | bytes 12292
  511.2 38.7 %copy-start.127 = (f32[3072]{0:T(1024)S(1)}, f32[3072]{0:T(1024)}, u32[]{:S(2)}) copy-start(f32[3072]{0:T(1024)} %convert_element_type.617) | copy-start | bytes 36868
  511.3 56.1 %slice-start = ((s8[4718592]{0:T(1024)(128)(4,1)}), s8[524288]{0:T(1024)(128)(4,1)S(1)}, s32[]{:S(2)}) async-start(s8[4718592]{0:T(1024)(128)(4,1)} %bitcast.521), calls=%async_computation.60 | async-start | bytes 1048576
  550.0 17.4 slice-start.1
  603.6 690.0 %reduce-scatter.29.cloned.1.call-start = ((), (), s32[]{:S(2)}) async-start(), calls=%async_computation.26 | async-start | bytes 2506752 | tf_op jit(solution)/shard_map/reduce_scatter | solution.py:340
  820.9 474.4 %reduce-scatter.45.cloned.1.call-start = ((), (), s32[]{:S(2)}) async-start(), calls=%async_computation.34 | async-start | bytes 2506752 | tf_op jit(solution)/shard_map/reduce_scatter | solution.py:343
  922.2 76.1 %copy-start.71 = (f32[1024]{0:T(1024)}, f32[1024]{0:T(1024)S(1)}, u32[]{:S(2)}) copy-start(f32[1024]{0:T(1024)S(1)} %broadcast_multiply_fusion) | copy-start | bytes 12292
  930.1 366.9 %reduce-scatter.37.cloned.1.call-start = ((), (), s32[]{:S(2)}) async-start(), calls=%async_computation.30 | async-start | bytes 2506752 | tf_op jit(solution)/shard_map/reduce_scatter | solution.py:342
  930.2 68.2 %copy-start.81 = (f32[1024]{0:T(1024)}, f32[1024]{0:T(1024)S(1)}, u32[]{:S(2)}) copy-start(f32[1024]{0:T(1024)S(1)} %fusion.230) | copy-start | bytes 12292
  954.4 344.2 %reduce-scatter.49.cloned.1.call-start = ((), (), s32[]{:S(2)}) async-start(), calls=%async_computation.36 | async-start | bytes 2506752 | tf_op jit(solution)/shard_map/reduce_scatter | solution.py:345
  954.9 28.0 %slice-start.2 = ((s8[4718592]{0:T(1024)(128)(4,1)}), s8[4194304]{0:T(1024)(128)(4,1)S(1)}, s32[]{:S(2)}) async-start(s8[4718592]{0:T(1024)(128)(4,1)} %bitcast.523), calls=%async_computation.62 | async-start | bytes 8388608
  1019.8 280.4 %reduce-scatter.25.cloned.1.call-start = ((), (), s32[]{:S(2)}) async-start(), calls=%async_computation.24 | async-start | bytes 2506752 | tf_op jit(solution)/shard_map/reduce_scatter | solution.py:340
  1236.7 127.8 %reduce-scatter.41.cloned.1.call-start = ((), (), s32[]{:S(2)}) async-start(), calls=%async_computation.32 | async-start | bytes 2506752 | tf_op jit(solution)/shard_map/reduce_scatter | solution.py:343
  1243.5 187.1 %reduce-scatter.33.cloned.1.call-start = ((), (), s32[]{:S(2)}) async-start(), calls=%async_computation.28 | async-start | bytes 2506752 | tf_op jit(solution)/shard_map/reduce_scatter | solution.py:342
  1248.8 462.0 %reduce-scatter.69.cloned.1.call-start = ((), (), s32[]{:S(2)}) async-start(), calls=%async_computation.46 | async-start | bytes 10027008 | tf_op jit(solution)/shard_map/reduce_scatter | solution.py:351
  1263.0 456.9 %reduce-scatter.61.cloned.1.call-start = ((), (), s32[]{:S(2)}) async-start(), calls=%async_computation.42 | async-start | bytes 10027008 | tf_op jit(solution)/shard_map/reduce_scatter | solution.py:349
  1276.1 501.4 %reduce-scatter.65.cloned.1.call-start = ((), (), s32[]{:S(2)}) async-start(), calls=%async_computation.44 | async-start | bytes 10027008 | tf_op jit(solution)/shard_map/reduce_scatter | solution.py:351
  1291.7 78.3 %copy-start.148 = (bf16[768]{0:T(1024)(128)(2,1)S(1)}, bf16[768]{0:T(1024)(128)(2,1)}, u32[]{:S(2)}) copy-start(bf16[768]{0:T(1024)(128)(2,1)} %get-tuple-element.815) | copy-start | bytes 4612
  1291.7 140.5 %copy-start.25 = (f32[1024,768]{0,1:T(8,128)S(1)}, f32[1024,768]{0,1:T(8,128)}, u32[]{:S(2)}) copy-start(f32[1024,768]{0,1:T(8,128)} %copy-done.23) | copy-start | bytes 9437188
  1291.7 140.6 %copy-start.72 = (f32[1024]{0:T(1024)S(1)}, f32[1024]{0:T(1024)}, u32[]{:S(2)}) copy-start(f32[1024]{0:T(1024)} %copy-done.71) | copy-start | bytes 12292
  1291.7 140.6 %copy-start.78 = (f32[768]{0:T(1024)S(1)}, f32[768]{0:T(1024)}, u32[]{:S(2)}) copy-start(f32[768]{0:T(1024)} %convert_element_type.606) | copy-start | bytes 9220
  1291.7 140.6 %copy-start.82 = (f32[1024]{0:T(1024)S(1)}, f32[1024]{0:T(1024)}, u32[]{:S(2)}) copy-start(f32[1024]{0:T(1024)} %copy-done.81) | copy-start | bytes 12292
  1291.8 140.6 %copy-start.89 = (f32[768]{0:T(1024)S(1)}, f32[768]{0:T(1024)}, u32[]{:S(2)}) copy-start(f32[768]{0:T(1024)} %convert_element_type.607) | copy-start | bytes 9220
  1291.8 497.6 %reduce-scatter.55.cloned.1.call-start = ((), (), s32[]{:S(2)}) async-start(), calls=%async_computation.39 | async-start | bytes 110592 | tf_op jit(solution)/shard_map/reduce_scatter | solution.py:376
  1293.6 508.6 %reduce-scatter.31.cloned.1.call-start = ((), (), s32[]{:S(2)}) async-start(), calls=%async_computation.27 | async-start | bytes 110592 | tf_op jit(solution)/shard_map/reduce_scatter | solution.py:361
  1295.2 519.6 %reduce-scatter.47.cloned.1.call-start = ((), (), s32[]{:S(2)}) async-start(), calls=%async_computation.35 | async-start | bytes 110592 | tf_op jit(solution)/shard_map/reduce_scatter | solution.py:370
  1296.9 530.5 %reduce-scatter.39.cloned.1.call-start = ((), (), s32[]{:S(2)}) async-start(), calls=%async_computation.31 | async-start | bytes 110592 | tf_op jit(solution)/shard_map/reduce_scatter | solution.py:367
  1298.5 541.1 %reduce-scatter.51.cloned.1.call-start = ((), (), s32[]{:S(2)}) async-start(), calls=%async_computation.37 | async-start | bytes 110592 | tf_op jit(solution)/shard_map/reduce_scatter | solution.py:376
  1300.2 552.3 %reduce-scatter.27.cloned.1.call-start = ((), (), s32[]{:S(2)}) async-start(), calls=%async_computation.25 | async-start | bytes 110592 | tf_op jit(solution)/shard_map/reduce_scatter | solution.py:361
  1301.8 562.7 %reduce-scatter.43.cloned.1.call-start = ((), (), s32[]{:S(2)}) async-start(), calls=%async_computation.33 | async-start | bytes 110592 | tf_op jit(solution)/shard_map/reduce_scatter | solution.py:370
  1366.1 511.2 %reduce-scatter.35.cloned.1.call-start = ((), (), s32[]{:S(2)}) async-start(), calls=%async_computation.29 | async-start | bytes 110592 | tf_op jit(solution)/shard_map/reduce_scatter | solution.py:367
  1432.2 561.1 %reduce-scatter.57.cloned.1.call-start = ((), (), s32[]{:S(2)}) async-start(), calls=%async_computation.40 | async-start | bytes 10027008 | tf_op jit(solution)/shard_map/reduce_scatter | solution.py:349
  1442.9 564.3 %reduce-scatter.71.cloned.1.call-start = ((), (), s32[]{:S(2)}) async-start(), calls=%async_computation.47 | async-start | bytes 442368 | tf_op jit(solution)/shard_map/reduce_scatter | solution.py:394
  1603.8 81.9 %copy-start.13 = (f32[1024,768]{0,1:T(8,128)S(1)}, f32[1024,768]{0,1:T(8,128)}, u32[]{:S(2)}) copy-start(f32[1024,768]{0,1:T(8,128)} %copy-done.11) | copy-start | bytes 9437188
  1603.8 81.9 %copy-start.138 = (f32[768]{0:T(1024)S(1)}, f32[768]{0:T(1024)}, u32[]{:S(2)}) copy-start(f32[768]{0:T(1024)} %convert_element_type.614) | copy-start | bytes 9220
  1691.0 21.7 %copy-start.19 = (bf16[1024,768]{0,1:T(8,128)(2,1)S(1)}, bf16[1024,768]{0,1:T(8,128)(2,1)}, u32[]{:S(2)}) copy-start(bf16[1024,768]{0,1:T(8,128)(2,1)} %copy-done.14) | copy-start | bytes 4718596
  1691.0 21.7 %copy-start.115 = (f32[1024]{0:T(1024)S(1)}, f32[1024]{0:T(1024)}, u32[]{:S(2)}) copy-start(f32[1024]{0:T(1024)} %copy-done.114) | copy-start | bytes 12292
  1712.6 309.5 %reduce-scatter.63.cloned.1.call-start = ((), (), s32[]{:S(2)}) async-start(), calls=%async_computation.43 | async-start | bytes 442368 | tf_op jit(solution)/shard_map/reduce_scatter | solution.py:388
  1721.8 314.6 %reduce-scatter.67.cloned.1.call-start = ((), (), s32[]{:S(2)}) async-start(), calls=%async_computation.45 | async-start | bytes 442368 | tf_op jit(solution)/shard_map/reduce_scatter | solution.py:394
  1779.4 271.8 %reduce-scatter.59.cloned.1.call-start = ((), (), s32[]{:S(2)}) async-start(), calls=%async_computation.41 | async-start | bytes 442368 | tf_op jit(solution)/shard_map/reduce_scatter | solution.py:388
  (150 other events, 741.2 us)
Sparse Core Ops, SparseCore 0:
  11.0 41.2 all-gather.42
  55.2 37.2 all-gather.44
  94.8 37.3 all-gather.46
  134.3 37.3 all-gather.48
  174.4 52.3 all-gather.50
  229.5 51.9 all-gather.52
  284.3 36.8 all-gather.54
  323.5 37.3 all-gather.56
  363.1 37.3 all-gather.58
  402.6 37.4 all-gather.60
  442.9 52.2 all-gather.62
  498.0 51.9 all-gather.64
  603.8 61.5 reduce-scatter.52
  821.1 61.4 reduce-scatter.28
  930.2 61.7 reduce-scatter.44
  996.1 61.9 reduce-scatter.36
  1061.7 62.0 reduce-scatter.48
  1236.8 61.9 reduce-scatter.24
  1302.6 61.9 reduce-scatter.40
  1368.6 61.9 reduce-scatter.32
  1434.8 110.3 reduce-scatter.68
  1549.8 112.3 reduce-scatter.60
  1666.3 111.1 reduce-scatter.64
  1779.7 9.6 reduce-scatter.54
  1792.2 9.8 reduce-scatter.30
  1804.9 9.8 reduce-scatter.46
  1817.5 9.8 reduce-scatter.38
  1829.7 9.8 reduce-scatter.50
  1842.5 9.8 reduce-scatter.26
  1854.6 9.8 reduce-scatter.42
  1867.4 9.8 reduce-scatter.34
  1882.0 111.3 reduce-scatter.56
  1995.4 11.7 reduce-scatter.70
  2010.0 12.0 reduce-scatter.62
  2024.3 12.0 reduce-scatter.66
  2039.1 12.0 reduce-scatter.58
where the time goes:
time: 2070 us
  matrix products  773 us (37%)
  waiting for transfers between devices  505 us (24%)
  other arithmetic  422 us (20%)
  blocking collectives  202 us (10%)
  local copies, waits for them, and re-layouts  138 us (7%)
  between operations  21.8 us (1%)
    dot_general x12, matrix products, masked_scores(): jnp.einsum('qhd,khd->hqk', query_heads, key_heads, preferred_element_type...  175 us
    sub x4, other arithmetic, one_block(): exponent = jnp.exp(scores - row_peak)  162 us
    unnamed x4, blocking collectives  137 us
    dot_general x8, matrix products, one_block(): jnp.einsum('hqk,khd->qhd', probs_low, value_heads, preferred_element_type...  118 us
    convert_element_type x4, other arithmetic, one_block(): grad_scores = (attn_probs * (grad_probs - row_dot)).astype(jnp.bfloat16)  111 us
    reduce_scatter x2, waiting for transfers between devices, on_device(): lax.psum_scatter(grad_terms[11], 'fsdp', scatter_dimension=0, tiled=True)  110 us
    dot_general x4, matrix products, one_block(): jnp.einsum('qhd,khd->hqk', grad_heads, value_heads, preferred_element_typ...  103 us
    dot_general x14, matrix products, product(): return jnp.dot(first, second, preferred_element_type=jnp.float32)  96.3 us
  transfers between devices with their start and end apart: 36, of which 21 were waited for; matrix products, arithmetic and copies ran while one was open for 60% of the time, Pallas kernels for 0%

commit v1 on v0

v1 whole, which is shorter than its diff:
```python
import functools
import math

import jax
import jax.numpy as jnp
from jax import lax
from jax.experimental import pallas as pl
from jax.experimental.pallas import tpu as pltpu
from jax.sharding import PartitionSpec as P

HEADS = 16
PIECES = 16
EXTRA = 16
EPSILON = 1e-06
BIG = 1e30
bf16 = jnp.bfloat16
f32 = jnp.float32
FORWARD_PARTS = 1
BACKWARD_PARTS = 4
UNROLL = 2
ATTN_PLAN = {0: [(0, 0)], 1: [(1, 0)], 2: [(0, 1)], 5: [(1, 1), (0, 2)], 7: [(1, 2), (0, 3)]}
ATTN_MIDDLE = []
ATTN_TILES = {0: [(1, 3), (0, 4)], 3: [(1, 4), (0, 5)]}
ATTN_END = [(1, 5)]
VMEM_BYTES = 60 * 1024 * 1024


def mm(a, b):
    return jnp.dot(a, b, preferred_element_type=f32)


def mm_tn(a, b):
    return lax.dot_general(a, b, (((0,), (0,)), ((), ())), preferred_element_type=f32)


def mm_nt(a, b):
    return lax.dot_general(a, b, (((1,), (1,)), ((), ())), preferred_element_type=f32)


def normalised(x):
    mean = jnp.mean(x, axis=-1, keepdims=True)
    centred = x - mean
    var = jnp.mean(centred * centred, axis=-1, keepdims=True)
    r = lax.rsqrt(var + EPSILON)
    return centred * r, r


def norm_back(d, xh, r, gain):
    e = d * gain
    m1 = jnp.mean(e, axis=-1, keepdims=True)
    m2 = jnp.mean(e * xh, axis=-1, keepdims=True)
    return r * (e - m1 - xh * m2)


def split3(x):
    hi = x.astype(bf16)
    rest = x - hi.astype(f32)
    mid = rest.astype(bf16)
    low = (rest - mid.astype(f32)).astype(bf16)
    return hi, mid, low


def joined(ref):
    x = ref[...]
    return x.reshape(x.shape[0] * x.shape[1], x.shape[2])


def weight(ref, index, rows):
    x = ref[:, index * rows : (index + 1) * rows, :]
    return x.reshape(x.shape[0] * rows, x.shape[2])


def window(w_any, w_ref, sem, base):
    return pltpu.make_async_copy(w_any.at[:, base : base + w_ref.shape[1], :], w_ref, sem)


def down(ref, j, rows, blocks):
    quarter = PIECES // blocks
    x = ref[quarter * j : quarter * (j + 1), rows * blocks : 2 * rows * blocks, :]
    return x.reshape(quarter * rows * blocks, x.shape[2])


def gelu_parts(u):
    c0 = math.sqrt(2.0 / math.pi)
    c1 = c0 * 0.044715
    u2 = u * u
    t = jnp.tanh(u * (c0 + c1 * u2))
    half = 0.5 * (1.0 + t)
    z = u * half
    slope = half + u * (half * (1.0 - t)) * (c0 + (3.0 * c1) * u2)
    return z, slope


def mask_rows(seg_ref, length, slots):
    width = length // slots
    qs, ks = [], []
    for s in range(slots):
        row = lax.broadcasted_iota(jnp.int32, (EXTRA, width), 0)
        seg = seg_ref[0, s]
        same = row == seg
        first = row < slots
        qs.append(jnp.where(same | ~first, 0.0, 1.0))
        ks.append(jnp.where(same, -BIG, jnp.where((row >= 4) & (row < 7), 1.0, 0.0)))
    return jnp.concatenate(qs, axis=1), jnp.concatenate(ks, axis=1)


class Links:
    def __init__(self):
        me = lax.axis_index("fsdp")
        x = lax.axis_index("rep")
        c = lax.rem(me, 2)
        y = lax.rem(lax.div(me, 2), 2)
        low = lax.rem(lax.div(me, 4), 2)
        high = lax.div(me, 8)
        self.at = {"c": c, "y": y, "l": low, "h": high, "x": x}
        self.peer = {
            "c": {"fsdp": me + 1 - 2 * c, "rep": x},
            "y": {"fsdp": me + 2 - 4 * y, "rep": x},
            "l": {"fsdp": me + 4 - 8 * low, "rep": x},
            "h": {"fsdp": me + 8 - 16 * high, "rep": x},
            "x": {"fsdp": me, "rep": 1 - x},
        }

    def meet(self):
        barrier = pltpu.get_barrier_semaphore()
        for who in self.peer.values():
            pl.semaphore_signal(barrier, inc=1, device_id=who, device_id_type=pl.DeviceIdType.MESH)
        pl.semaphore_wait(barrier, len(self.peer))


class Reduction(Links):
    ORDERS = ("yxlh", "xylh", "lhyx")
    STEPS = 6

    @classmethod
    def paths(cls, rows, subs):
        found, start = [], 0
        for sub in range(subs):
            units = rows // 32 * (sub + 1) // subs - rows // 32 * sub // subs
            third = (units + 2) // 4
            first = (units - third + 1) // 2
            for order, count in zip(cls.ORDERS, (first, units - third - first, third)):
                found.append((order, start, 32 * count))
                start += 32 * count
        return found

    @classmethod
    def scratch(cls, rows, subs, width):
        shapes = [pltpu.VMEM((2, 2, 2, rows, width), bf16)] * 2
        for order, _, count in cls.paths(rows, subs):
            free = 3
            for axis in order:
                if axis == "x":
                    count //= 2
                else:
                    free -= 1
                shapes.append(pltpu.VMEM((2,) * free + (count, width), bf16))
        return shapes + [pltpu.SemaphoreType.DMA((18 * subs,)), pltpu.SemaphoreType.DMA((21 * subs,))]

    def __init__(self, subs, v_any, fin_ref, refs):
        self.subs, self.v, self.fin = subs, v_any, fin_ref
        self.own, self.got = refs[0], refs[1]
        self.bufs = [refs[2 + 4 * k : 6 + 4 * k] for k in range(3 * subs)]
        self.send_sem, self.recv_sem = refs[-2], refs[-1]
        self.parts = self.paths(self.own.shape[3], subs)
        super().__init__()

    def remote(self, src, dst, sem, who):
        return pltpu.make_async_remote_copy(
            src_ref=src,
            dst_ref=dst,
            send_sem=self.send_sem.at[sem],
            recv_sem=self.recv_sem.at[sem],
            device_id=self.peer[who],
            device_id_type=pl.DeviceIdType.MESH,
        )

    def local(self, path):
        _, start, count = self.parts[path]
        rows = pl.ds(start, count)
        return pltpu.make_async_copy(
            self.v.at[:, :, :, self.at["c"], rows, :], self.own.at[:, :, :, rows, :], self.recv_sem.at[18 * self.subs + path]
        )

    def cores(self, path):
        _, start, count = self.parts[path]
        rows = pl.ds(start, count)
        src = self.v.at[:, :, :, 1 - self.at["c"], rows, :]
        return self.remote(src, self.got.at[:, :, :, rows, :], 6 * path, "c")

    def places(self, path, step):
        order, start, count = self.parts[path]
        fixed = {}
        rows = pl.ds(start, count)
        send = None
        for axis in order[: step + 1]:
            send = (dict(fixed), rows)
            if axis == "x":
                half = count // 2
                send = (dict(fixed), pl.ds(pl.multiple_of(start + (1 - self.at["x"]) * half, 16), half))
                rows = pl.ds(pl.multiple_of(start + self.at["x"] * half, 16), half)
            else:
                send[0][axis] = 1 - self.at[axis]
                fixed[axis] = self.at[axis]
        return send, (fixed, rows)

    @staticmethod
    def index(place, free=()):
        fixed, rows = place
        found, free = [], list(free)
        for axis in "hly":
            found.append(fixed[axis] if axis in fixed else (free.pop(0) if free else slice(None)))
        return (*found, rows, slice(None))

    def exchange(self, path, step):
        sem = 6 * path + 1 + step
        if step == 4:
            keep = self.places(path, 3)[1]
            return self.remote(self.own.at[self.index(keep)], self.fin.at[keep[1], :], sem, "x")
        send, _ = self.places(path, step)
        return self.remote(self.own.at[self.index(send)], self.bufs[path][step], sem, self.parts[path][0][step])

    def start(self):
        self.meet()
        for path in range(3 * self.subs):
            self.cores(path).start()
            self.local(path).start()

    def add(self, place, other):
        free = 3 - len(place[0])

        def one(i, carry):
            bits = [lax.rem(lax.div(i, 2 ** (free - 1 - b)), 2) for b in range(free)]
            where = self.index(place, bits)
            self.own[where] = self.own[where] + other(bits)
            return carry

        if free:
            lax.fori_loop(0, 2**free, one, 0)
        else:
            one(0, 0)

    def advance(self, path, step):
        if step == 0:
            self.cores(path).wait()
            self.local(path).wait()
            _, start, count = self.parts[path]
            place = ({}, pl.ds(start, count))
            self.add(place, lambda bits: self.got[self.index(place, bits)])
            self.exchange(path, 0).start()
            return
        k = step - 1
        self.exchange(path, k).wait()
        if k == 4:
            return
        place = self.places(path, k)[1]
        buf = self.bufs[path][k]
        self.add(place, lambda bits: buf[(*bits, slice(None), slice(None))])
        self.exchange(path, k + 1).start()
        if k == 3:
            self.fin[place[1], :] = self.own[self.index(place)]

    def run(self, moves):
        for sub, step in moves:
            for path in range(3 * sub, 3 * sub + 3):
                self.advance(path, step)


def reduction_kernel(subs, v_any, fin_ref, *refs):
    red = Reduction(subs, v_any, fin_ref, refs)
    red.start()
    for step in range(Reduction.STEPS):
        red.run([(sub, step) for sub in range(subs)])


def six(x):
    return x.reshape((2, 2, 2, 2) + x.shape[1:])


def reduced(x, subs, ident):
    rows, width = x.shape[1:]
    return pl.pallas_call(
        functools.partial(reduction_kernel, subs),
        name="reduction",
        in_specs=[pl.BlockSpec(memory_space=pl.ANY)],
        out_specs=pl.BlockSpec(memory_space=pltpu.VMEM),
        out_shape=sds((rows, width), bf16),
        scratch_shapes=Reduction.scratch(rows, subs, width),
        compiler_params=pltpu.CompilerParams(
            vmem_limit_bytes=VMEM_BYTES, collective_id=ident, has_side_effects=True
        ),
    )(six(x))


def gather_kernel(ident, x_any, out_any, send_sem, recv_sem, own_sem):
    red = Links()
    at = red.at
    rows = x_any.shape[0]
    mine = (at["h"], at["l"], at["y"], at["c"])
    own = pltpu.make_async_copy(x_any, out_any.at[(*mine, slice(None), slice(None))], own_sem)
    own.start()
    own.wait()
    red.meet()

    def copy(path, step):
        order, start, count = path
        order = order[::-1] + "c"
        free = order[:step]
        half = count // 2
        if "x" in free:
            span = pl.ds(start, count)
        else:
            span = pl.ds(pl.multiple_of(start + at["x"] * half, 16), half)
        where = tuple(slice(None) if a in free else at[a] for a in "hlyc") + (span, slice(None))
        sem = 5 * paths.index(path) + step
        return pltpu.make_async_remote_copy(
            src_ref=out_any.at[where],
            dst_ref=out_any.at[where],
            send_sem=send_sem.at[sem],
            recv_sem=recv_sem.at[sem],
            device_id=red.peer[order[step]],
            device_id_type=pl.DeviceIdType.MESH,
        )

    paths = Reduction.paths(rows, 1)
    for path in paths:
        copy(path, 0).start()
    for step in range(5):
        for path in paths:
            copy(path, step).wait()
            if step < 4:
                copy(path, step + 1).start()


def gathered(x, ident):
    rows, width = x.shape
    out = pl.pallas_call(
        functools.partial(gather_kernel, ident),
        name="gather",
        in_specs=[pl.BlockSpec(memory_space=pl.ANY)],
        out_specs=pl.BlockSpec(memory_space=pl.ANY),
        out_shape=sds((2, 2, 2, 2, rows, width), bf16),
        scratch_shapes=[pltpu.SemaphoreType.DMA((15,)), pltpu.SemaphoreType.DMA((15,)), pltpu.SemaphoreType.DMA],
        compiler_params=pltpu.CompilerParams(
            vmem_limit_bytes=8 * 1024 * 1024, collective_id=ident, has_side_effects=True
        ),
        cost_estimate=pl.CostEstimate(flops=0, bytes_accessed=100 << 20, transcendentals=0),
    )(x)
    return out.reshape(PIECES, rows, width)


def attn_forward_kernel(
    base, red, h_ref, w_any, vec_ref, seg_ref,
    g_ref, at_ref, qe_ref, ke_ref, ve_ref, ot_ref, ol_ref, w_ref, w_sem,
):
    length, width = h_ref.shape
    hd = width // HEADS
    rows = width // PIECES
    scale = math.log2(math.e) / math.sqrt(hd)
    fetch = window(w_any, w_ref, w_sem, base)
    fetch.start()
    x = h_ref[...].astype(f32)
    xh, _ = normalised(x)
    a = (xh * vec_ref[0:1, :] + vec_ref[1:2, :]).astype(bf16)
    at_ref[...] = a.T
    fetch.wait()
    q = (mm(a, weight(w_ref, 0, rows)) + vec_ref[2:3, :]).astype(bf16)
    qe_ref[:, 0:hd, :] = q.T.reshape(HEADS, hd, length)
    k = mm(a, weight(w_ref, 1, rows)).astype(bf16)
    ke_ref[:, 0:hd, :] = k.T.reshape(HEADS, hd, length)
    v = (mm(a, weight(w_ref, 2, rows)) + vec_ref[3:4, :]).astype(bf16)
    ve_ref[:, 0:hd, :] = v.T.reshape(HEADS, hd, length)
    mask_q, mask_k = mask_rows(seg_ref, length, seg_ref.shape[1])
    qe_ref[:, hd:, :] = jnp.broadcast_to(mask_q.astype(bf16)[None], (HEADS, EXTRA, length))
    ke_ref[:, hd:, :] = jnp.broadcast_to(mask_k.astype(bf16)[None], (HEADS, EXTRA, length))
    ve_ref[:, hd:, :] = jnp.ones((HEADS, EXTRA, length), bf16)
    row = lax.broadcasted_iota(jnp.int32, (EXTRA, length // FORWARD_PARTS), 0)

    part = length // FORWARD_PARTS

    def head(i):
        for t in range(FORWARD_PARTS):
            cols = slice(t * part, (t + 1) * part)
            st = mm_tn(ke_ref[i], qe_ref[i, :, cols])
            peak = jnp.max(st, axis=0, keepdims=True)
            e = jnp.exp2((st - peak) * scale).astype(bf16)
            mix = mm(ve_ref[i], e)
            total = mix[hd : hd + 1, :]
            o = mix[0:hd, :] * (1.0 / total)
            high = o.astype(bf16)
            ot_ref[i, :, cols] = high
            ol_ref[i, :, cols] = (o - high.astype(f32)).astype(bf16)
            lse = -(peak + jnp.log2(total) * (1.0 / scale))
            hi, mid, low = split3(lse)
            ext = jnp.where(row == 6, low.astype(f32), mask_q[:, cols])
            ext = jnp.where(row == 4, hi.astype(f32), jnp.where(row == 5, mid.astype(f32), ext))
            qe_ref[i, hd:, cols] = ext.astype(bf16)

    def pair(j, carry):
        for k in range(UNROLL):
            head(UNROLL * j + k)
        return carry

    lax.fori_loop(0, HEADS // UNROLL, pair, 0)
    g_ref[...] = x + (mm_tn(joined(ot_ref), weight(w_ref, 3, rows)) + vec_ref[4:5, :])


def full(shape):
    return pl.BlockSpec(shape, lambda: (0,) * len(shape))


ANY = pl.BlockSpec(memory_space=pl.ANY)


def call(kernel, name, args, specs, outs, flops, nbytes, scratch, carry=None, ident=None):
    n_in, n_out, n_scratch = len(args), len(outs), len(scratch)
    args, outs, scratch = list(args), list(outs), list(scratch)
    specs = list(specs)
    out_specs = [full(s.shape) for s in outs]
    if carry is None:
        body = functools.partial(kernel, None)
    else:
        grads, subs = carry
        rows, width = grads.shape[1:]
        args.append(six(grads))
        specs.append(ANY)
        outs.append(sds((rows, width), bf16))
        out_specs.append(full((rows, width)))
        scratch += Reduction.scratch(rows, subs, width)

        def body(*refs):
            ins, v = refs[:n_in], refs[n_in]
            results = refs[n_in + 1 : n_in + 1 + n_out]
            fin = refs[n_in + 1 + n_out]
            rest = refs[n_in + 2 + n_out :]
            kernel(Reduction(subs, v, fin, rest[n_scratch:]), *ins, *results, *rest[:n_scratch])

    return pl.pallas_call(
        body,
        name=name,
        in_specs=specs,
        out_specs=out_specs,
        out_shape=outs,
        scratch_shapes=scratch,
        compiler_params=pltpu.CompilerParams(
            vmem_limit_bytes=VMEM_BYTES, collective_id=ident, has_side_effects=ident is not None
        ),
        cost_estimate=pl.CostEstimate(flops=flops, bytes_accessed=nbytes, transcendentals=0),
    )(*args)


def advance_at(red, index, plan):
    if red is None:
        return
    for at, moves in plan.items():

        @pl.when(index == at)
        def _(moves=moves):
            red.run(moves)


def sds(shape, dtype):
    return jax.ShapeDtypeStruct(shape, dtype)


SMEM = pltpu.SMEM


def attn_forward(h, square, vec, seg):
    square, base = square
    n, d = h.shape
    hd = d // HEADS
    rows = d // PIECES
    ext = hd + EXTRA
    outs = (
        sds((n, d), f32),
        sds((d, n), bf16),
        sds((HEADS, ext, n), bf16),
        sds((HEADS, ext, n), bf16),
        sds((HEADS, ext, n), bf16),
        sds((HEADS, hd, n), bf16),
        sds((HEADS, hd, n), bf16),
    )
    specs = [full(h.shape), pl.BlockSpec(memory_space=pl.ANY)]
    specs += [full(vec.shape), pl.BlockSpec(memory_space=SMEM)]
    flops = 8 * n * d * d + 2 * HEADS * 2 * n * n * 256
    scratch = [pltpu.VMEM((PIECES, 4 * rows, d), bf16), pltpu.SemaphoreType.DMA]
    return call(
        functools.partial(attn_forward_kernel, base), "attn_forward", (h, square, vec, seg),
        specs, outs, flops, 30 << 20, scratch,
    )


def ff_forward_kernel(base, g_ref, w_any, vec_ref, h_ref, b_ref, z_ref, s_ref, w_ref, w_sem):
    width = g_ref.shape[1]
    rows = width // PIECES
    blocks = z_ref.shape[1] // width

    @pl.when(pl.program_id(0) == 0)
    def _():
        fetch = window(w_any, w_ref, w_sem, base)
        fetch.start()
        fetch.wait()

    gg = g_ref[...]
    xh, _ = normalised(gg)
    b = (xh * vec_ref[5:6, :] + vec_ref[6:7, :]).astype(bf16)
    b_ref[...] = b
    acc = gg + vec_ref[7:8, :]
    for j in range(blocks):
        w = weight(w_ref, j, rows)
        u = mm(b, w) + vec_ref[8 + j : 9 + j, :]
        z, slope = gelu_parts(u)
        zb = z.astype(bf16)
        z_ref[:, j * width : (j + 1) * width] = zb
        s_ref[:, j * width : (j + 1) * width] = slope.astype(bf16)
        wd = down(w_ref, j, rows, blocks)
        acc = acc + mm(zb, wd)
    h_ref[...] = acc


def ff_forward(g, wide, vec, ff):
    wide, base = wide
    n, d = g.shape
    tile = 256
    outs = (sds((n, d), f32), sds((n, d), bf16), sds((n, ff), bf16), sds((n, ff), bf16))
    row = lambda w: pl.BlockSpec((tile, w), lambda i: (i, 0))
    return pl.pallas_call(
        functools.partial(ff_forward_kernel, base),
        name="ff_forward",
        grid=(n // tile,),
        in_specs=[
            row(d),
            pl.BlockSpec(memory_space=pl.ANY),
            pl.BlockSpec(vec.shape, lambda i: (0, 0)),
        ],
        out_specs=[row(d), row(d), row(ff), row(ff)],
        out_shape=outs,
        scratch_shapes=[pltpu.VMEM((PIECES, 2 * ff // PIECES, d), bf16), pltpu.SemaphoreType.DMA],
        compiler_params=pltpu.CompilerParams(vmem_limit_bytes=VMEM_BYTES),
        cost_estimate=pl.CostEstimate(flops=4 * n * d * ff, bytes_accessed=30 << 20, transcendentals=0),
    )(g, wide, vec)


def put_vectors(grad_ref, base, cols_ref, per):
    pad = grad_ref.shape[1] - base
    lanes = grad_ref.shape[2] // 128
    count = per // lanes
    for m in range(lanes):
        part = cols_ref[pl.ds(m, PIECES * count, stride=lanes), :]
        part = part.reshape(PIECES, count, 128)
        part = jnp.concatenate([part, jnp.zeros((PIECES, pad - count, 128), f32)], axis=1)
        grad_ref[:, base : base + pad, m * 128 : (m + 1) * 128] = part.astype(bf16)


def ff_tail(z_ref, du_ref, b_ref, cm_ref, grad_ref, cols_ref, vecs, width, blocks, red=None):
    rows = width // PIECES
    quarter = PIECES // blocks
    n = b_ref.shape[0]

    def block(j, carry):
        advance_at(red, j, {1: [(0, 2)], 2: [(0, 3)], 3: [(0, 4)]})
        cols = pl.ds(pl.multiple_of(j * width, 128), width)
        dwd = mm_tn(z_ref[:, cols], cm_ref[...])
        grad_ref[pl.ds(quarter * j, quarter), rows * blocks : 2 * rows * blocks, :] = (
            dwd.reshape(quarter, rows * blocks, width).astype(bf16)
        )
        dwu = mm_tn(b_ref[...], du_ref[:, cols])
        grad_ref[:, pl.ds(pl.multiple_of(rows * j, 16), rows), :] = (
            dwu.reshape(PIECES, rows, width).astype(bf16)
        )
        return carry

    lax.fori_loop(0, blocks, block, 0)
    ones = jnp.ones((n, 128), bf16)
    vt = jnp.concatenate([*vecs, jnp.zeros((128 - len(vecs), width), f32)], axis=0).T
    vt = vt.reshape(PIECES, rows, 128)
    lane = lax.broadcasted_iota(jnp.int32, (quarter, rows, 128), 2)
    for j in range(blocks):
        part = mm_tn(du_ref[:, j * width : (j + 1) * width], ones)
        part = part.reshape(quarter, blocks, rows, 128)
        piece = vt[quarter * j : quarter * (j + 1)]
        for c in range(blocks):
            piece = jnp.where(lane == len(vecs) + c, part[:, c], piece)
        cols_ref[quarter * rows * j : quarter * rows * (j + 1), :] = piece.reshape(quarter * rows, 128)
    put_vectors(grad_ref, 2 * rows * blocks, cols_ref, rows)
    if red is not None:
        red.run([(0, 5)])


def ff_last_kernel(
    base, red, g_ref, w_any, vec_ref, cot_ref, live_ref, out_ref, dg_ref, grad_ref,
    z_ref, du_ref, b_ref, cm_ref, cols_ref, w_ref, w_sem,
):
    n, width = g_ref.shape
    rows = width // PIECES
    blocks = z_ref.shape[1] // width
    tile = n // 4
    gain = vec_ref[5:6, :]
    fetch = window(w_any, w_ref, w_sem, base)
    fetch.start()
    fetch.wait()

    def step(t, sums):
        sum_gain, sum_bias, sum_down = sums
        span = pl.ds(pl.multiple_of(t * tile, 16), tile)
        gg = g_ref[span, :]
        xh, r = normalised(gg)
        b = (xh * gain + vec_ref[6:7, :]).astype(bf16)
        b_ref[span, :] = b
        grad = cot_ref[span, :].astype(f32) * live_ref[0, t].astype(f32)
        cm = grad.astype(bf16)
        cm_ref[span, :] = cm
        acc = gg + vec_ref[7:8, :]
        db = jnp.zeros((tile, width), f32)
        for j in range(blocks):
            cols = slice(j * width, (j + 1) * width)
            w = weight(w_ref, j, rows)
            wd = down(w_ref, j, rows, blocks)
            u = mm(b, w) + vec_ref[8 + j : 9 + j, :]
            dz = mm_nt(cm, wd)
            z, slope = gelu_parts(u)
            zb = z.astype(bf16)
            z_ref[span, cols] = zb
            acc = acc + mm(zb, wd)
            du = (slope * dz).astype(bf16)
            du_ref[span, cols] = du
            db = db + mm_nt(du, w)
        out_ref[span, :] = acc.astype(bf16)
        dg_ref[span, :] = grad + norm_back(db, xh, r, gain)
        sum_gain = sum_gain + jnp.sum(db * xh, axis=0, keepdims=True)
        sum_bias = sum_bias + jnp.sum(db, axis=0, keepdims=True)
        sum_down = sum_down + jnp.sum(cm.astype(f32), axis=0, keepdims=True)
        return sum_gain, sum_bias, sum_down

    zero = jnp.zeros((1, width), f32)
    sums = lax.fori_loop(0, 4, step, (zero, zero, zero))
    ff_tail(z_ref, du_ref, b_ref, cm_ref, grad_ref, cols_ref, sums, width, blocks)


def ff_last(g, wide, vec, cot, live, ff):
    wide, base = wide
    n, d = g.shape
    rows = d // PIECES
    outs = (sds((n, d), bf16), sds((n, d), f32), sds((PIECES, 2 * rows * (ff // d) + 2 * EXTRA, d), bf16))
    specs = [full(g.shape), pl.BlockSpec(memory_space=pl.ANY), full(vec.shape), full(cot.shape), pl.BlockSpec(memory_space=SMEM)]
    scratch = [
        pltpu.VMEM((n, ff), bf16), pltpu.VMEM((n, ff), bf16), pltpu.VMEM((n, d), bf16),
        pltpu.VMEM((n, d), bf16), pltpu.VMEM((d, 128), f32),
        pltpu.VMEM((PIECES, 2 * ff // PIECES, d), bf16), pltpu.SemaphoreType.DMA,
    ]
    return call(
        functools.partial(ff_last_kernel, base), "ff_last", (g, wide, vec, cot, live),
        specs, outs, 12 * n * d * ff, 30 << 20, scratch,
    )


def ff_backward_kernel(
    base, red, g_ref, w_any, vec_ref, c_ref, b_ref, z_ref, s_ref, dg_ref, grad_ref, du_ref, cm_ref, cols_ref,
    w_ref, w_sem,
):
    n, width = g_ref.shape
    rows = width // PIECES
    blocks = z_ref.shape[1] // width
    tile = n // 4
    gain = vec_ref[5:6, :]
    fetch = window(w_any, w_ref, w_sem, base)
    fetch.start()
    if red is not None:
        red.start()
    fetch.wait()

    def step(t, sums):
        advance_at(red, t, {0: [(0, 0)], 3: [(0, 1)]})
        sum_gain, sum_bias, sum_down = sums
        span = pl.ds(pl.multiple_of(t * tile, 16), tile)
        xh, r = normalised(g_ref[span, :])
        grad = c_ref[span, :]
        cm = grad.astype(bf16)
        cm_ref[span, :] = cm
        db = jnp.zeros((tile, width), f32)
        for j in range(blocks):
            cols = slice(j * width, (j + 1) * width)
            w = weight(w_ref, j, rows)
            wd = down(w_ref, j, rows, blocks)
            du = (s_ref[span, cols].astype(f32) * mm_nt(cm, wd)).astype(bf16)
            du_ref[span, cols] = du
            db = db + mm_nt(du, w)
        dg_ref[span, :] = grad + norm_back(db, xh, r, gain)
        sum_gain = sum_gain + jnp.sum(db * xh, axis=0, keepdims=True)
        sum_bias = sum_bias + jnp.sum(db, axis=0, keepdims=True)
        sum_down = sum_down + jnp.sum(cm.astype(f32), axis=0, keepdims=True)
        return sum_gain, sum_bias, sum_down

    zero = jnp.zeros((1, width), f32)
    sums = lax.fori_loop(0, 4, step, (zero, zero, zero))
    ff_tail(z_ref, du_ref, b_ref, cm_ref, grad_ref, cols_ref, sums, width, blocks, red)


def ff_backward(g, wide, vec, c, b, z, s, carry=None, ident=None):
    wide, base = wide
    n, d = g.shape
    ff = z.shape[1]
    rows = d // PIECES
    outs = (sds((n, d), f32), sds((PIECES, 2 * rows * (ff // d) + 2 * EXTRA, d), bf16))
    specs = [full(g.shape), pl.BlockSpec(memory_space=pl.ANY)] + [full(x.shape) for x in (vec, c, b, z, s)]
    scratch = [pltpu.VMEM((n, ff), bf16), pltpu.VMEM((n, d), bf16), pltpu.VMEM((d, 128), f32)]
    scratch += [pltpu.VMEM((PIECES, 2 * ff // PIECES, d), bf16), pltpu.SemaphoreType.DMA]
    return call(
        functools.partial(ff_backward_kernel, base), "ff_backward", (g, wide, vec, c, b, z, s),
        specs, outs, 8 * n * d * ff, 40 << 20, scratch, carry, ident,
    )


def attn_backward_kernel(
    base, red, h_ref, dg_ref, w_any, vec_ref, at_ref, qe_ref, ke_ref, ve_ref, ot_ref, ol_ref,
    c_ref, grad_ref, doe_ref, dq_ref, dk_ref, dv_ref, cols_ref, w_ref, w_sem,
):
    n, width = h_ref.shape
    hd = width // HEADS
    rows = width // PIECES
    scale = math.log2(math.e) / math.sqrt(hd)
    factor = 1.0 / math.sqrt(hd)
    fetch = window(w_any, w_ref, w_sem, base)
    fetch.start()
    if red is not None:
        red.start()
    co = dg_ref[...].astype(bf16)
    grad_ref[:, 3 * rows : 4 * rows, :] = mm(joined(ot_ref), co).reshape(PIECES, rows, width).astype(bf16)
    fetch.wait()
    dot = mm_nt(weight(w_ref, 3, rows), co).astype(bf16)
    doe_ref[:, 0:hd, :] = dot.reshape(HEADS, hd, n)
    row = lax.broadcasted_iota(jnp.int32, (EXTRA, n), 0)
    part = n // BACKWARD_PARTS

    def head(i):
        doh = doe_ref[i, 0:hd, :]
        delta = jnp.sum(doh.astype(f32) * (ot_ref[i].astype(f32) + ol_ref[i].astype(f32)), axis=0, keepdims=True)
        hi, mid, low = split3(-delta)
        ext = jnp.where(row == 0, hi.astype(f32), jnp.where(row == 1, mid.astype(f32), jnp.where(row == 2, low.astype(f32), 0.0)))
        doe_ref[i, hd:, :] = ext.astype(bf16)
        dk = dv = None
        for t in range(BACKWARD_PARTS):
            cols = slice(t * part, (t + 1) * part)
            s = mm_tn(qe_ref[i, :, cols], ke_ref[i])
            p = jnp.exp2(s * scale)
            dp = mm_tn(doe_ref[i, :, cols], ve_ref[i])
            ds = (p * dp).astype(bf16)
            dv_t = mm(doe_ref[i, 0:hd, cols], p.astype(bf16))
            dk_t = mm(qe_ref[i, 0:hd, cols], ds)
            dv = dv_t if t == 0 else dv + dv_t
            dk = dk_t if t == 0 else dk + dk_t
            dq_ref[i, :, cols] = (mm_nt(ke_ref[i, 0:hd, :], ds) * factor).astype(bf16)
        dv_ref[i] = dv.astype(bf16)
        dk_ref[i] = (dk * factor).astype(bf16)

    def pair(j, carry):
        advance_at(red, j, ATTN_PLAN)
        for k in range(UNROLL):
            head(UNROLL * j + k)
        return carry

    lax.fori_loop(0, HEADS // UNROLL, pair, 0)
    if red is not None:
        red.run(ATTN_MIDDLE)
    at = at_ref[...]
    dq = joined(dq_ref)
    dk = joined(dk_ref)
    dv = joined(dv_ref)
    grad_ref[:, 0:rows, :] = mm_nt(at, dq).reshape(PIECES, rows, width).astype(bf16)
    grad_ref[:, rows : 2 * rows, :] = mm_nt(at, dk).reshape(PIECES, rows, width).astype(bf16)
    grad_ref[:, 2 * rows : 3 * rows, :] = mm_nt(at, dv).reshape(PIECES, rows, width).astype(bf16)
    tile = n // 4

    def norm_tile(t, sums):
        advance_at(red, t, ATTN_TILES)
        sum_gain, sum_bias, sum_out = sums
        span = pl.ds(pl.multiple_of(t * tile, 128), tile)
        dat = mm(weight(w_ref, 0, rows), dq_ref[:, :, span].reshape(width, tile))
        dat = dat + mm(weight(w_ref, 1, rows), dk_ref[:, :, span].reshape(width, tile))
        dat = dat + mm(weight(w_ref, 2, rows), dv_ref[:, :, span].reshape(width, tile))
        da = dat.T
        xh, r = normalised(h_ref[span, :].astype(f32))
        dg = dg_ref[span, :]
        c_ref[span, :] = dg + norm_back(da, xh, r, vec_ref[0:1, :])
        sum_gain = sum_gain + jnp.sum(da * xh, axis=0, keepdims=True)
        sum_bias = sum_bias + jnp.sum(da, axis=0, keepdims=True)
        sum_out = sum_out + jnp.sum(dg.astype(bf16).astype(f32), axis=0, keepdims=True)
        return sum_gain, sum_bias, sum_out

    zero = jnp.zeros((1, width), f32)
    vecs = lax.fori_loop(0, 4, norm_tile, (zero, zero, zero))
    vt = jnp.concatenate([*vecs, jnp.zeros((128 - len(vecs), width), f32)], axis=0).T
    lane = lax.broadcasted_iota(jnp.int32, (width, 128), 1)
    vt = jnp.where(lane == 3, jnp.sum(dq.astype(f32), axis=1, keepdims=True), vt)
    vt = jnp.where(lane == 4, jnp.sum(dv.astype(f32), axis=1, keepdims=True), vt)
    cols_ref[...] = vt
    put_vectors(grad_ref, 4 * rows, cols_ref, rows)
    if red is not None:
        red.run(ATTN_END)


def attn_backward(h, dg, square, vec, kept, carry=None, ident=None):
    square, base = square
    n, d = h.shape
    hd = d // HEADS
    rows = d // PIECES
    at, qe, ke, ve, ot, ol = kept
    outs = (sds((n, d), f32), sds((PIECES, 4 * rows + 2 * EXTRA, d), bf16))
    specs = [full(h.shape), full(dg.shape), pl.BlockSpec(memory_space=pl.ANY)]
    specs += [full(x.shape) for x in (vec, at, qe, ke, ve, ot, ol)]
    scratch = [pltpu.VMEM((HEADS, hd + EXTRA, n), bf16)] + [pltpu.VMEM((HEADS, hd, n), bf16)] * 3
    scratch += [pltpu.VMEM((d, 128), f32), pltpu.VMEM((PIECES, 4 * rows, d), bf16), pltpu.SemaphoreType.DMA]
    flops = 16 * n * d * d + 5 * HEADS * 2 * n * n * 256
    return call(
        functools.partial(attn_backward_kernel, base), "attn_backward", (h, dg, square, vec, at, qe, ke, ve, ot, ol),
        specs, outs, flops, 40 << 20, scratch, carry, ident,
    )


NAMES = (
    "ln1_gain", "ln1_bias", "q_weight", "q_bias", "k_weight", "v_weight", "v_bias", "o_weight", "o_bias",
    "ln2_gain", "ln2_bias", "up_weight", "up_bias", "down_weight", "down_bias",
)
ROW_VECTORS = ("ln1_gain", "ln1_bias", "q_bias", "v_bias", "o_bias", "ln2_gain", "ln2_bias", "down_bias")


def gather(x, axis="fsdp"):
    return lax.all_gather(x, axis, axis=0, tiled=True)


def column_blocks(up, d):
    return [up[:, j * d : (j + 1) * d] for j in range(up.shape[1] // d)]


def fetch_even(w, layers, shards):
    d = w["q_weight"].shape[2]
    per = w["q_weight"].shape[1]
    ff = w["up_weight"].shape[2]
    packed = []
    for l in range(layers):
        row = jnp.concatenate([w[x][l] for x in ROW_VECTORS] + [w["up_bias"][l]])
        packed.append(jnp.pad(row, (0, d - row.shape[0]))[None])
    rows = jnp.concatenate(packed + [jnp.zeros((2 * EXTRA - layers, d), bf16)], axis=0)
    square = lambda l: [w[x][l] for x in ("q_weight", "k_weight", "v_weight", "o_weight")]
    wide = lambda l: column_blocks(w["up_weight"][l], d) + [w["down_weight"][l]]
    first = jnp.concatenate(square(0) + [rows], axis=0)
    first = gathered(first, 20)
    rest = wide(0)
    for l in range(1, layers):
        rest = rest + square(l) + wide(l)
    rest = gather(jnp.concatenate(rest, axis=0)).reshape(shards, -1, d)
    flat = first[:, 4 * per : 4 * per + layers, :]
    count = len(ROW_VECTORS)
    vecs = flat[:, :, : count * per].reshape(shards, layers, count, per).transpose(1, 2, 0, 3)
    vecs = vecs.reshape(layers, count, d)
    ups = flat[:, :, count * per : count * per + ff // shards].transpose(1, 0, 2).reshape(layers, ff // d, d)
    vec = jnp.concatenate([vecs, ups], axis=1).astype(f32)
    wides = [(rest, 0)]
    squares = [(first, 0)]
    base = 2 * per * (ff // d)
    for l in range(1, layers):
        squares.append((rest, base))
        wides.append((rest, base + 4 * per))
        base += 4 * per + 2 * per * (ff // d)
    return squares, wides, [vec[l] for l in range(layers)]


def fetch_any(w, layers):
    d = w["q_weight"].shape[2]
    squares, wides, vecs = [], [], []
    for l in range(layers):
        whole = {x: gather(w[x][l]) for x in NAMES}
        cut = lambda x: x.reshape(PIECES, x.shape[0] // PIECES, d)
        squares.append((jnp.concatenate([cut(whole[x]) for x in ("q_weight", "k_weight", "v_weight", "o_weight")], axis=1), 0))
        blocks = [cut(x) for x in column_blocks(whole["up_weight"], d)] + [cut(whole["down_weight"])]
        wides.append((jnp.concatenate(blocks, axis=1), 0))
        rows = [whole[x][None] for x in ROW_VECTORS] + [whole["up_bias"].reshape(-1, d)]
        vecs.append(jnp.concatenate(rows, axis=0).astype(f32))
    return squares, wides, vecs


def over_rep(x):
    size = lax.axis_size("rep")
    if size == 1:
        return x.astype(f32)
    other = lax.ppermute(x, "rep", [(i, (i + 1) % size) for i in range(size)])
    return x.astype(f32) + other.astype(f32)


def restack(grads_square, grads_wide, d, ff):
    per = d // PIECES
    blocks = ff // d
    gs, gw = grads_square, grads_wide
    out = {x: gs[:, j * per : (j + 1) * per].reshape(d, d) for j, x in enumerate(("q_weight", "k_weight", "v_weight", "o_weight"))}
    out["up_weight"] = jnp.concatenate([gw[:, j * per : (j + 1) * per].reshape(d, d) for j in range(blocks)], axis=1)
    out["down_weight"] = gw[:, blocks * per : 2 * blocks * per].reshape(ff, d)
    count = per // (d // 128)
    vs = gs[:, 4 * per : 4 * per + count].reshape(d, 128)
    vw = gw[:, 2 * blocks * per : 2 * blocks * per + count].reshape(PIECES, per, 128)
    for j, x in enumerate(("ln1_gain", "ln1_bias", "o_bias", "q_bias", "v_bias")):
        out[x] = vs[:, j]
    for j, x in enumerate(("ln2_gain", "ln2_bias", "down_bias")):
        out[x] = vw[:, :, j].reshape(d)
    out["up_bias"] = vw[:, :, 3 : 3 + blocks].transpose(0, 2, 1).reshape(ff)
    sums = {}
    for x, g in out.items():
        sums[x] = over_rep(lax.psum_scatter(g, "fsdp", scatter_dimension=0, tiled=True))
    return sums


def finish_kernel(layers, blocks, *refs):
    ins, outs, cols_ref = refs[: 2 * layers], dict(zip(NAMES, refs[2 * layers : -1])), refs[-1]
    per = outs["q_weight"].shape[1]
    width = outs["q_weight"].shape[2]
    lanes = width // 128
    for l in range(layers):
        square, wide = ins[2 * l], ins[2 * l + 1]
        for j, x in enumerate(("q_weight", "k_weight", "v_weight", "o_weight")):
            outs[x][l] = square[j * per : (j + 1) * per, :].astype(f32)
        for j in range(blocks):
            outs["up_weight"][l, :, j * width : (j + 1) * width] = wide[j * per : (j + 1) * per, :].astype(f32)
        outs["down_weight"][l] = wide[blocks * per : 2 * blocks * per, :].astype(f32)
        for ref, base, names in (
            (square, 4 * per, ("ln1_gain", "ln1_bias", "o_bias", "q_bias", "v_bias")),
            (wide, 2 * blocks * per, ("ln2_gain", "ln2_bias", "down_bias")),
        ):
            for m in range(lanes):
                part = ref[base : base + per // lanes, m * 128 : (m + 1) * 128].astype(f32)
                cols_ref[pl.ds(m, per // lanes, stride=lanes), :] = part
            turned = cols_ref[...].T
            for j, x in enumerate(names):
                outs[x][l : l + 1, :] = turned[j : j + 1, :]
            if ref is wide:
                for c in range(blocks):
                    row = turned[len(names) + c : len(names) + c + 1, :]
                    outs["up_bias"][l : l + 1, c * per : (c + 1) * per] = row


def finish(pairs, d, ff):
    layers, per = len(pairs), d // PIECES
    shapes = {x: (layers, per) for x in NAMES}
    for x in ("q_weight", "k_weight", "v_weight", "o_weight"):
        shapes[x] = (layers, per, d)
    shapes["up_weight"], shapes["down_weight"], shapes["up_bias"] = (layers, per, ff), (layers, ff // PIECES, d), (layers, ff // PIECES)
    args = [x for pair in pairs for x in pair]
    return pl.pallas_call(
        functools.partial(finish_kernel, layers, ff // d),
        name="finish",
        in_specs=[full(x.shape) for x in args],
        out_specs=[full(shapes[x]) for x in NAMES],
        out_shape=[sds(shapes[x], f32) for x in NAMES],
        scratch_shapes=[pltpu.VMEM((per, 128), f32)],
        compiler_params=pltpu.CompilerParams(vmem_limit_bytes=VMEM_BYTES),
    )(*args)


def on_device(tokens, segment, live, cotangent, *weights):
    w = dict(zip(NAMES, weights))
    layers, per, d = w["q_weight"].shape
    ff = w["up_weight"].shape[2]
    shards = lax.axis_size("fsdp")
    even = shards == PIECES and lax.axis_size("rep") == 2
    squares, wides, vecs = fetch_even(w, layers, shards) if even else fetch_any(w, layers)
    hidden = tokens
    kept = []
    for l in range(layers - 1):
        g, *saved = attn_forward(hidden, squares[l], vecs[l], segment)
        after, *more = ff_forward(g, wides[l], vecs[l], ff)
        kept.append((hidden, g, saved, more))
        hidden = after
    l = layers - 1
    g, *saved = attn_forward(hidden, squares[l], vecs[l], segment)
    block_out, grad, gw = ff_last(g, wides[l], vecs[l], cotangent, live, ff)
    if not even:
        grad, gs = attn_backward(hidden, grad, squares[l], vecs[l], saved)
        results = [restack(gs, gw, d, ff)]
        for l in reversed(range(layers - 1)):
            hidden, g, saved, more = kept[l]
            grad, gw = ff_backward(g, wides[l], vecs[l], grad, *more)
            grad, gs = attn_backward(hidden, grad, squares[l], vecs[l], saved)
            results.insert(0, restack(gs, gw, d, ff))
    else:
        grad, gs, rw = attn_backward(hidden, grad, squares[l], vecs[l], saved, (gw, 2), 2 + 2 * l)
        pairs = []
        for l in reversed(range(layers - 1)):
            hidden, g, saved, more = kept[l]
            grad, gw, rs = ff_backward(g, wides[l], vecs[l], grad, *more, carry=(gs, 1), ident=3 + 2 * l)
            pairs.insert(0, (rs, rw))
            grad, gs, rw = attn_backward(hidden, grad, squares[l], vecs[l], saved, (gw, 2), 2 + 2 * l)
        pairs.insert(0, (reduced(gs, 1, 1), rw))
        return (block_out, grad) + tuple(finish(pairs, d, ff))
    return (block_out, grad) + tuple(jnp.stack([r[x] for r in results]) for x in NAMES)


def solution(mesh):
    tok = P(("fsdp", "rep"), None)
    specs = tuple(P(None, "fsdp", None) if x.endswith("weight") else P(None, "fsdp") for x in NAMES)
    return jax.shard_map(
        on_device,
        mesh=mesh,
        in_specs=(tok, tok, tok, tok) + specs,
        out_specs=(tok, tok) + specs,
        check_vma=False,
    )
```

time: 2070 us -> 529 us (0.26)
  matrix products: 773 us -> 0 us
  waiting for transfers between devices: 505 us -> 38.9 us
  Pallas kernels: 0 us -> 459 us
  other arithmetic: 422 us -> 0.01 us
  blocking collectives: 202 us -> 0 us
  local copies, waits for them, and re-layouts: 138 us -> 8 us
    dot_general x74 -> x0, matrix products: 773 us -> none  [the longest x12 175 us: masked_scores(): jnp.einsum('qhd,khd->hqk', query_heads, key_heads, preferred_element_type...]
    pallas_call x0 -> x10, Pallas kernels: none -> 459 us  [the longest x6 325 us: call(): pl.pallas_call(body, name=name, in_specs=specs, out_specs=out_specs, out_...]
    reduce_scatter x24 -> x0, waiting for transfers between devices: 377 us -> none  [the longest x2 110 us: on_device(): lax.psum_scatter(grad_terms[11], 'fsdp', scatter_dimension=0, tiled=True)]
    sub x4 -> x0, other arithmetic: 162 us -> none  [one_block(): exponent = jnp.exp(scores - row_peak)]
    convert_element_type x38 -> x1, other arithmetic: 144 us -> 0.01 us  [fetch_even(): vec = jnp.concatenate([vecs, ups], axis=1).astype(f32)]
    unnamed x4 -> x0, blocking collectives: 137 us -> none
    reduce_sum x24 -> x0, other arithmetic: 90.4 us -> none  [the longest x4 61.3 us: one_block(): row_total = jnp.sum(exponent, axis=-1, keepdims=True)]
    all_gather x12 -> x1, waiting for transfers between devices: 124 us -> 38.9 us  [gather(): return lax.all_gather(x, axis, axis=0, tiled=True)]
  transfers between devices with their start and end apart: 36 -> 1, of which waited for: 21 -> 1; matrix products, arithmetic and copies ran while one was open for 60% -> 0% of each run, Pallas kernels for 0% -> 19%
where the time goes in v1:
time: 529 us; the launch traced here: 521 us
  Pallas kernels  459 us (87%)
  waiting for transfers between devices  38.9 us (7%)
  between operations  15.1 us (3%)
  local copies, waits for them, and re-layouts  8 us (2%)
    pallas_call x6, Pallas kernels, call(): pl.pallas_call(body, name=name, in_specs=specs, out_specs=out_specs, out_...  325 us
    pallas_call x1, Pallas kernels, gathered(): pl.pallas_call(functools.partial(gather_kernel, ident), name='gather', in...  63.8 us
    pallas_call x1, Pallas kernels, reduced(): pl.pallas_call(functools.partial(reduction_kernel, subs), name='reduction...  45.2 us
    all_gather x1, waiting for transfers between devices, gather(): return lax.all_gather(x, axis, axis=0, tiled=True)  38.9 us
    pallas_call x1, Pallas kernels, ff_forward(): pl.pallas_call(functools.partial(ff_forward_kernel, base), name='ff_forwa...  21.6 us
  transfers between devices with their start and end apart: 1, of which 1 were waited for; matrix products, arithmetic and copies ran while one was open for 0% of the time, Pallas kernels for 19%

profile of v1, /device:TPU:0, one launch (start us, length us, event | category | flops | bytes accessed | tf_op | source)
XLA Modules:
  0.0 521.2 jit_solution(5985552876279581834)
XLA Ops:
  7.2 0.0 copy-start.3
  7.2 0.0 copy-start.5
  7.2 0.0 copy-start.4
  7.2 0.0 copy-start.7
  7.2 0.0 copy-start.6
  7.2 0.0 all-gather.2.cloned.1.call-start
  7.3 1.2 slice_bitcast_fusion
  8.5 0.0 copy-done.3
  8.6 0.0 copy-done.5
  8.6 0.0 copy-done.4
  8.6 0.0 copy-done.7
  8.6 0.0 copy-start.8
  8.6 0.0 copy-start.9
  8.6 0.0 copy-start.10
  8.7 0.0 copy-start.11
  8.7 0.0 copy-start.12
  8.7 0.0 copy-start.13
  8.7 0.0 copy-start.14
  8.7 0.0 copy-start.15
  8.7 0.0 copy-start.16
  8.7 0.0 copy-done.6
  8.9 0.0 copy-start.2
  8.9 1.1 copy-done.2
  10.0 0.0 all-gather.2.cloned.1.call-update
  10.0 0.0 copy-done.8
  10.0 0.0 copy-done.9
  10.1 0.0 copy-done.10
  10.1 0.0 copy-done.11
  10.1 0.0 copy-done.12
  10.1 0.0 copy-done.13
  10.1 0.0 copy-done.14
  10.1 0.0 copy-done.15
  10.2 0.0 copy-done.16
  10.2 0.1 concatenate.16
  10.3 0.1 concatenate.15
  10.5 0.2 concatenate.17.x_any
  10.7 63.8 %gather.1 = bf16[2,2,2,2,224,768]{5,4,3,2,1,0:T(8,128)(2,1)S(1)} custom-call(bf16[224,768]{1,0:T(8,128)(2,1)S(1)} %concatenate.17.x_any), custom_call_target="tpu_custom_call" | custom-call | bytes 104857600 | tf_op jit(solution)/shard_map/gather/pallas_call | solution.py:337
  74.5 0.0 copy-start
  74.6 2.3 copy-done
  76.9 0.1 reshape.64
  77.0 0.1 reshape.62
  77.1 0.1 reshape.63
  77.3 0.6 slice_bitcast_fusion.6
  77.9 36.0 %attn_forward.2 = (f32[1024,768]{1,0:T(8,128)}, bf16[768,1024]{1,0:T(8,128)(2,1)}, bf16[16,64,1024]{2,1,0:T(8,128)(2,1)}, bf16[16,64,1024]{2,1,0:T(8,128)(2,1)},...) custom-call(bf16[1024,768]{1,0:T(8,128)(2,1)} %refs_0_.1, ...), custom_call_target="tpu_custom_call" | custom-call | flops 22011707392 | bytes 31457280 | tf_op jit(solution)/shard_map/attn_forward/pallas_call | solution.py:438
  113.9 38.9 %all-gather.2.cloned.1.call-done = bf16[15360,768]{1,0:T(8,128)(2,1)} async-done(((bf16[960,768]{1,0:T(8,128)(2,1)}), bf16[15360,768]{1,0:T(8,128)(2,1)}) %all-gather.2.cloned.1.call-update) | async-done | bytes 23592976 | tf_op jit(solution)/shard_map/all_gather | solution.py:829
  152.9 21.6 %ff_forward.1 = (f32[1024,768]{1,0:T(8,128)}, bf16[1024,768]{1,0:T(8,128)(2,1)}, bf16[1024,3072]{1,0:T(8,128)(2,1)}, bf16[1024,3072]{1,0:T(8,128)(2,1)}) custom-call(f32[1024,768]{1,0:T(8,128)} %get-tuple-element.62.g_ref.refs_0_, bf16[16,960,768]{2,1,0:T(8,128)(2,1)} %bitcast.79, f32[12,768]{1,0:T(8,128)} %get-tuple-element.112.vec_ref.refs_2_.refs_3_), custom_call_target="tpu_custom_call" | custom-call | flops 9663676416 | bytes 31457280 | tf_op jit(solution)/shard_map/ff_forward/pallas_call | solution.py:528
  174.4 36.2 %attn_forward.3 = (f32[1024,768]{1,0:T(8,128)}, bf16[768,1024]{1,0:T(8,128)(2,1)}, bf16[16,64,1024]{2,1,0:T(8,128)(2,1)}, bf16[16,64,1024]{2,1,0:T(8,128)(2,1)},...) custom-call(f32[1024,768]{1,0:T(8,128)} %get-tuple-element.63.h_ref.refs_0_, ...), custom_call_target="tpu_custom_call" | custom-call | flops 22011707392 | bytes 31457280 | tf_op jit(solution)/shard_map/attn_forward/pallas_call | solution.py:438
  210.7 47.2 %ff_last.1 = (bf16[1024,768]{1,0:T(8,128)(2,1)}, f32[1024,768]{1,0:T(8,128)}, bf16[16,416,768]{2,1,0:T(8,128)(2,1)}) custom-call(f32[1024,768]{1,0:T(8,128)} %get-tuple-element.64.g_ref, bf16[16,960,768]{2,1,0:T(8,128)(2,1)} %bitcast.81, f32[12,768]{1,0:T(8,128)} %get-tuple-element.111.vec_ref.refs_3_, bf16[1024,768]{1,0:T(8,128)(2,1)} %cot_ref.1, ...), custom_call_target="tpu_custom_call" | custom-call | flops 28991029248 | bytes 31457280 | tf_op jit(solution)/shard_map/ff_last/pallas_call | solution.py:438
  257.9 75.3 %attn_backward.2 = (f32[1024,768]{1,0:T(8,128)}, bf16[16,224,768]{2,1,0:T(8,128)(2,1)}, bf16[416,768]{1,0:T(8,128)(2,1)}) custom-call(f32[1024,768]{1,0:T(8,128)} %get-tuple-element.63.h_ref.refs_0_, f32[1024,768]{1,0:T(8,128)} %get-tuple-element.66.refs_1_, bf16[16,960,768]{2,1,0:T(8,128)(2,1)} %bitcast.82, f32[12,768]{1,0:T(8,128)} %get-tuple-element.111.vec_ref.refs_3_, ...), custom_call_target="tpu_custom_call" | custom-call | flops 52613349376 | bytes 41943040 | tf_op jit(solution)/shard_map/attn_backward/pallas_call | solution.py:438
  333.2 56.3 %ff_backward.1 = (f32[1024,768]{1,0:T(8,128)}, bf16[16,416,768]{2,1,0:T(8,128)(2,1)}, bf16[224,768]{1,0:T(8,128)(2,1)}) custom-call(f32[1024,768]{1,0:T(8,128)} %get-tuple-element.62.g_ref.refs_0_, bf16[16,960,768]{2,1,0:T(8,128)(2,1)} %bitcast.83, f32[12,768]{1,0:T(8,128)} %get-tuple-element.112.vec_ref.refs_2_.refs_3_, ...), custom_call_target="tpu_custom_call" | custom-call | flops 19327352832 | bytes 41943040 | tf_op jit(solution)/shard_map/ff_backward/pallas_call | solution.py:438
  389.6 74.0 %attn_backward.3 = (f32[1024,768]{1,0:T(8,128)}, bf16[16,224,768]{2,1,0:T(8,128)(2,1)}, bf16[416,768]{1,0:T(8,128)(2,1)}) custom-call(bf16[1024,768]{1,0:T(8,128)(2,1)} %refs_0_.1, f32[1024,768]{1,0:T(8,128)} %get-tuple-element.79.refs_1_, bf16[16,224,768]{2,1,0:T(8,128)(2,1)} %bitcast.76, f32[12,768]{1,0:T(8,128)} %get-tuple-element.112.vec_ref.refs_2_.refs_3_, ...), custom_call_target="tpu_custom_call" | custom-call | flops 52613349376 | bytes 41943040 | tf_op jit(solution)/shard_map/attn_backward/pallas_call | solution.py:438
  463.5 0.0 copy-start.1
  463.5 45.2 %reduction.1.refs_0_ = bf16[224,768]{1,0:T(8,128)(2,1)} custom-call(bf16[2,2,2,2,224,768]{5,4,3,2,1,0:T(8,128)(2,1)} %bitcast.77), custom_call_target="tpu_custom_call" | custom-call | tf_op jit(solution)/shard_map/reduction/pallas_call | solution.py:282
  508.8 3.4 finish.1
  512.2 0.0 copy-done.1
  512.2 1.7 copy.54
  (31 shorter events, 0.3 us)
Async XLA Ops:
  7.2 1.3 copy-start.3
  7.2 1.4 copy-start.5
  7.2 1.4 copy-start.4
  7.2 1.4 copy-start.7
  7.2 1.5 copy-start.6
  7.2 145.6 %all-gather.2.cloned.1.call-start = ((), (), s32[]{:S(2)}) async-start(), calls=%async_computation | async-start | bytes 25067520 | tf_op jit(solution)/shard_map/all_gather | solution.py:829
  8.6 1.4 copy-start.8
  8.6 1.4 copy-start.9
  8.6 1.4 copy-start.10
  8.7 1.4 copy-start.11
  8.7 1.4 copy-start.12
  8.7 1.4 copy-start.13
  8.7 1.4 copy-start.14
  8.7 1.4 copy-start.15
  8.7 1.4 copy-start.16
  8.9 1.1 copy-start.2
  74.5 2.3 copy-start
  463.5 48.7 %copy-start.1 = (f32[1024,768]{1,0:T(8,128)S(1)}, f32[1024,768]{1,0:T(8,128)}, u32[]{:S(2)}) copy-start(f32[1024,768]{1,0:T(8,128)} %get-tuple-element.159) | copy-start | bytes 9437188
Sparse Core Ops, SparseCore 0:
  10.2 142.5 all-gather.1

commit v2 on v1

--- a/solution.py
+++ b/solution.py
@@ -18,10 +18,13 @@
 FORWARD_PARTS = 1
 BACKWARD_PARTS = 4
 UNROLL = 2
-ATTN_PLAN = {0: [(0, 0)], 1: [(1, 0)], 2: [(0, 1)], 5: [(1, 1), (0, 2)], 7: [(1, 2), (0, 3)]}
-ATTN_MIDDLE = []
-ATTN_TILES = {0: [(1, 3), (0, 4)], 3: [(1, 4), (0, 5)]}
+ATTN_PLAN = {2: [(0, 1)], 4: [(1, 1)], 5: [(0, 2)], 6: [(1, 2)], 7: [(0, 3)]}
+ATTN_MIDDLE = [(1, 3), (0, 4)]
+ATTN_TILES = {0: [(0, 5)], 1: [(1, 4)]}
 ATTN_END = [(1, 5)]
+FF_TILES = {3: [(0, 1)]}
+FF_BLOCKS = {1: [(0, 2)], 2: [(0, 3)], 3: [(0, 4)]}
+FF_END = [(0, 5)]
 VMEM_BYTES = 60 * 1024 * 1024
 
 
@@ -121,14 +124,24 @@
             "x": {"fsdp": me, "rep": 1 - x},
         }
 
-    def meet(self):
+    def meet(self, names="cylhx"):
         barrier = pltpu.get_barrier_semaphore()
-        for who in self.peer.values():
-            pl.semaphore_signal(barrier, inc=1, device_id=who, device_id_type=pl.DeviceIdType.MESH)
-        pl.semaphore_wait(barrier, len(self.peer))
-
-
-class Reduction(Links):
+        for name in names:
+            pl.semaphore_signal(barrier, inc=1, device_id=self.peer[name], device_id_type=pl.DeviceIdType.MESH)
+        pl.semaphore_wait(barrier, len(names))
+
+    def remote(self, src, dst, sems, who):
+        return pltpu.make_async_remote_copy(
+            src_ref=src,
+            dst_ref=dst,
+            send_sem=sems[0],
+            recv_sem=sems[1],
+            device_id=self.peer[who],
+            device_id_type=pl.DeviceIdType.MESH,
+        )
+
+
+class Reduction:
     ORDERS = ("yxlh", "xylh", "lhyx")
     STEPS = 6
 
@@ -146,7 +159,7 @@
 
     @classmethod
     def scratch(cls, rows, subs, width):
-        shapes = [pltpu.VMEM((2, 2, 2, rows, width), bf16)] * 2
+        shapes = []
         for order, _, count in cls.paths(rows, subs):
             free = 3
             for axis in order:
@@ -155,38 +168,18 @@
                 else:
                     free -= 1
                 shapes.append(pltpu.VMEM((2,) * free + (count, width), bf16))
-        return shapes + [pltpu.SemaphoreType.DMA((18 * subs,)), pltpu.SemaphoreType.DMA((21 * subs,))]
-
-    def __init__(self, subs, v_any, fin_ref, refs):
-        self.subs, self.v, self.fin = subs, v_any, fin_ref
-        self.own, self.got = refs[0], refs[1]
-        self.bufs = [refs[2 + 4 * k : 6 + 4 * k] for k in range(3 * subs)]
+        return shapes + [pltpu.SemaphoreType.DMA((15 * subs,)), pltpu.SemaphoreType.DMA((15 * subs,))]
+
+    @staticmethod
+    def scratch_count(subs):
+        return 12 * subs + 2
+
+    def __init__(self, links, subs, own, core, fin_ref, refs):
+        self.links, self.subs, self.own, self.core, self.fin = links, subs, own, core, fin_ref
+        self.at = links.at
+        self.bufs = [refs[4 * k : 4 + 4 * k] for k in range(3 * subs)]
         self.send_sem, self.recv_sem = refs[-2], refs[-1]
-        self.parts = self.paths(self.own.shape[3], subs)
-        super().__init__()
-
-    def remote(self, src, dst, sem, who):
-        return pltpu.make_async_remote_copy(
-            src_ref=src,
-            dst_ref=dst,
-            send_sem=self.send_sem.at[sem],
-            recv_sem=self.recv_sem.at[sem],
-            device_id=self.peer[who],
-            device_id_type=pl.DeviceIdType.MESH,
-        )
-
-    def local(self, path):
-        _, start, count = self.parts[path]
-        rows = pl.ds(start, count)
-        return pltpu.make_async_copy(
-            self.v.at[:, :, :, self.at["c"], rows, :], self.own.at[:, :, :, rows, :], self.recv_sem.at[18 * self.subs + path]
-        )
-
-    def cores(self, path):
-        _, start, count = self.parts[path]
-        rows = pl.ds(start, count)
-        src = self.v.at[:, :, :, 1 - self.at["c"], rows, :]
-        return self.remote(src, self.got.at[:, :, :, rows, :], 6 * path, "c")
+        self.parts = self.paths(own.shape[-2], subs)
 
     def places(self, path, step):
         order, start, count = self.parts[path]
@@ -204,27 +197,26 @@
                 fixed[axis] = self.at[axis]
         return send, (fixed, rows)
 
-    @staticmethod
-    def index(place, free=()):
+    def index(self, place, free=()):
         fixed, rows = place
         found, free = [], list(free)
         for axis in "hly":
             found.append(fixed[axis] if axis in fixed else (free.pop(0) if free else slice(None)))
+        if self.core is not None:
+            found.append(self.core)
         return (*found, rows, slice(None))
 
     def exchange(self, path, step):
-        sem = 6 * path + 1 + step
+        sems = (self.send_sem.at[5 * path + step], self.recv_sem.at[5 * path + step])
         if step == 4:
             keep = self.places(path, 3)[1]
-            return self.remote(self.own.at[self.index(keep)], self.fin.at[keep[1], :], sem, "x")
+            return self.links.remote(self.own.at[self.index(keep)], self.fin.at[keep[1], :], sems, "x")
         send, _ = self.places(path, step)
-        return self.remote(self.own.at[self.index(send)], self.bufs[path][step], sem, self.parts[path][0][step])
-
-    def start(self):
-        self.meet()
-        for path in range(3 * self.subs):
-            self.cores(path).start()
-            self.local(path).start()
+        axis = self.parts[path][0][step]
+        return self.links.remote(self.own.at[self.index(send)], self.bufs[path][step], sems, axis)
+
+    def begin(self, path):
+        self.exchange(path, 0).start()
 
     def add(self, place, other):
         free = 3 - len(place[0])
@@ -241,14 +233,6 @@
             one(0, 0)
 
     def advance(self, path, step):
-        if step == 0:
-            self.cores(path).wait()
-            self.local(path).wait()
-            _, start, count = self.parts[path]
-            place = ({}, pl.ds(start, count))
-            self.add(place, lambda bits: self.got[self.index(place, bits)])
-            self.exchange(path, 0).start()
-            return
         k = step - 1
         self.exchange(path, k).wait()
         if k == 4:
@@ -266,30 +250,51 @@
                 self.advance(path, step)
 
 
-def reduction_kernel(subs, v_any, fin_ref, *refs):
-    red = Reduction(subs, v_any, fin_ref, refs)
-    red.start()
-    for step in range(Reduction.STEPS):
-        red.run([(sub, step) for sub in range(subs)])
-
-
-def six(x):
-    return x.reshape((2, 2, 2, 2) + x.shape[1:])
-
-
-def reduced(x, subs, ident):
-    rows, width = x.shape[1:]
-    return pl.pallas_call(
-        functools.partial(reduction_kernel, subs),
-        name="reduction",
-        in_specs=[pl.BlockSpec(memory_space=pl.ANY)],
-        out_specs=pl.BlockSpec(memory_space=pltpu.VMEM),
-        out_shape=sds((rows, width), bf16),
-        scratch_shapes=Reduction.scratch(rows, subs, width),
-        compiler_params=pltpu.CompilerParams(
-            vmem_limit_bytes=VMEM_BYTES, collective_id=ident, has_side_effects=True
-        ),
-    )(six(x))
+class Halving:
+    def __init__(self, links, grad, refs, half_any):
+        self.links, self.grad, self.half = links, grad, half_any
+        self.got, self.send_sem, self.recv_sem, self.out_sem = refs
+        self.core = links.at["c"]
+
+    @staticmethod
+    def scratch(rows, width, regions):
+        dma = pltpu.SemaphoreType.DMA
+        return [pltpu.VMEM((2, 2, 2, rows, width), bf16), dma((regions,)), dma((regions,)), dma]
+
+    def copy(self, k, where):
+        h, l, y, rows = where
+        src = self.grad.at[h, l, y, 1 - self.core, rows, :]
+        sems = (self.send_sem.at[k], self.recv_sem.at[k])
+        return self.links.remote(src, self.got.at[h, l, y, rows, :], sems, "c")
+
+    def send(self, k, where):
+        self.copy(k, where).start()
+
+    def settle(self, k, where):
+        self.copy(k, where).wait()
+        h, l, y, rows = where
+        whole = [isinstance(i, slice) for i in (h, l, y)]
+        free = sum(whole)
+
+        def one(i, carry):
+            bits = [lax.rem(lax.div(i, 2 ** (free - 1 - b)), 2) for b in range(free)]
+            at = [bits.pop(0) if w else i for w, i in zip(whole, (h, l, y))]
+            mine = (*at, self.core, rows, slice(None))
+            self.grad[mine] = self.grad[mine] + self.got[(*at, rows, slice(None))]
+            return carry
+
+        lax.fori_loop(0, 2**free, one, 0)
+        if self.half is not None:
+            pltpu.make_async_copy(
+                self.grad.at[h, l, y, self.core, rows, :], self.half.at[h, l, y, rows, :], self.out_sem
+            ).start()
+
+    def drain(self):
+        if self.half is not None:
+            every = slice(None)
+            pltpu.make_async_copy(
+                self.grad.at[every, every, every, self.core, every, every], self.half, self.out_sem
+            ).wait()
 
 
 def gather_kernel(ident, x_any, out_any, send_sem, recv_sem, own_sem):
@@ -322,7 +327,7 @@
             device_id_type=pl.DeviceIdType.MESH,
         )
 
-    paths = Reduction.paths(rows, 1)
+    paths = [("xylh", start, count) for _, start, count in Reduction.paths(rows, 1)]
     for path in paths:
         copy(path, 0).start()
     for step in range(5):
@@ -350,20 +355,20 @@
 
 
 def attn_forward_kernel(
-    base, red, h_ref, w_any, vec_ref, seg_ref,
-    g_ref, at_ref, qe_ref, ke_ref, ve_ref, ot_ref, ol_ref, w_ref, w_sem,
+    tools, h_ref, w_ref, vec_ref, seg_ref,
+    g_ref, at_ref, qe_ref, ke_ref, ve_ref, ot_ref, ol_ref,
 ):
     length, width = h_ref.shape
     hd = width // HEADS
     rows = width // PIECES
     scale = math.log2(math.e) / math.sqrt(hd)
-    fetch = window(w_any, w_ref, w_sem, base)
-    fetch.start()
+    tools.wait(0)
     x = h_ref[...].astype(f32)
     xh, _ = normalised(x)
     a = (xh * vec_ref[0:1, :] + vec_ref[1:2, :]).astype(bf16)
     at_ref[...] = a.T
-    fetch.wait()
+    tools.flush(1, ...)
+    tools.wait(1)
     q = (mm(a, weight(w_ref, 0, rows)) + vec_ref[2:3, :]).astype(bf16)
     qe_ref[:, 0:hd, :] = q.T.reshape(HEADS, hd, length)
     k = mm(a, weight(w_ref, 1, rows)).astype(bf16)
@@ -374,6 +379,8 @@
     qe_ref[:, hd:, :] = jnp.broadcast_to(mask_q.astype(bf16)[None], (HEADS, EXTRA, length))
     ke_ref[:, hd:, :] = jnp.broadcast_to(mask_k.astype(bf16)[None], (HEADS, EXTRA, length))
     ve_ref[:, hd:, :] = jnp.ones((HEADS, EXTRA, length), bf16)
+    tools.flush(3, ...)
+    tools.flush(4, ...)
     row = lax.broadcasted_iota(jnp.int32, (EXTRA, length // FORWARD_PARTS), 0)
 
     part = length // FORWARD_PARTS
@@ -395,14 +402,17 @@
             ext = jnp.where(row == 6, low.astype(f32), mask_q[:, cols])
             ext = jnp.where(row == 4, hi.astype(f32), jnp.where(row == 5, mid.astype(f32), ext))
             qe_ref[i, hd:, cols] = ext.astype(bf16)
-
-    def pair(j, carry):
+        for k in (2, 5, 6):
+            tools.flush(k, i)
+
+    def some_heads(j, carry):
         for k in range(UNROLL):
             head(UNROLL * j + k)
         return carry
 
-    lax.fori_loop(0, HEADS // UNROLL, pair, 0)
+    lax.fori_loop(0, HEADS // UNROLL, some_heads, 0)
     g_ref[...] = x + (mm_tn(joined(ot_ref), weight(w_ref, 3, rows)) + vec_ref[4:5, :])
+    tools.flush(0, ...)
 
 
 def full(shape):
@@ -412,36 +422,128 @@
 ANY = pl.BlockSpec(memory_space=pl.ANY)
 
 
-def call(kernel, name, args, specs, outs, flops, nbytes, scratch, carry=None, ident=None):
-    n_in, n_out, n_scratch = len(args), len(outs), len(scratch)
-    args, outs, scratch = list(args), list(outs), list(scratch)
-    specs = list(specs)
-    out_specs = [full(s.shape) for s in outs]
-    if carry is None:
-        body = functools.partial(kernel, None)
-    else:
-        grads, subs = carry
-        rows, width = grads.shape[1:]
-        args.append(six(grads))
-        specs.append(ANY)
-        outs.append(sds((rows, width), bf16))
-        out_specs.append(full((rows, width)))
-        scratch += Reduction.scratch(rows, subs, width)
-
-        def body(*refs):
-            ins, v = refs[:n_in], refs[n_in]
-            results = refs[n_in + 1 : n_in + 1 + n_out]
-            fin = refs[n_in + 1 + n_out]
-            rest = refs[n_in + 2 + n_out :]
-            kernel(Reduction(subs, v, fin, rest[n_scratch:]), *ins, *results, *rest[:n_scratch])
+class Late:
+    def __init__(self, turn, base=0, rows=None):
+        self.turn, self.base, self.rows = turn, base, rows
+
+
+class Tools:
+    red = pair = tail = None
+
+    def wait(self, *numbers):
+        for i in numbers:
+            self.fetch[i].wait()
+
+    def flush(self, k, index):
+        pltpu.make_async_copy(self.made[k].at[index], self.out[k].at[index], self.out_sem.at[k]).start()
+
+    def finish(self):
+        for k in self.made:
+            pltpu.make_async_copy(self.made[k], self.out[k], self.out_sem.at[k]).wait()
+        if self.pair is not None:
+            self.pair.drain()
+
+
+def call(kernel, name, args, specs, outs, flops, nbytes, scratch, grads=None, ident=None, carry=None, tail=False):
+    args, specs = list(args), list(specs)
+    n_args = len(args)
+    late = sorted((i for i in range(n_args) if isinstance(specs[i], Late)), key=lambda i: specs[i].turn)
+    shapes = {}
+    for i in late:
+        a = args[i]
+        rows = specs[i].rows
+        shapes[i] = (a.shape[0], rows) + a.shape[2:] if rows else a.shape
+    use = [pltpu.VMEM(shapes[i], args[i].dtype) for i in late] + [pltpu.SemaphoreType.DMA((max(1, len(late)),))]
+    use += [pltpu.VMEM(o.shape, o.dtype) for o in outs] + [pltpu.SemaphoreType.DMA((max(1, len(outs)),))]
+    results = list(outs)
+    out_specs = [ANY] * len(outs)
+    if grads is not None:
+        rows, width, regions = grads
+        six_shape = (2, 2, 2, 2, rows, width)
+        use.append(pltpu.VMEM(six_shape, bf16))
+        if ident is None:
+            use.append(pltpu.SemaphoreType.DMA)
+            results.append(sds(six_shape, bf16))
+            out_specs.append(ANY)
+        else:
+            use += Halving.scratch(rows, width, regions)
+            if tail:
+                use += Reduction.scratch(rows, 1, width)
+                results.append(sds((rows, width), bf16))
+                out_specs.append(full((rows, width)))
+            else:
+                results.append(sds((2, 2, 2, rows, width), bf16))
+                out_specs.append(ANY)
+    if carry is not None:
+        held, subs = carry
+        crows, cwidth = held.shape[3:]
+        args.append(held)
+        specs.append(None)
+        use += [pltpu.VMEM(held.shape, bf16), pltpu.SemaphoreType.DMA] + Reduction.scratch(crows, subs, cwidth)
+        results.append(sds((crows, cwidth), bf16))
+        out_specs.append(full((crows, cwidth)))
+    n_use = len(use)
+    base_specs = [ANY if s is None or isinstance(s, Late) else s for s in specs]
+
+    def body(*refs):
+        refs = list(refs)
+        ins, refs = refs[: len(args)], refs[len(args) :]
+        res, refs = refs[: len(results)], refs[len(results) :]
+        used, own_scratch = refs[:n_use], refs[n_use:]
+        take = lambda n: [used.pop(0) for _ in range(n)]
+        t = Tools()
+        buffers, (in_sem,) = take(len(late)), take(1)
+        made, (t.out_sem,) = take(len(outs)), take(1)
+        t.fetch = {}
+        for k, i in enumerate(late):
+            src = ins[i]
+            if specs[i].rows:
+                src = src.at[:, specs[i].base : specs[i].base + specs[i].rows]
+            t.fetch[i] = pltpu.make_async_copy(src, buffers[k], in_sem.at[k])
+            ins[i] = buffers[k]
+        t.made, t.out = dict(enumerate(made)), dict(enumerate(res))
+        links = Links() if ident is not None else None
+        grad = ()
+        after = len(outs)
+        if grads is not None:
+            (grad_ref,) = take(1)
+            grad = (grad_ref,)
+            if ident is None:
+                t.made[after], t.out[after] = grad_ref, res[after]
+                (t.grad_sem,) = take(1)
+            else:
+                t.pair = Halving(links, grad_ref, take(4), None if tail else res[after])
+                if tail:
+                    t.tail = Reduction(links, 1, grad_ref, links.at["c"], res[after], take(Reduction.scratch_count(1)))
+            after += 1
+        if carry is not None:
+            own, own_sem = take(2)
+            t.red = Reduction(links, subs, own, None, res[after], take(Reduction.scratch_count(subs)))
+            load = pltpu.make_async_copy(ins[n_args], own, own_sem)
+            load.start()
+        for i in late:
+            t.fetch[i].start()
+        if ident is not None:
+            links.meet("cylhx" if carry is not None or tail else "c")
+        if carry is not None:
+            load.wait()
+            for path in range(3 * subs):
+                t.red.begin(path)
+        kernel(t, *ins[:n_args], *made, *grad, *own_scratch)
+        if grads is not None and ident is None:
+            k = len(outs)
+            pltpu.make_async_copy(t.made[k], t.out[k], t.grad_sem).start()
+            pltpu.make_async_copy(t.made[k], t.out[k], t.grad_sem).wait()
+            del t.made[k]
+        t.finish()
 
     return pl.pallas_call(
         body,
         name=name,
-        in_specs=specs,
+        in_specs=base_specs,
         out_specs=out_specs,
-        out_shape=outs,
-        scratch_shapes=scratch,
+        out_shape=results,
+        scratch_shapes=use + list(scratch),
         compiler_params=pltpu.CompilerParams(
             vmem_limit_bytes=VMEM_BYTES, collective_id=ident, has_side_effects=ident is not None
         ),
@@ -481,14 +583,9 @@
         sds((HEADS, hd, n), bf16),
         sds((HEADS, hd, n), bf16),
     )
-    specs = [full(h.shape), pl.BlockSpec(memory_space=pl.ANY)]
-    specs += [full(vec.shape), pl.BlockSpec(memory_space=SMEM)]
+    specs = [Late(0), Late(1, base, 4 * rows), full(vec.shape), pl.BlockSpec(memory_space=SMEM)]
     flops = 8 * n * d * d + 2 * HEADS * 2 * n * n * 256
-    scratch = [pltpu.VMEM((PIECES, 4 * rows, d), bf16), pltpu.SemaphoreType.DMA]
-    return call(
-        functools.partial(attn_forward_kernel, base), "attn_forward", (h, square, vec, seg),
-        specs, outs, flops, 30 << 20, scratch,
-    )
+    return call(attn_forward_kernel, "attn_forward", (h, square, vec, seg), specs, outs, flops, 30 << 20, ())
 
 
 def ff_forward_kernel(base, g_ref, w_any, vec_ref, h_ref, b_ref, z_ref, s_ref, w_ref, w_sem):
@@ -543,32 +640,53 @@
 
 
 def put_vectors(grad_ref, base, cols_ref, per):
-    pad = grad_ref.shape[1] - base
-    lanes = grad_ref.shape[2] // 128
+    pad = grad_ref.shape[4] - base
+    lanes = grad_ref.shape[5] // 128
     count = per // lanes
     for m in range(lanes):
         part = cols_ref[pl.ds(m, PIECES * count, stride=lanes), :]
         part = part.reshape(PIECES, count, 128)
         part = jnp.concatenate([part, jnp.zeros((PIECES, pad - count, 128), f32)], axis=1)
-        grad_ref[:, base : base + pad, m * 128 : (m + 1) * 128] = part.astype(bf16)
-
-
-def ff_tail(z_ref, du_ref, b_ref, cm_ref, grad_ref, cols_ref, vecs, width, blocks, red=None):
+        part = part.reshape(2, 2, 2, 2, pad, 128)
+        grad_ref[:, :, :, :, base : base + pad, m * 128 : (m + 1) * 128] = part.astype(bf16)
+
+
+EVERY = slice(None)
+
+
+def ff_tail(tools, z_ref, du_ref, b_ref, cm_ref, grad_ref, cols_ref, vecs, width, blocks):
     rows = width // PIECES
     quarter = PIECES // blocks
     n = b_ref.shape[0]
+    pair = tools.pair
+    lower = pl.ds(rows * blocks, rows * blocks)
+
+    def regions(j):
+        up = (EVERY, EVERY, EVERY, pl.ds(pl.multiple_of(rows * j, 16), rows))
+        return (j, (lax.div(j, 2), lax.rem(j, 2), EVERY, lower)), (blocks + j, up)
+
+    def settle(j):
+        if pair is not None:
+            for k, where in regions(j):
+                pair.settle(k, where)
 
     def block(j, carry):
-        advance_at(red, j, {1: [(0, 2)], 2: [(0, 3)], 3: [(0, 4)]})
+        advance_at(tools.red, j, FF_BLOCKS)
         cols = pl.ds(pl.multiple_of(j * width, 128), width)
-        dwd = mm_tn(z_ref[:, cols], cm_ref[...])
-        grad_ref[pl.ds(quarter * j, quarter), rows * blocks : 2 * rows * blocks, :] = (
-            dwd.reshape(quarter, rows * blocks, width).astype(bf16)
-        )
+        (kd, where_d), (ku, where_u) = regions(j)
+        dwd = mm_tn(z_ref[:, cols], cm_ref[...]).reshape(2, 2, rows * blocks, width)
+        grad_ref[lax.div(j, 2), lax.rem(j, 2), :, :, lower, :] = dwd.astype(bf16)
+        if pair is not None:
+            pair.send(kd, where_d)
         dwu = mm_tn(b_ref[...], du_ref[:, cols])
-        grad_ref[:, pl.ds(pl.multiple_of(rows * j, 16), rows), :] = (
-            dwu.reshape(PIECES, rows, width).astype(bf16)
-        )
+        grad_ref[:, :, :, :, where_u[3], :] = dwu.reshape(2, 2, 2, 2, rows, width).astype(bf16)
+        if pair is not None:
+            pair.send(ku, where_u)
+
+            @pl.when(j > 0)
+            def _():
+                settle(j - 1)
+
         return carry
 
     lax.fori_loop(0, blocks, block, 0)
@@ -584,22 +702,22 @@
             piece = jnp.where(lane == len(vecs) + c, part[:, c], piece)
         cols_ref[quarter * rows * j : quarter * rows * (j + 1), :] = piece.reshape(quarter * rows, 128)
     put_vectors(grad_ref, 2 * rows * blocks, cols_ref, rows)
-    if red is not None:
-        red.run([(0, 5)])
+    if pair is not None:
+        last = (EVERY, EVERY, EVERY, pl.ds(2 * rows * blocks, 2 * EXTRA))
+        pair.send(2 * blocks, last)
+        settle(blocks - 1)
+        pair.settle(2 * blocks, last)
 
 
 def ff_last_kernel(
-    base, red, g_ref, w_any, vec_ref, cot_ref, live_ref, out_ref, dg_ref, grad_ref,
-    z_ref, du_ref, b_ref, cm_ref, cols_ref, w_ref, w_sem,
+    tools, g_ref, w_ref, vec_ref, cot_ref, live_ref, out_ref, dg_ref, grad_ref, z_ref, du_ref, b_ref, cm_ref, cols_ref,
 ):
     n, width = g_ref.shape
     rows = width // PIECES
     blocks = z_ref.shape[1] // width
     tile = n // 4
     gain = vec_ref[5:6, :]
-    fetch = window(w_any, w_ref, w_sem, base)
-    fetch.start()
-    fetch.wait()
+    tools.wait(0, 3, 1)
 
     def step(t, sums):
         sum_gain, sum_bias, sum_down = sums
@@ -628,6 +746,8 @@
             db = db + mm_nt(du, w)
         out_ref[span, :] = acc.astype(bf16)
         dg_ref[span, :] = grad + norm_back(db, xh, r, gain)
+        tools.flush(0, (span, EVERY))
+        tools.flush(1, (span, EVERY))
         sum_gain = sum_gain + jnp.sum(db * xh, axis=0, keepdims=True)
         sum_bias = sum_bias + jnp.sum(db, axis=0, keepdims=True)
         sum_down = sum_down + jnp.sum(cm.astype(f32), axis=0, keepdims=True)
@@ -635,43 +755,39 @@
 
     zero = jnp.zeros((1, width), f32)
     sums = lax.fori_loop(0, 4, step, (zero, zero, zero))
-    ff_tail(z_ref, du_ref, b_ref, cm_ref, grad_ref, cols_ref, sums, width, blocks)
-
-
-def ff_last(g, wide, vec, cot, live, ff):
+    ff_tail(tools, z_ref, du_ref, b_ref, cm_ref, grad_ref, cols_ref, sums, width, blocks)
+
+
+def ff_last(g, wide, vec, cot, live, ff, ident=None):
     wide, base = wide
     n, d = g.shape
     rows = d // PIECES
-    outs = (sds((n, d), bf16), sds((n, d), f32), sds((PIECES, 2 * rows * (ff // d) + 2 * EXTRA, d), bf16))
-    specs = [full(g.shape), pl.BlockSpec(memory_space=pl.ANY), full(vec.shape), full(cot.shape), pl.BlockSpec(memory_space=SMEM)]
+    blocks = ff // d
+    outs = (sds((n, d), bf16), sds((n, d), f32))
+    specs = [Late(0), Late(1, base, 2 * rows * blocks), full(vec.shape), Late(2), pl.BlockSpec(memory_space=SMEM)]
     scratch = [
         pltpu.VMEM((n, ff), bf16), pltpu.VMEM((n, ff), bf16), pltpu.VMEM((n, d), bf16),
         pltpu.VMEM((n, d), bf16), pltpu.VMEM((d, 128), f32),
-        pltpu.VMEM((PIECES, 2 * ff // PIECES, d), bf16), pltpu.SemaphoreType.DMA,
     ]
+    grads = (2 * rows * blocks + 2 * EXTRA, d, 2 * blocks + 1)
     return call(
-        functools.partial(ff_last_kernel, base), "ff_last", (g, wide, vec, cot, live),
-        specs, outs, 12 * n * d * ff, 30 << 20, scratch,
+        ff_last_kernel, "ff_last", (g, wide, vec, cot, live), specs, outs, 12 * n * d * ff, 30 << 20, scratch,
+        grads, ident,
     )
 
 
 def ff_backward_kernel(
-    base, red, g_ref, w_any, vec_ref, c_ref, b_ref, z_ref, s_ref, dg_ref, grad_ref, du_ref, cm_ref, cols_ref,
-    w_ref, w_sem,
+    tools, g_ref, w_ref, vec_ref, c_ref, b_ref, z_ref, s_ref, dg_ref, grad_ref, cm_ref, cols_ref,
 ):
     n, width = g_ref.shape
     rows = width // PIECES
     blocks = z_ref.shape[1] // width
     tile = n // 4
     gain = vec_ref[5:6, :]
-    fetch = window(w_any, w_ref, w_sem, base)
-    fetch.start()
-    if red is not None:
-        red.start()
-    fetch.wait()
+    tools.wait(3, 1, 6, 0)
 
     def step(t, sums):
-        advance_at(red, t, {0: [(0, 0)], 3: [(0, 1)]})
+        advance_at(tools.red, t, FF_TILES)
         sum_gain, sum_bias, sum_down = sums
         span = pl.ds(pl.multiple_of(t * tile, 16), tile)
         xh, r = normalised(g_ref[span, :])
@@ -684,9 +800,10 @@
             w = weight(w_ref, j, rows)
             wd = down(w_ref, j, rows, blocks)
             du = (s_ref[span, cols].astype(f32) * mm_nt(cm, wd)).astype(bf16)
-            du_ref[span, cols] = du
+            s_ref[span, cols] = du
             db = db + mm_nt(du, w)
         dg_ref[span, :] = grad + norm_back(db, xh, r, gain)
+        tools.flush(0, (span, EVERY))
         sum_gain = sum_gain + jnp.sum(db * xh, axis=0, keepdims=True)
         sum_bias = sum_bias + jnp.sum(db, axis=0, keepdims=True)
         sum_down = sum_down + jnp.sum(cm.astype(f32), axis=0, keepdims=True)
@@ -694,43 +811,55 @@
 
     zero = jnp.zeros((1, width), f32)
     sums = lax.fori_loop(0, 4, step, (zero, zero, zero))
-    ff_tail(z_ref, du_ref, b_ref, cm_ref, grad_ref, cols_ref, sums, width, blocks, red)
-
-
-def ff_backward(g, wide, vec, c, b, z, s, carry=None, ident=None):
+    tools.wait(5, 4)
+    ff_tail(tools, z_ref, s_ref, b_ref, cm_ref, grad_ref, cols_ref, sums, width, blocks)
+    if tools.red is not None:
+        tools.red.run(FF_END)
+
+
+def ff_backward(g, wide, vec, c, b, z, s, ident=None, carry=None):
     wide, base = wide
     n, d = g.shape
     ff = z.shape[1]
     rows = d // PIECES
-    outs = (sds((n, d), f32), sds((PIECES, 2 * rows * (ff // d) + 2 * EXTRA, d), bf16))
-    specs = [full(g.shape), pl.BlockSpec(memory_space=pl.ANY)] + [full(x.shape) for x in (vec, c, b, z, s)]
-    scratch = [pltpu.VMEM((n, ff), bf16), pltpu.VMEM((n, d), bf16), pltpu.VMEM((d, 128), f32)]
-    scratch += [pltpu.VMEM((PIECES, 2 * ff // PIECES, d), bf16), pltpu.SemaphoreType.DMA]
+    blocks = ff // d
+    outs = (sds((n, d), f32),)
+    specs = [Late(3), Late(1, base, 2 * rows * blocks), full(vec.shape), Late(0), Late(5), Late(4), Late(2)]
+    scratch = [pltpu.VMEM((n, d), bf16), pltpu.VMEM((d, 128), f32)]
+    grads = (2 * rows * blocks + 2 * EXTRA, d, 2 * blocks + 1)
     return call(
-        functools.partial(ff_backward_kernel, base), "ff_backward", (g, wide, vec, c, b, z, s),
-        specs, outs, 8 * n * d * ff, 40 << 20, scratch, carry, ident,
+        ff_backward_kernel, "ff_backward", (g, wide, vec, c, b, z, s), specs, outs, 8 * n * d * ff, 40 << 20, scratch,
+        grads, ident, carry,
     )
 
 
 def attn_backward_kernel(
-    base, red, h_ref, dg_ref, w_any, vec_ref, at_ref, qe_ref, ke_ref, ve_ref, ot_ref, ol_ref,
-    c_ref, grad_ref, doe_ref, dq_ref, dk_ref, dv_ref, cols_ref, w_ref, w_sem,
+    tools, h_ref, dg_ref, w_ref, vec_ref, at_ref, qe_ref, ke_ref, ve_ref, ot_ref, ol_ref,
+    c_ref, grad_ref, doe_ref, dq_ref, dk_ref, dv_ref, cols_ref,
 ):
     n, width = h_ref.shape
     hd = width // HEADS
     rows = width // PIECES
     scale = math.log2(math.e) / math.sqrt(hd)
     factor = 1.0 / math.sqrt(hd)
-    fetch = window(w_any, w_ref, w_sem, base)
-    fetch.start()
-    if red is not None:
-        red.start()
+    red, pair, tail = tools.red, tools.pair, tools.tail
+
+    def region(j):
+        return (EVERY, EVERY, EVERY, pl.ds(j * rows, rows if j < 4 else 2 * EXTRA))
+
+    def put(j, value):
+        grad_ref[:, :, :, :, j * rows : (j + 1) * rows, :] = value.reshape(2, 2, 2, 2, rows, width).astype(bf16)
+        if pair is not None:
+            pair.send(j, region(j))
+
+    tools.wait(1, 8)
     co = dg_ref[...].astype(bf16)
-    grad_ref[:, 3 * rows : 4 * rows, :] = mm(joined(ot_ref), co).reshape(PIECES, rows, width).astype(bf16)
-    fetch.wait()
+    put(3, mm(joined(ot_ref), co))
+    tools.wait(2)
     dot = mm_nt(weight(w_ref, 3, rows), co).astype(bf16)
     doe_ref[:, 0:hd, :] = dot.reshape(HEADS, hd, n)
     row = lax.broadcasted_iota(jnp.int32, (EXTRA, n), 0)
+    tools.wait(5, 6, 7, 9)
     part = n // BACKWARD_PARTS
 
     def head(i):
@@ -754,22 +883,28 @@
         dv_ref[i] = dv.astype(bf16)
         dk_ref[i] = (dk * factor).astype(bf16)
 
-    def pair(j, carry):
+    def some_heads(j, carry):
         advance_at(red, j, ATTN_PLAN)
         for k in range(UNROLL):
             head(UNROLL * j + k)
         return carry
 
-    lax.fori_loop(0, HEADS // UNROLL, pair, 0)
+    lax.fori_loop(0, HEADS // UNROLL, some_heads, 0)
+    tools.wait(4, 0)
     if red is not None:
         red.run(ATTN_MIDDLE)
+    if pair is not None:
+        pair.settle(3, region(3))
     at = at_ref[...]
-    dq = joined(dq_ref)
-    dk = joined(dk_ref)
-    dv = joined(dv_ref)
-    grad_ref[:, 0:rows, :] = mm_nt(at, dq).reshape(PIECES, rows, width).astype(bf16)
-    grad_ref[:, rows : 2 * rows, :] = mm_nt(at, dk).reshape(PIECES, rows, width).astype(bf16)
-    grad_ref[:, 2 * rows : 3 * rows, :] = mm_nt(at, dv).reshape(PIECES, rows, width).astype(bf16)
+    put(0, mm_nt(at, joined(dq_ref)))
+    put(1, mm_nt(at, joined(dk_ref)))
+    put(2, mm_nt(at, joined(dv_ref)))
+    if pair is not None:
+        for j in range(3):
+            pair.settle(j, region(j))
+    if tail is not None:
+        tail.begin(0)
+        tail.begin(1)
     tile = n // 4
 
     def norm_tile(t, sums):
@@ -783,6 +918,7 @@
         xh, r = normalised(h_ref[span, :].astype(f32))
         dg = dg_ref[span, :]
         c_ref[span, :] = dg + norm_back(da, xh, r, vec_ref[0:1, :])
+        tools.flush(0, (span, EVERY))
         sum_gain = sum_gain + jnp.sum(da * xh, axis=0, keepdims=True)
         sum_bias = sum_bias + jnp.sum(da, axis=0, keepdims=True)
         sum_out = sum_out + jnp.sum(dg.astype(bf16).astype(f32), axis=0, keepdims=True)
@@ -792,29 +928,36 @@
     vecs = lax.fori_loop(0, 4, norm_tile, (zero, zero, zero))
     vt = jnp.concatenate([*vecs, jnp.zeros((128 - len(vecs), width), f32)], axis=0).T
     lane = lax.broadcasted_iota(jnp.int32, (width, 128), 1)
-    vt = jnp.where(lane == 3, jnp.sum(dq.astype(f32), axis=1, keepdims=True), vt)
-    vt = jnp.where(lane == 4, jnp.sum(dv.astype(f32), axis=1, keepdims=True), vt)
+    vt = jnp.where(lane == 3, jnp.sum(joined(dq_ref).astype(f32), axis=1, keepdims=True), vt)
+    vt = jnp.where(lane == 4, jnp.sum(joined(dv_ref).astype(f32), axis=1, keepdims=True), vt)
     cols_ref[...] = vt
     put_vectors(grad_ref, 4 * rows, cols_ref, rows)
+    if pair is not None:
+        pair.send(4, region(4))
+        pair.settle(4, region(4))
+    if tail is not None:
+        tail.begin(2)
     if red is not None:
         red.run(ATTN_END)
-
-
-def attn_backward(h, dg, square, vec, kept, carry=None, ident=None):
+    if tail is not None:
+        for step in range(1, Reduction.STEPS):
+            tail.run([(0, step)])
+
+
+def attn_backward(h, dg, square, vec, kept, ident=None, carry=None, tail=False):
     square, base = square
     n, d = h.shape
     hd = d // HEADS
     rows = d // PIECES
     at, qe, ke, ve, ot, ol = kept
-    outs = (sds((n, d), f32), sds((PIECES, 4 * rows + 2 * EXTRA, d), bf16))
-    specs = [full(h.shape), full(dg.shape), pl.BlockSpec(memory_space=pl.ANY)]
-    specs += [full(x.shape) for x in (vec, at, qe, ke, ve, ot, ol)]
+    outs = (sds((n, d), f32),)
+    specs = [Late(8), Late(0), Late(2, base, 4 * rows), full(vec.shape), Late(7), Late(3), Late(4), Late(5), Late(1), Late(6)]
     scratch = [pltpu.VMEM((HEADS, hd + EXTRA, n), bf16)] + [pltpu.VMEM((HEADS, hd, n), bf16)] * 3
-    scratch += [pltpu.VMEM((d, 128), f32), pltpu.VMEM((PIECES, 4 * rows, d), bf16), pltpu.SemaphoreType.DMA]
+    scratch += [pltpu.VMEM((d, 128), f32)]
     flops = 16 * n * d * d + 5 * HEADS * 2 * n * n * 256
     return call(
-        functools.partial(attn_backward_kernel, base), "attn_backward", (h, dg, square, vec, at, qe, ke, ve, ot, ol),
-        specs, outs, flops, 40 << 20, scratch, carry, ident,
+        attn_backward_kernel, "attn_backward", (h, dg, square, vec, at, qe, ke, ve, ot, ol), specs, outs, flops, 40 << 20,
+        scratch, (4 * rows + 2 * EXTRA, d, 5), ident, carry, tail,
     )
 
 
@@ -971,24 +1114,26 @@
         hidden = after
     l = layers - 1
     g, *saved = attn_forward(hidden, squares[l], vecs[l], segment)
-    block_out, grad, gw = ff_last(g, wides[l], vecs[l], cotangent, live, ff)
     if not even:
+        whole = lambda x: x.reshape((PIECES,) + x.shape[4:])
+        block_out, grad, gw = ff_last(g, wides[l], vecs[l], cotangent, live, ff)
         grad, gs = attn_backward(hidden, grad, squares[l], vecs[l], saved)
-        results = [restack(gs, gw, d, ff)]
+        results = [restack(whole(gs), whole(gw), d, ff)]
         for l in reversed(range(layers - 1)):
             hidden, g, saved, more = kept[l]
             grad, gw = ff_backward(g, wides[l], vecs[l], grad, *more)
             grad, gs = attn_backward(hidden, grad, squares[l], vecs[l], saved)
-            results.insert(0, restack(gs, gw, d, ff))
+            results.insert(0, restack(whole(gs), whole(gw), d, ff))
     else:
-        grad, gs, rw = attn_backward(hidden, grad, squares[l], vecs[l], saved, (gw, 2), 2 + 2 * l)
+        block_out, grad, gw = ff_last(g, wides[l], vecs[l], cotangent, live, ff, 1)
+        grad, gs, rw = attn_backward(hidden, grad, squares[l], vecs[l], saved, 2 + 2 * l, (gw, 2), l == 0)
         pairs = []
         for l in reversed(range(layers - 1)):
             hidden, g, saved, more = kept[l]
-            grad, gw, rs = ff_backward(g, wides[l], vecs[l], grad, *more, carry=(gs, 1), ident=3 + 2 * l)
+            grad, gw, rs = ff_backward(g, wides[l], vecs[l], grad, *more, ident=3 + 2 * l, carry=(gs, 1))
             pairs.insert(0, (rs, rw))
-            grad, gs, rw = attn_backward(hidden, grad, squares[l], vecs[l], saved, (gw, 2), 2 + 2 * l)
-        pairs.insert(0, (reduced(gs, 1, 1), rw))
+            grad, gs, rw = attn_backward(hidden, grad, squares[l], vecs[l], saved, 2 + 2 * l, (gw, 2), l == 0)
+        pairs.insert(0, (gs, rw))
         return (block_out, grad) + tuple(finish(pairs, d, ff))
     return (block_out, grad) + tuple(jnp.stack([r[x] for r in results]) for x in NAMES)
 

time: 529 us -> 513 us (0.970)
  waiting for transfers between devices: 38.9 us -> 29.6 us
  Pallas kernels: 459 us -> 450 us
    pallas_call x7 -> x6, Pallas kernels: 370 us -> 356 us  [call(): pl.pallas_call(body, name=name, in_specs=base_specs, out_specs=out_specs,...]
    all_gather x1, waiting for transfers between devices: 38.9 us -> 29.6 us  [gather(): return lax.all_gather(x, axis, axis=0, tiled=True)]
  transfers between devices with their start and end apart: 1 -> 1, of which waited for: 1 -> 1; matrix products, arithmetic and copies ran while one was open for 0% -> 0% of each run, Pallas kernels for 19% -> 21%
where the time goes in v2:
time: 513 us; the launch traced here: 505 us
  Pallas kernels  450 us (88%)
  waiting for transfers between devices  29.6 us (6%)
  between operations  15.1 us (3%)
  local copies, waits for them, and re-layouts  10.5 us (2%)
    pallas_call x6, Pallas kernels, call(): pl.pallas_call(body, name=name, in_specs=base_specs, out_specs=out_specs,...  356 us
    pallas_call x1, Pallas kernels, gathered(): pl.pallas_call(functools.partial(gather_kernel, ident), name='gather', in...  68.9 us
    all_gather x1, waiting for transfers between devices, gather(): return lax.all_gather(x, axis, axis=0, tiled=True)  29.6 us
    pallas_call x1, Pallas kernels, ff_forward(): pl.pallas_call(functools.partial(ff_forward_kernel, base), name='ff_forwa...  21.5 us
  transfers between devices with their start and end apart: 1, of which 1 were waited for; matrix products, arithmetic and copies ran while one was open for 0% of the time, Pallas kernels for 21%

profile of v2, /device:TPU:0, one launch (start us, length us, event | category | flops | bytes accessed | tf_op | source)
XLA Modules:
  0.0 505.3 jit_solution(18181397329764178355)
XLA Ops:
  7.2 0.0 copy-start.4
  7.2 0.0 copy-start.6
  7.2 0.0 copy-start.5
  7.2 0.0 copy-start.8
  7.2 0.0 copy-start.7
  7.2 0.0 all-gather.2.cloned.1.call-start
  7.3 1.2 slice_bitcast_fusion
  8.5 0.0 copy-done.4
  8.6 0.0 copy-done.6
  8.6 0.0 copy-done.5
  8.6 0.0 copy-done.8
  8.6 0.0 copy-start.9
  8.6 0.0 copy-start.10
  8.6 0.0 copy-start.11
  8.7 0.0 copy-start.12
  8.7 0.0 copy-start.13
  8.7 0.0 copy-start.14
  8.7 0.0 copy-start.15
  8.7 0.0 copy-start.16
  8.7 0.0 copy-start.17
  8.7 0.0 copy-done.7
  8.9 0.0 copy-start.2
  8.9 1.1 copy-done.2
  10.0 0.0 all-gather.2.cloned.1.call-update
  10.0 0.0 copy-done.9
  10.1 0.0 copy-done.10
  10.1 0.0 copy-done.11
  10.1 0.0 copy-done.12
  10.1 0.0 copy-done.13
  10.1 0.0 copy-done.14
  10.1 0.0 copy-done.15
  10.2 0.0 copy-done.16
  10.2 0.0 copy-done.17
  10.2 0.1 concatenate.16
  10.3 0.1 concatenate.15
  10.5 0.2 concatenate.17.x_any
  10.7 68.9 %gather.1 = bf16[2,2,2,2,224,768]{5,4,3,2,1,0:T(8,128)(2,1)S(1)} custom-call(bf16[224,768]{1,0:T(8,128)(2,1)S(1)} %concatenate.17.x_any), custom_call_target="tpu_custom_call" | custom-call | bytes 104857600 | tf_op jit(solution)/shard_map/gather/pallas_call | solution.py:342
  79.6 0.0 copy-start
  79.7 2.3 copy-done
  82.0 0.1 reshape.52
  82.1 0.1 reshape.50
  82.3 0.1 reshape.51
  82.4 0.6 slice_bitcast_fusion.6
  83.1 35.9 %attn_forward.2 = (f32[1024,768]{1,0:T(8,128)}, bf16[768,1024]{1,0:T(8,128)(2,1)}, bf16[16,64,1024]{2,1,0:T(8,128)(2,1)}, bf16[16,64,1024]{2,1,0:T(8,128)(2,1)},...) custom-call(bf16[1024,768]{1,0:T(8,128)(2,1)} %refs_0_.3, ...), custom_call_target="tpu_custom_call" | custom-call | flops 22011707392 | bytes 31457280 | tf_op jit(solution)/shard_map/attn_forward/pallas_call | solution.py:540
  118.9 29.6 %all-gather.2.cloned.1.call-done = bf16[15360,768]{1,0:T(8,128)(2,1)} async-done(((bf16[960,768]{1,0:T(8,128)(2,1)}), bf16[15360,768]{1,0:T(8,128)(2,1)}) %all-gather.2.cloned.1.call-update) | async-done | bytes 23592976 | tf_op jit(solution)/shard_map/all_gather | solution.py:972
  148.5 21.5 %ff_forward.1 = (f32[1024,768]{1,0:T(8,128)}, bf16[1024,768]{1,0:T(8,128)(2,1)}, bf16[1024,3072]{1,0:T(8,128)(2,1)}, bf16[1024,3072]{1,0:T(8,128)(2,1)}) custom-call(f32[1024,768]{1,0:T(8,128)} %get-tuple-element.62.g_ref.refs_0_, bf16[16,960,768]{2,1,0:T(8,128)(2,1)} %bitcast.74, f32[12,768]{1,0:T(8,128)} %get-tuple-element.112.refs_2_.vec_ref.refs_3_), custom_call_target="tpu_custom_call" | custom-call | flops 9663676416 | bytes 31457280 | tf_op jit(solution)/shard_map/ff_forward/pallas_call | solution.py:625
  170.0 36.1 %attn_forward.3 = (f32[1024,768]{1,0:T(8,128)}, bf16[768,1024]{1,0:T(8,128)(2,1)}, bf16[16,64,1024]{2,1,0:T(8,128)(2,1)}, bf16[16,64,1024]{2,1,0:T(8,128)(2,1)},...) custom-call(f32[1024,768]{1,0:T(8,128)} %get-tuple-element.63.refs_0_, ...), custom_call_target="tpu_custom_call" | custom-call | flops 22011707392 | bytes 31457280 | tf_op jit(solution)/shard_map/attn_forward/pallas_call | solution.py:540
  206.2 50.8 %ff_last.1 = (bf16[1024,768]{1,0:T(8,128)(2,1)}, f32[1024,768]{1,0:T(8,128)}, bf16[2,2,2,416,768]{4,3,2,1,0:T(8,128)(2,1)}) custom-call(f32[1024,768]{1,0:T(8,128)} %get-tuple-element.64.refs_0_, bf16[16,960,768]{2,1,0:T(8,128)(2,1)} %bitcast.76, f32[12,768]{1,0:T(8,128)} %get-tuple-element.111.refs_2_.refs_3_, bf16[1024,768]{1,0:T(8,128)(2,1)} %refs_3_.5, ...), custom_call_target="tpu_custom_call" | custom-call | flops 28991029248 | bytes 31457280 | tf_op jit(solution)/shard_map/ff_last/pallas_call | solution.py:540
  257.0 71.1 %attn_backward.2 = (f32[1024,768]{1,0:T(8,128)}, bf16[2,2,2,224,768]{4,3,2,1,0:T(8,128)(2,1)}, bf16[416,768]{1,0:T(8,128)(2,1)}) custom-call(f32[1024,768]{1,0:T(8,128)} %get-tuple-element.63.refs_0_, f32[1024,768]{1,0:T(8,128)} %get-tuple-element.66.refs_1_, bf16[16,960,768]{2,1,0:T(8,128)(2,1)} %bitcast.77, f32[12,768]{1,0:T(8,128)} %get-tuple-element.111.refs_2_.refs_3_, ...), custom_call_target="tpu_custom_call" | custom-call | flops 52613349376 | bytes 41943040 | tf_op jit(solution)/shard_map/attn_backward/pallas_call | solution.py:540
  328.1 57.2 %ff_backward.1 = (f32[1024,768]{1,0:T(8,128)}, bf16[2,2,2,416,768]{4,3,2,1,0:T(8,128)(2,1)}, bf16[224,768]{1,0:T(8,128)(2,1)}) custom-call(f32[1024,768]{1,0:T(8,128)} %get-tuple-element.62.g_ref.refs_0_, bf16[16,960,768]{2,1,0:T(8,128)(2,1)} %bitcast.78, f32[12,768]{1,0:T(8,128)} %get-tuple-element.112.refs_2_.vec_ref.refs_3_, ...), custom_call_target="tpu_custom_call" | custom-call | flops 19327352832 | bytes 41943040 | tf_op jit(solution)/shard_map/ff_backward/pallas_call | solution.py:540
  385.3 105.0 %attn_backward.3 = (f32[1024,768]{1,0:T(8,128)}, bf16[224,768]{1,0:T(8,128)(2,1)}, bf16[416,768]{1,0:T(8,128)(2,1)}) custom-call(bf16[1024,768]{1,0:T(8,128)(2,1)} %refs_0_.3, f32[1024,768]{1,0:T(8,128)} %get-tuple-element.79.refs_1_, bf16[16,224,768]{2,1,0:T(8,128)(2,1)} %bitcast.72, f32[12,768]{1,0:T(8,128)} %get-tuple-element.112.refs_2_.vec_ref.refs_3_, ...), custom_call_target="tpu_custom_call" | custom-call | flops 52613349376 | bytes 41943040 | tf_op jit(solution)/shard_map/attn_backward/pallas_call | solution.py:540
  490.2 0.0 copy-start.3
  490.3 3.6 finish.1
  493.8 0.0 copy-done.3
  493.8 0.0 copy-start.1
  493.8 1.1 copy.55
  495.0 1.3 copy-done.1
  496.3 1.7 copy.56
  (31 shorter events, 0.3 us)
Async XLA Ops:
  7.2 1.3 copy-start.4
  7.2 1.4 copy-start.6
  7.2 1.4 copy-start.5
  7.2 1.4 copy-start.8
  7.2 1.5 copy-start.7
  7.2 141.3 %all-gather.2.cloned.1.call-start = ((), (), s32[]{:S(2)}) async-start(), calls=%async_computation | async-start | bytes 25067520 | tf_op jit(solution)/shard_map/all_gather | solution.py:972
  8.6 1.4 copy-start.9
  8.6 1.4 copy-start.10
  8.6 1.4 copy-start.11
  8.7 1.4 copy-start.12
  8.7 1.4 copy-start.13
  8.7 1.4 copy-start.14
  8.7 1.4 copy-start.15
  8.7 1.5 copy-start.16
  8.7 1.5 copy-start.17
  8.9 1.1 copy-start.2
  79.6 2.4 copy-start
  490.2 3.6 copy-start.3
  493.8 2.5 copy-start.1
Sparse Core Ops, SparseCore 0:
  10.1 138.3 all-gather.1

commit v3 on v2

--- a/solution.py
+++ b/solution.py
@@ -22,9 +22,9 @@
 ATTN_MIDDLE = [(1, 3), (0, 4)]
 ATTN_TILES = {0: [(0, 5)], 1: [(1, 4)]}
 ATTN_END = [(1, 5)]
-FF_TILES = {3: [(0, 1)]}
-FF_BLOCKS = {1: [(0, 2)], 2: [(0, 3)], 3: [(0, 4)]}
-FF_END = [(0, 5)]
+FF_TILES = {7: [(0, 1)], 13: [(1, 1), (0, 2)]}
+FF_BLOCKS = {1: [(0, 3), (1, 2)], 4: [(0, 4), (1, 3)], 7: [(0, 5), (1, 4)]}
+FF_END = [(1, 5)]
 VMEM_BYTES = 60 * 1024 * 1024
 
 
@@ -297,14 +297,12 @@
             ).wait()
 
 
-def gather_kernel(ident, x_any, out_any, send_sem, recv_sem, own_sem):
+def gather_kernel(x_ref, out_ref, send_sem, recv_sem):
     red = Links()
     at = red.at
-    rows = x_any.shape[0]
+    rows = x_ref.shape[0]
     mine = (at["h"], at["l"], at["y"], at["c"])
-    own = pltpu.make_async_copy(x_any, out_any.at[(*mine, slice(None), slice(None))], own_sem)
-    own.start()
-    own.wait()
+    out_ref[(*mine, slice(None), slice(None))] = x_ref[...]
     red.meet()
 
     def copy(path, step):
@@ -319,8 +317,8 @@
         where = tuple(slice(None) if a in free else at[a] for a in "hlyc") + (span, slice(None))
         sem = 5 * paths.index(path) + step
         return pltpu.make_async_remote_copy(
-            src_ref=out_any.at[where],
-            dst_ref=out_any.at[where],
+            src_ref=out_ref.at[where],
+            dst_ref=out_ref.at[where],
             send_sem=send_sem.at[sem],
             recv_sem=recv_sem.at[sem],
             device_id=red.peer[order[step]],
@@ -340,14 +338,14 @@
 def gathered(x, ident):
     rows, width = x.shape
     out = pl.pallas_call(
-        functools.partial(gather_kernel, ident),
+        gather_kernel,
         name="gather",
-        in_specs=[pl.BlockSpec(memory_space=pl.ANY)],
-        out_specs=pl.BlockSpec(memory_space=pl.ANY),
+        in_specs=[full(x.shape)],
+        out_specs=full((2, 2, 2, 2, rows, width)),
         out_shape=sds((2, 2, 2, 2, rows, width), bf16),
-        scratch_shapes=[pltpu.SemaphoreType.DMA((15,)), pltpu.SemaphoreType.DMA((15,)), pltpu.SemaphoreType.DMA],
+        scratch_shapes=[pltpu.SemaphoreType.DMA((15,)), pltpu.SemaphoreType.DMA((15,))],
         compiler_params=pltpu.CompilerParams(
-            vmem_limit_bytes=8 * 1024 * 1024, collective_id=ident, has_side_effects=True
+            vmem_limit_bytes=24 * 1024 * 1024, collective_id=ident, has_side_effects=True
         ),
         cost_estimate=pl.CostEstimate(flops=0, bytes_accessed=100 << 20, transcendentals=0),
     )(x)
@@ -355,7 +353,7 @@
 
 
 def attn_forward_kernel(
-    tools, h_ref, w_ref, vec_ref, seg_ref,
+    tools, h_ref, wa_ref, wb_ref, vec_ref, seg_ref,
     g_ref, at_ref, qe_ref, ke_ref, ve_ref, ot_ref, ol_ref,
 ):
     length, width = h_ref.shape
@@ -368,12 +366,12 @@
     a = (xh * vec_ref[0:1, :] + vec_ref[1:2, :]).astype(bf16)
     at_ref[...] = a.T
     tools.flush(1, ...)
-    tools.wait(1)
-    q = (mm(a, weight(w_ref, 0, rows)) + vec_ref[2:3, :]).astype(bf16)
+    tools.wait(1, 2)
+    q = (mm(a, weight(wa_ref, 0, rows)) + vec_ref[2:3, :]).astype(bf16)
     qe_ref[:, 0:hd, :] = q.T.reshape(HEADS, hd, length)
-    k = mm(a, weight(w_ref, 1, rows)).astype(bf16)
+    k = mm(a, weight(wa_ref, 1, rows)).astype(bf16)
     ke_ref[:, 0:hd, :] = k.T.reshape(HEADS, hd, length)
-    v = (mm(a, weight(w_ref, 2, rows)) + vec_ref[3:4, :]).astype(bf16)
+    v = (mm(a, weight(wb_ref, 0, rows)) + vec_ref[3:4, :]).astype(bf16)
     ve_ref[:, 0:hd, :] = v.T.reshape(HEADS, hd, length)
     mask_q, mask_k = mask_rows(seg_ref, length, seg_ref.shape[1])
     qe_ref[:, hd:, :] = jnp.broadcast_to(mask_q.astype(bf16)[None], (HEADS, EXTRA, length))
@@ -411,7 +409,7 @@
         return carry
 
     lax.fori_loop(0, HEADS // UNROLL, some_heads, 0)
-    g_ref[...] = x + (mm_tn(joined(ot_ref), weight(w_ref, 3, rows)) + vec_ref[4:5, :])
+    g_ref[...] = x + (mm_tn(joined(ot_ref), weight(wb_ref, 1, rows)) + vec_ref[4:5, :])
     tools.flush(0, ...)
 
 
@@ -569,7 +567,7 @@
 
 
 def attn_forward(h, square, vec, seg):
-    square, base = square
+    (first, base_a), (second, base_b) = square
     n, d = h.shape
     hd = d // HEADS
     rows = d // PIECES
@@ -583,9 +581,9 @@
         sds((HEADS, hd, n), bf16),
         sds((HEADS, hd, n), bf16),
     )
-    specs = [Late(0), Late(1, base, 4 * rows), full(vec.shape), pl.BlockSpec(memory_space=SMEM)]
+    specs = [Late(0), Late(1, base_a, 2 * rows), Late(2, base_b, 2 * rows), full(vec.shape), pl.BlockSpec(memory_space=SMEM)]
     flops = 8 * n * d * d + 2 * HEADS * 2 * n * n * 256
-    return call(attn_forward_kernel, "attn_forward", (h, square, vec, seg), specs, outs, flops, 30 << 20, ())
+    return call(attn_forward_kernel, "attn_forward", (h, first, second, vec, seg), specs, outs, flops, 30 << 20, ())
 
 
 def ff_forward_kernel(base, g_ref, w_any, vec_ref, h_ref, b_ref, z_ref, s_ref, w_ref, w_sem):
@@ -671,13 +669,14 @@
                 pair.settle(k, where)
 
     def block(j, carry):
-        advance_at(tools.red, j, FF_BLOCKS)
+        advance_at(tools.red, 2 * j, FF_BLOCKS)
         cols = pl.ds(pl.multiple_of(j * width, 128), width)
         (kd, where_d), (ku, where_u) = regions(j)
         dwd = mm_tn(z_ref[:, cols], cm_ref[...]).reshape(2, 2, rows * blocks, width)
         grad_ref[lax.div(j, 2), lax.rem(j, 2), :, :, lower, :] = dwd.astype(bf16)
         if pair is not None:
             pair.send(kd, where_d)
+        advance_at(tools.red, 2 * j + 1, FF_BLOCKS)
         dwu = mm_tn(b_ref[...], du_ref[:, cols])
         grad_ref[:, :, :, :, where_u[3], :] = dwu.reshape(2, 2, 2, 2, rows, width).astype(bf16)
         if pair is not None:
@@ -787,7 +786,6 @@
     tools.wait(3, 1, 6, 0)
 
     def step(t, sums):
-        advance_at(tools.red, t, FF_TILES)
         sum_gain, sum_bias, sum_down = sums
         span = pl.ds(pl.multiple_of(t * tile, 16), tile)
         xh, r = normalised(g_ref[span, :])
@@ -797,6 +795,7 @@
         db = jnp.zeros((tile, width), f32)
         for j in range(blocks):
             cols = slice(j * width, (j + 1) * width)
+            advance_at(tools.red, t * blocks + j, FF_TILES)
             w = weight(w_ref, j, rows)
             wd = down(w_ref, j, rows, blocks)
             du = (s_ref[span, cols].astype(f32) * mm_nt(cm, wd)).astype(bf16)
@@ -834,7 +833,7 @@
 
 
 def attn_backward_kernel(
-    tools, h_ref, dg_ref, w_ref, vec_ref, at_ref, qe_ref, ke_ref, ve_ref, ot_ref, ol_ref,
+    tools, h_ref, dg_ref, wa_ref, wb_ref, vec_ref, at_ref, qe_ref, ke_ref, ve_ref, ot_ref, ol_ref,
     c_ref, grad_ref, doe_ref, dq_ref, dk_ref, dv_ref, cols_ref,
 ):
     n, width = h_ref.shape
@@ -852,14 +851,14 @@
         if pair is not None:
             pair.send(j, region(j))
 
-    tools.wait(1, 8)
+    tools.wait(1, 9)
     co = dg_ref[...].astype(bf16)
     put(3, mm(joined(ot_ref), co))
-    tools.wait(2)
-    dot = mm_nt(weight(w_ref, 3, rows), co).astype(bf16)
+    tools.wait(3)
+    dot = mm_nt(weight(wb_ref, 1, rows), co).astype(bf16)
     doe_ref[:, 0:hd, :] = dot.reshape(HEADS, hd, n)
     row = lax.broadcasted_iota(jnp.int32, (EXTRA, n), 0)
-    tools.wait(5, 6, 7, 9)
+    tools.wait(6, 7, 8, 10)
     part = n // BACKWARD_PARTS
 
     def head(i):
@@ -890,7 +889,7 @@
         return carry
 
     lax.fori_loop(0, HEADS // UNROLL, some_heads, 0)
-    tools.wait(4, 0)
+    tools.wait(5, 0, 2)
     if red is not None:
         red.run(ATTN_MIDDLE)
     if pair is not None:
@@ -911,9 +910,9 @@
         advance_at(red, t, ATTN_TILES)
         sum_gain, sum_bias, sum_out = sums
         span = pl.ds(pl.multiple_of(t * tile, 128), tile)
-        dat = mm(weight(w_ref, 0, rows), dq_ref[:, :, span].reshape(width, tile))
-        dat = dat + mm(weight(w_ref, 1, rows), dk_ref[:, :, span].reshape(width, tile))
-        dat = dat + mm(weight(w_ref, 2, rows), dv_ref[:, :, span].reshape(width, tile))
+        dat = mm(weight(wa_ref, 0, rows), dq_ref[:, :, span].reshape(width, tile))
+        dat = dat + mm(weight(wa_ref, 1, rows), dk_ref[:, :, span].reshape(width, tile))
+        dat = dat + mm(weight(wb_ref, 0, rows), dv_ref[:, :, span].reshape(width, tile))
         da = dat.T
         xh, r = normalised(h_ref[span, :].astype(f32))
         dg = dg_ref[span, :]
@@ -945,18 +944,19 @@
 
 
 def attn_backward(h, dg, square, vec, kept, ident=None, carry=None, tail=False):
-    square, base = square
+    (first, base_a), (second, base_b) = square
     n, d = h.shape
     hd = d // HEADS
     rows = d // PIECES
     at, qe, ke, ve, ot, ol = kept
     outs = (sds((n, d), f32),)
-    specs = [Late(8), Late(0), Late(2, base, 4 * rows), full(vec.shape), Late(7), Late(3), Late(4), Late(5), Late(1), Late(6)]
+    specs = [Late(8), Late(0), Late(9, base_a, 2 * rows), Late(2, base_b, 2 * rows), full(vec.shape)]
+    specs += [Late(7), Late(3), Late(4), Late(5), Late(1), Late(6)]
     scratch = [pltpu.VMEM((HEADS, hd + EXTRA, n), bf16)] + [pltpu.VMEM((HEADS, hd, n), bf16)] * 3
     scratch += [pltpu.VMEM((d, 128), f32)]
     flops = 16 * n * d * d + 5 * HEADS * 2 * n * n * 256
     return call(
-        attn_backward_kernel, "attn_backward", (h, dg, square, vec, at, qe, ke, ve, ot, ol), specs, outs, flops, 40 << 20,
+        attn_backward_kernel, "attn_backward", (h, dg, first, second, vec, at, qe, ke, ve, ot, ol), specs, outs, flops, 40 << 20,
         scratch, (4 * rows + 2 * EXTRA, d, 5), ident, carry, tail,
     )
 
@@ -976,36 +976,76 @@
     return [up[:, j * d : (j + 1) * d] for j in range(up.shape[1] // d)]
 
 
+def pack_kernel(first_rows, rest_rows, *refs):
+    names = [n for n in NAMES if n.endswith("weight")]
+    weights = dict(zip(names, refs))
+    vectors = refs[len(names) : len(names) + len(ROW_VECTORS) + 1]
+    first, rest, wide_ref, rows_ref, sems = refs[len(names) + len(ROW_VECTORS) + 1 :]
+    per, d = vectors[0].shape[1], first.shape[1]
+    moves = []
+    for target, pieces in ((rest, rest_rows), (first, first_rows)):
+        at = 0
+        for name, l, column in pieces:
+            src = weights[name].at[l]
+            if column is not None:
+                src = src.at[:, column * d : (column + 1) * d]
+            count = src.shape[0]
+            copy = pltpu.make_async_copy(src, target.at[at : at + count, :], sems.at[len(moves)])
+            copy.start()
+            moves.append(copy)
+            at += count
+    wide_ref[...] = jnp.zeros_like(wide_ref)
+    for l in range(vectors[0].shape[0]):
+        for k, ref in enumerate(vectors):
+            wide_ref[l : l + 1, k * per : k * per + ref.shape[1]] = ref[l : l + 1, :].astype(f32)
+    rows_ref[...] = wide_ref[...].astype(bf16)
+    copy = pltpu.make_async_copy(rows_ref, first.at[at : at + 2 * EXTRA, :], sems.at[len(moves)])
+    copy.start()
+    for move in moves + [copy]:
+        move.wait()
+
+
 def fetch_even(w, layers, shards):
     d = w["q_weight"].shape[2]
     per = w["q_weight"].shape[1]
     ff = w["up_weight"].shape[2]
-    packed = []
-    for l in range(layers):
-        row = jnp.concatenate([w[x][l] for x in ROW_VECTORS] + [w["up_bias"][l]])
-        packed.append(jnp.pad(row, (0, d - row.shape[0]))[None])
-    rows = jnp.concatenate(packed + [jnp.zeros((2 * EXTRA - layers, d), bf16)], axis=0)
-    square = lambda l: [w[x][l] for x in ("q_weight", "k_weight", "v_weight", "o_weight")]
-    wide = lambda l: column_blocks(w["up_weight"][l], d) + [w["down_weight"][l]]
-    first = jnp.concatenate(square(0) + [rows], axis=0)
+    blocks = ff // d
+    square = lambda l, names: [(n + "_weight", l, None) for n in names]
+    wide = lambda l: [("up_weight", l, j) for j in range(blocks)] + [("down_weight", l, None)]
+    first, rest = square(0, "qkvo"), wide(0)
+    for l in range(1, layers):
+        first = first + square(l, "qk")
+        rest = rest + square(l, "vo") + wide(l)
+    tall = 4 * per + 2 * per * (layers - 1)
+    long = 2 * per * blocks * layers + 2 * per * (layers - 1)
+    names = [n for n in NAMES if n.endswith("weight")]
+    vectors = [w[x] for x in (*ROW_VECTORS, "up_bias")]
+    first, rest = pl.pallas_call(
+        functools.partial(pack_kernel, first, rest),
+        name="pack",
+        in_specs=[full(w[n].shape) for n in names] + [full(x.shape) for x in vectors],
+        out_specs=[ANY, ANY],
+        out_shape=[sds((tall + 2 * EXTRA, d), bf16), sds((long, d), bf16)],
+        scratch_shapes=[
+            pltpu.VMEM((2 * EXTRA, d), f32), pltpu.VMEM((2 * EXTRA, d), bf16),
+            pltpu.SemaphoreType.DMA((len(first) + len(rest) + 1,)),
+        ],
+    )(*(w[n] for n in names), *vectors)
+    rest = gather(rest).reshape(shards, -1, d)
     first = gathered(first, 20)
-    rest = wide(0)
-    for l in range(1, layers):
-        rest = rest + square(l) + wide(l)
-    rest = gather(jnp.concatenate(rest, axis=0)).reshape(shards, -1, d)
-    flat = first[:, 4 * per : 4 * per + layers, :]
+    flat = first[:, tall : tall + layers, :]
     count = len(ROW_VECTORS)
     vecs = flat[:, :, : count * per].reshape(shards, layers, count, per).transpose(1, 2, 0, 3)
     vecs = vecs.reshape(layers, count, d)
     ups = flat[:, :, count * per : count * per + ff // shards].transpose(1, 0, 2).reshape(layers, ff // d, d)
     vec = jnp.concatenate([vecs, ups], axis=1).astype(f32)
     wides = [(rest, 0)]
-    squares = [(first, 0)]
-    base = 2 * per * (ff // d)
+    squares = [((first, 0), (first, 2 * per))]
+    base = 2 * per * blocks
     for l in range(1, layers):
-        squares.append((rest, base))
-        wides.append((rest, base + 4 * per))
-        base += 4 * per + 2 * per * (ff // d)
+        squares.append(((first, 2 * per * (l + 1)), (rest, base)))
+        wides.append((rest, base + 2 * per))
+        base += 2 * per + 2 * per * blocks
     return squares, wides, [vec[l] for l in range(layers)]
 
 
@@ -1015,7 +1055,8 @@
     for l in range(layers):
         whole = {x: gather(w[x][l]) for x in NAMES}
         cut = lambda x: x.reshape(PIECES, x.shape[0] // PIECES, d)
-        squares.append((jnp.concatenate([cut(whole[x]) for x in ("q_weight", "k_weight", "v_weight", "o_weight")], axis=1), 0))
+        four = jnp.concatenate([cut(whole[x]) for x in ("q_weight", "k_weight", "v_weight", "o_weight")], axis=1)
+        squares.append(((four, 0), (four, 2 * (d // PIECES))))
         blocks = [cut(x) for x in column_blocks(whole["up_weight"], d)] + [cut(whole["down_weight"])]
         wides.append((jnp.concatenate(blocks, axis=1), 0))
         rows = [whole[x][None] for x in ROW_VECTORS] + [whole["up_bias"].reshape(-1, d)]
@@ -1053,7 +1094,11 @@
 
 
 def finish_kernel(layers, blocks, *refs):
-    ins, outs, cols_ref = refs[: 2 * layers], dict(zip(NAMES, refs[2 * layers : -1])), refs[-1]
+    given, made, (cols_ref, sems) = refs[: 2 * layers + 2], refs[2 * layers + 2 : -2], refs[-2:]
+    ins, outs = given[2:], dict(zip(NAMES, made[2:]))
+    moves = [pltpu.make_async_copy(given[k], made[k], sems.at[k]) for k in range(2)]
+    for move in moves:
+        move.start()
     per = outs["q_weight"].shape[1]
     width = outs["q_weight"].shape[2]
     lanes = width // 128
@@ -1078,9 +1123,11 @@
                 for c in range(blocks):
                     row = turned[len(names) + c : len(names) + c + 1, :]
                     outs["up_bias"][l : l + 1, c * per : (c + 1) * per] = row
-
-
-def finish(pairs, d, ff):
+    for move in moves:
+        move.wait()
+
+
+def finish(block_out, grad, pairs, d, ff):
     layers, per = len(pairs), d // PIECES
     shapes = {x: (layers, per) for x in NAMES}
     for x in ("q_weight", "k_weight", "v_weight", "o_weight"):
@@ -1090,12 +1137,12 @@
     return pl.pallas_call(
         functools.partial(finish_kernel, layers, ff // d),
         name="finish",
-        in_specs=[full(x.shape) for x in args],
-        out_specs=[full(shapes[x]) for x in NAMES],
-        out_shape=[sds(shapes[x], f32) for x in NAMES],
-        scratch_shapes=[pltpu.VMEM((per, 128), f32)],
+        in_specs=[full(x.shape) for x in (block_out, grad, *args)],
+        out_specs=[ANY, ANY] + [full(shapes[x]) for x in NAMES],
+        out_shape=[sds(x.shape, x.dtype) for x in (block_out, grad)] + [sds(shapes[x], f32) for x in NAMES],
+        scratch_shapes=[pltpu.VMEM((per, 128), f32), pltpu.SemaphoreType.DMA((2,))],
         compiler_params=pltpu.CompilerParams(vmem_limit_bytes=VMEM_BYTES),
-    )(*args)
+    )(block_out, grad, *args)
 
 
 def on_device(tokens, segment, live, cotangent, *weights):
@@ -1130,11 +1177,11 @@
         pairs = []
         for l in reversed(range(layers - 1)):
             hidden, g, saved, more = kept[l]
-            grad, gw, rs = ff_backward(g, wides[l], vecs[l], grad, *more, ident=3 + 2 * l, carry=(gs, 1))
+            grad, gw, rs = ff_backward(g, wides[l], vecs[l], grad, *more, ident=3 + 2 * l, carry=(gs, 2))
             pairs.insert(0, (rs, rw))
             grad, gs, rw = attn_backward(hidden, grad, squares[l], vecs[l], saved, 2 + 2 * l, (gw, 2), l == 0)
         pairs.insert(0, (gs, rw))
-        return (block_out, grad) + tuple(finish(pairs, d, ff))
+        return tuple(finish(block_out, grad, pairs, d, ff))
     return (block_out, grad) + tuple(jnp.stack([r[x] for r in results]) for x in NAMES)
 
 

time: 513 us -> 500 us (0.975)
  waiting for transfers between devices: 29.6 us -> 0.94 us
  Pallas kernels: 450 us -> 475 us
  local copies, waits for them, and re-layouts: 10.5 us -> 5.12 us
    all_gather x1, waiting for transfers between devices: 29.6 us -> 0.92 us  [gather(): return lax.all_gather(x, axis, axis=0, tiled=True)]
    pallas_call x1 -> x2, Pallas kernels: 68.9 us -> 94.2 us  [the longest x1 91.2 us: gathered(): pl.pallas_call(gather_kernel, name='gather', in_specs=[full(x.shape)], ou...]
  transfers between devices with their start and end apart: 1 -> 1, of which waited for: 1 -> 1; matrix products, arithmetic and copies ran while one was open for 0% -> 0% of each run, Pallas kernels for 21% -> 26%
where the time goes in v3:
time: 500 us; the launch traced here: 496 us
  Pallas kernels  475 us (95%)
  between operations  14.4 us (3%)
  local copies, waits for them, and re-layouts  5.12 us (1%)
    pallas_call x6, Pallas kernels, call(): pl.pallas_call(body, name=name, in_specs=base_specs, out_specs=out_specs,...  353 us
    pallas_call x1, Pallas kernels, gathered(): pl.pallas_call(gather_kernel, name='gather', in_specs=[full(x.shape)], ou...  91.2 us
    pallas_call x1, Pallas kernels, ff_forward(): pl.pallas_call(functools.partial(ff_forward_kernel, base), name='ff_forwa...  21.3 us
  transfers between devices with their start and end apart: 1, of which 1 were waited for; matrix products, arithmetic and copies ran while one was open for 0% of the time, Pallas kernels for 26%

profile of v3, /device:TPU:0, one launch (start us, length us, event | category | flops | bytes accessed | tf_op | source)
XLA Modules:
  0.0 495.6 jit_solution(3953506680591717478)
XLA Ops:
  7.2 0.0 all-gather.2.cloned.1.call-start
  7.2 2.9 pack.1
  10.2 0.0 all-gather.2.cloned.1.call-update
  10.2 0.0 copy-start.1
  10.2 1.0 copy-done.1
  11.2 91.2 %gather.1 = bf16[2,2,2,2,320,768]{5,4,3,2,1,0:T(8,128)(2,1)S(1)} custom-call(bf16[320,768]{1,0:T(8,128)(2,1)S(1)} %copy-done.1), custom_call_target="tpu_custom_call" | custom-call | bytes 104857600 | tf_op jit(solution)/shard_map/gather/pallas_call | solution.py:340
  102.5 0.0 copy-start
  102.5 3.1 copy-done
  105.6 0.1 reshape.52
  105.7 0.1 reshape.50
  105.8 0.1 reshape.51
  106.0 0.6 slice_bitcast_fusion
  106.6 36.4 %attn_forward.2 = (f32[1024,768]{1,0:T(8,128)}, bf16[768,1024]{1,0:T(8,128)(2,1)}, bf16[16,64,1024]{2,1,0:T(8,128)(2,1)}, bf16[16,64,1024]{2,1,0:T(8,128)(2,1)},...) custom-call(bf16[1024,768]{1,0:T(8,128)(2,1)} %refs_0_.5, ...), custom_call_target="tpu_custom_call" | custom-call | flops 22011707392 | bytes 31457280 | tf_op jit(solution)/shard_map/attn_forward/pallas_call | solution.py:538
  143.0 0.9 all-gather.2.cloned.1.call-done
  143.9 21.3 %ff_forward.1 = (f32[1024,768]{1,0:T(8,128)}, bf16[1024,768]{1,0:T(8,128)(2,1)}, bf16[1024,3072]{1,0:T(8,128)(2,1)}, bf16[1024,3072]{1,0:T(8,128)(2,1)}) custom-call(f32[1024,768]{1,0:T(8,128)} %get-tuple-element.50.g_ref.refs_0_, bf16[16,864,768]{2,1,0:T(8,128)(2,1)} %bitcast.22, f32[12,768]{1,0:T(8,128)} %get-tuple-element.82.refs_3_.vec_ref.refs_2_.refs_4_), custom_call_target="tpu_custom_call" | custom-call | flops 9663676416 | bytes 31457280 | tf_op jit(solution)/shard_map/ff_forward/pallas_call | solution.py:623
  165.2 36.4 %attn_forward.3 = (f32[1024,768]{1,0:T(8,128)}, bf16[768,1024]{1,0:T(8,128)(2,1)}, bf16[16,64,1024]{2,1,0:T(8,128)(2,1)}, bf16[16,64,1024]{2,1,0:T(8,128)(2,1)},...) custom-call(f32[1024,768]{1,0:T(8,128)} %get-tuple-element.52.refs_0_, ...), custom_call_target="tpu_custom_call" | custom-call | flops 22011707392 | bytes 31457280 | tf_op jit(solution)/shard_map/attn_forward/pallas_call | solution.py:538
  201.6 50.3 %ff_last.1 = (bf16[1024,768]{1,0:T(8,128)(2,1)}, f32[1024,768]{1,0:T(8,128)}, bf16[2,2,2,416,768]{4,3,2,1,0:T(8,128)(2,1)}) custom-call(f32[1024,768]{1,0:T(8,128)} %get-tuple-element.53.refs_0_, bf16[16,864,768]{2,1,0:T(8,128)(2,1)} %bitcast.24, f32[12,768]{1,0:T(8,128)} %get-tuple-element.81.refs_3_.refs_2_.refs_4_, bf16[1024,768]{1,0:T(8,128)(2,1)} %refs_3_.3, ...), custom_call_target="tpu_custom_call" | custom-call | flops 28991029248 | bytes 31457280 | tf_op jit(solution)/shard_map/ff_last/pallas_call | solution.py:538
  251.9 71.6 %attn_backward.2 = (f32[1024,768]{1,0:T(8,128)}, bf16[2,2,2,224,768]{4,3,2,1,0:T(8,128)(2,1)}, bf16[416,768]{1,0:T(8,128)(2,1)}) custom-call(f32[1024,768]{1,0:T(8,128)} %get-tuple-element.52.refs_0_, f32[1024,768]{1,0:T(8,128)} %get-tuple-element.55.refs_1_, bf16[16,320,768]{2,1,0:T(8,128)(2,1)} %bitcast.18, bf16[16,864,768]{2,1,0:T(8,128)(2,1)} %bitcast.25, ...), custom_call_target="tpu_custom_call" | custom-call | flops 52613349376 | bytes 41943040 | tf_op jit(solution)/shard_map/attn_backward/pallas_call | solution.py:538
  323.6 53.1 %ff_backward.1 = (f32[1024,768]{1,0:T(8,128)}, bf16[2,2,2,416,768]{4,3,2,1,0:T(8,128)(2,1)}, bf16[224,768]{1,0:T(8,128)(2,1)}) custom-call(f32[1024,768]{1,0:T(8,128)} %get-tuple-element.50.g_ref.refs_0_, bf16[16,864,768]{2,1,0:T(8,128)(2,1)} %bitcast.26, f32[12,768]{1,0:T(8,128)} %get-tuple-element.82.refs_3_.vec_ref.refs_2_.refs_4_, ...), custom_call_target="tpu_custom_call" | custom-call | flops 19327352832 | bytes 41943040 | tf_op jit(solution)/shard_map/ff_backward/pallas_call | solution.py:538
  376.6 105.0 %attn_backward.3 = (f32[1024,768]{1,0:T(8,128)}, bf16[224,768]{1,0:T(8,128)(2,1)}, bf16[416,768]{1,0:T(8,128)(2,1)}) custom-call(bf16[1024,768]{1,0:T(8,128)(2,1)} %refs_0_.5, f32[1024,768]{1,0:T(8,128)} %get-tuple-element.68.refs_1_, bf16[16,320,768]{2,1,0:T(8,128)(2,1)} %bitcast.19, bf16[16,320,768]{2,1,0:T(8,128)(2,1)} %bitcast.20, ...), custom_call_target="tpu_custom_call" | custom-call | flops 52613349376 | bytes 41943040 | tf_op jit(solution)/shard_map/attn_backward/pallas_call | solution.py:538
  481.6 6.9 %finish.1 = (bf16[1024,768]{1,0:T(8,128)(2,1)}, f32[1024,768]{1,0:T(8,128)}, f32[2,48]{1,0:T(2,128)}, f32[2,48]{1,0:T(2,128)}, f32[2,48,768]{2,1,0:T(8,128)}, /*...) custom-call(bf16[1024,768]{1,0:T(8,128)(2,1)} %get-tuple-element.54., ...), custom_call_target="tpu_custom_call" | custom-call | tf_op jit(solution)/shard_map/finish/pallas_call | solution.py:1137
  (5 shorter events, 0.1 us)
Async XLA Ops:
  7.2 136.8 %all-gather.2.cloned.1.call-start = ((), (), s32[]{:S(2)}) async-start(), calls=%async_computation | async-start | bytes 22560768 | tf_op jit(solution)/shard_map/all_gather | solution.py:972
  10.2 1.0 copy-start.1
  102.5 3.1 copy-start
Sparse Core Ops, SparseCore 0:
  10.3 133.5 all-gather.1

commit v4 on v3

--- a/solution.py
+++ b/solution.py
@@ -18,6 +18,7 @@
 FORWARD_PARTS = 1
 BACKWARD_PARTS = 4
 UNROLL = 2
+FORWARD_UNROLL = 4
 ATTN_PLAN = {2: [(0, 1)], 4: [(1, 1)], 5: [(0, 2)], 6: [(1, 2)], 7: [(0, 3)]}
 ATTN_MIDDLE = [(1, 3), (0, 4)]
 ATTN_TILES = {0: [(0, 5)], 1: [(1, 4)]}
@@ -404,11 +405,11 @@
             tools.flush(k, i)
 
     def some_heads(j, carry):
-        for k in range(UNROLL):
-            head(UNROLL * j + k)
+        for k in range(FORWARD_UNROLL):
+            head(FORWARD_UNROLL * j + k)
         return carry
 
-    lax.fori_loop(0, HEADS // UNROLL, some_heads, 0)
+    lax.fori_loop(0, HEADS // FORWARD_UNROLL, some_heads, 0)
     g_ref[...] = x + (mm_tn(joined(ot_ref), weight(wb_ref, 1, rows)) + vec_ref[4:5, :])
     tools.flush(0, ...)
 
@@ -650,9 +651,10 @@
 
 
 EVERY = slice(None)
-
-
-def ff_tail(tools, z_ref, du_ref, b_ref, cm_ref, grad_ref, cols_ref, vecs, width, blocks):
+ATTN_VECTORS = 5
+
+
+def ff_tail(tools, z_ref, du_ref, b_ref, cm_ref, grad_ref, cols_ref, number, vecs, width, blocks):
     rows = width // PIECES
     quarter = PIECES // blocks
     n = b_ref.shape[0]
@@ -690,7 +692,9 @@
 
     lax.fori_loop(0, blocks, block, 0)
     ones = jnp.ones((n, 128), bf16)
-    vt = jnp.concatenate([*vecs, jnp.zeros((128 - len(vecs), width), f32)], axis=0).T
+    first = ATTN_VECTORS
+    blank = jnp.zeros((first, width), f32)
+    vt = jnp.concatenate([blank, *vecs, jnp.zeros((128 - first - len(vecs), width), f32)], axis=0).T
     vt = vt.reshape(PIECES, rows, 128)
     lane = lax.broadcasted_iota(jnp.int32, (quarter, rows, 128), 2)
     for j in range(blocks):
@@ -698,18 +702,15 @@
         part = part.reshape(quarter, blocks, rows, 128)
         piece = vt[quarter * j : quarter * (j + 1)]
         for c in range(blocks):
-            piece = jnp.where(lane == len(vecs) + c, part[:, c], piece)
+            piece = jnp.where(lane == first + len(vecs) + c, part[:, c], piece)
         cols_ref[quarter * rows * j : quarter * rows * (j + 1), :] = piece.reshape(quarter * rows, 128)
-    put_vectors(grad_ref, 2 * rows * blocks, cols_ref, rows)
+    tools.flush(number, ...)
     if pair is not None:
-        last = (EVERY, EVERY, EVERY, pl.ds(2 * rows * blocks, 2 * EXTRA))
-        pair.send(2 * blocks, last)
         settle(blocks - 1)
-        pair.settle(2 * blocks, last)
 
 
 def ff_last_kernel(
-    tools, g_ref, w_ref, vec_ref, cot_ref, live_ref, out_ref, dg_ref, grad_ref, z_ref, du_ref, b_ref, cm_ref, cols_ref,
+    tools, g_ref, w_ref, vec_ref, cot_ref, live_ref, out_ref, dg_ref, cols_ref, grad_ref, z_ref, du_ref, b_ref, cm_ref,
 ):
     n, width = g_ref.shape
     rows = width // PIECES
@@ -754,7 +755,7 @@
 
     zero = jnp.zeros((1, width), f32)
     sums = lax.fori_loop(0, 4, step, (zero, zero, zero))
-    ff_tail(tools, z_ref, du_ref, b_ref, cm_ref, grad_ref, cols_ref, sums, width, blocks)
+    ff_tail(tools, z_ref, du_ref, b_ref, cm_ref, grad_ref, cols_ref, 2, sums, width, blocks)
 
 
 def ff_last(g, wide, vec, cot, live, ff, ident=None):
@@ -762,13 +763,13 @@
     n, d = g.shape
     rows = d // PIECES
     blocks = ff // d
-    outs = (sds((n, d), bf16), sds((n, d), f32))
+    outs = (sds((n, d), bf16), sds((n, d), f32), sds((d, 128), f32))
     specs = [Late(0), Late(1, base, 2 * rows * blocks), full(vec.shape), Late(2), pl.BlockSpec(memory_space=SMEM)]
     scratch = [
         pltpu.VMEM((n, ff), bf16), pltpu.VMEM((n, ff), bf16), pltpu.VMEM((n, d), bf16),
-        pltpu.VMEM((n, d), bf16), pltpu.VMEM((d, 128), f32),
+        pltpu.VMEM((n, d), bf16),
     ]
-    grads = (2 * rows * blocks + 2 * EXTRA, d, 2 * blocks + 1)
+    grads = (2 * rows * blocks, d, 2 * blocks)
     return call(
         ff_last_kernel, "ff_last", (g, wide, vec, cot, live), specs, outs, 12 * n * d * ff, 30 << 20, scratch,
         grads, ident,
@@ -776,7 +777,7 @@
 
 
 def ff_backward_kernel(
-    tools, g_ref, w_ref, vec_ref, c_ref, b_ref, z_ref, s_ref, dg_ref, grad_ref, cm_ref, cols_ref,
+    tools, g_ref, w_ref, vec_ref, c_ref, b_ref, z_ref, s_ref, dg_ref, cols_ref, grad_ref, cm_ref,
 ):
     n, width = g_ref.shape
     rows = width // PIECES
@@ -811,7 +812,7 @@
     zero = jnp.zeros((1, width), f32)
     sums = lax.fori_loop(0, 4, step, (zero, zero, zero))
     tools.wait(5, 4)
-    ff_tail(tools, z_ref, s_ref, b_ref, cm_ref, grad_ref, cols_ref, sums, width, blocks)
+    ff_tail(tools, z_ref, s_ref, b_ref, cm_ref, grad_ref, cols_ref, 1, sums, width, blocks)
     if tools.red is not None:
         tools.red.run(FF_END)
 
@@ -822,10 +823,10 @@
     ff = z.shape[1]
     rows = d // PIECES
     blocks = ff // d
-    outs = (sds((n, d), f32),)
+    outs = (sds((n, d), f32), sds((d, 128), f32))
     specs = [Late(3), Late(1, base, 2 * rows * blocks), full(vec.shape), Late(0), Late(5), Late(4), Late(2)]
-    scratch = [pltpu.VMEM((n, d), bf16), pltpu.VMEM((d, 128), f32)]
-    grads = (2 * rows * blocks + 2 * EXTRA, d, 2 * blocks + 1)
+    scratch = [pltpu.VMEM((n, d), bf16)]
+    grads = (2 * rows * blocks, d, 2 * blocks)
     return call(
         ff_backward_kernel, "ff_backward", (g, wide, vec, c, b, z, s), specs, outs, 8 * n * d * ff, 40 << 20, scratch,
         grads, ident, carry,
@@ -833,7 +834,7 @@
 
 
 def attn_backward_kernel(
-    tools, h_ref, dg_ref, wa_ref, wb_ref, vec_ref, at_ref, qe_ref, ke_ref, ve_ref, ot_ref, ol_ref,
+    tools, h_ref, dg_ref, wa_ref, wb_ref, vec_ref, at_ref, qe_ref, ke_ref, ve_ref, ot_ref, ol_ref, extra_ref,
     c_ref, grad_ref, doe_ref, dq_ref, dk_ref, dv_ref, cols_ref,
 ):
     n, width = h_ref.shape
@@ -889,7 +890,7 @@
         return carry
 
     lax.fori_loop(0, HEADS // UNROLL, some_heads, 0)
-    tools.wait(5, 0, 2)
+    tools.wait(5, 0, 2, 11)
     if red is not None:
         red.run(ATTN_MIDDLE)
     if pair is not None:
@@ -929,7 +930,7 @@
     lane = lax.broadcasted_iota(jnp.int32, (width, 128), 1)
     vt = jnp.where(lane == 3, jnp.sum(joined(dq_ref).astype(f32), axis=1, keepdims=True), vt)
     vt = jnp.where(lane == 4, jnp.sum(joined(dv_ref).astype(f32), axis=1, keepdims=True), vt)
-    cols_ref[...] = vt
+    cols_ref[...] = vt + extra_ref[...]
     put_vectors(grad_ref, 4 * rows, cols_ref, rows)
     if pair is not None:
         pair.send(4, region(4))
@@ -943,7 +944,7 @@
             tail.run([(0, step)])
 
 
-def attn_backward(h, dg, square, vec, kept, ident=None, carry=None, tail=False):
+def attn_backward(h, dg, square, vec, kept, extra, ident=None, carry=None, tail=False):
     (first, base_a), (second, base_b) = square
     n, d = h.shape
     hd = d // HEADS
@@ -951,12 +952,12 @@
     at, qe, ke, ve, ot, ol = kept
     outs = (sds((n, d), f32),)
     specs = [Late(8), Late(0), Late(9, base_a, 2 * rows), Late(2, base_b, 2 * rows), full(vec.shape)]
-    specs += [Late(7), Late(3), Late(4), Late(5), Late(1), Late(6)]
+    specs += [Late(7), Late(3), Late(4), Late(5), Late(1), Late(6), Late(10)]
     scratch = [pltpu.VMEM((HEADS, hd + EXTRA, n), bf16)] + [pltpu.VMEM((HEADS, hd, n), bf16)] * 3
     scratch += [pltpu.VMEM((d, 128), f32)]
     flops = 16 * n * d * d + 5 * HEADS * 2 * n * n * 256
     return call(
-        attn_backward_kernel, "attn_backward", (h, dg, first, second, vec, at, qe, ke, ve, ot, ol), specs, outs, flops, 40 << 20,
+        attn_backward_kernel, "attn_backward", (h, dg, first, second, vec, at, qe, ke, ve, ot, ol, extra), specs, outs, flops, 40 << 20,
         scratch, (4 * rows + 2 * EXTRA, d, 5), ident, carry, tail,
     )
 
@@ -965,6 +966,7 @@
     "ln1_gain", "ln1_bias", "q_weight", "q_bias", "k_weight", "v_weight", "v_bias", "o_weight", "o_bias",
     "ln2_gain", "ln2_bias", "up_weight", "up_bias", "down_weight", "down_bias",
 )
+COLUMN_VECTORS = ("ln1_gain", "ln1_bias", "o_bias", "q_bias", "v_bias", "ln2_gain", "ln2_bias", "down_bias")
 ROW_VECTORS = ("ln1_gain", "ln1_bias", "q_bias", "v_bias", "o_bias", "ln2_gain", "ln2_bias", "down_bias")
 
 
@@ -1080,13 +1082,11 @@
     out["up_weight"] = jnp.concatenate([gw[:, j * per : (j + 1) * per].reshape(d, d) for j in range(blocks)], axis=1)
     out["down_weight"] = gw[:, blocks * per : 2 * blocks * per].reshape(ff, d)
     count = per // (d // 128)
-    vs = gs[:, 4 * per : 4 * per + count].reshape(d, 128)
-    vw = gw[:, 2 * blocks * per : 2 * blocks * per + count].reshape(PIECES, per, 128)
-    for j, x in enumerate(("ln1_gain", "ln1_bias", "o_bias", "q_bias", "v_bias")):
-        out[x] = vs[:, j]
-    for j, x in enumerate(("ln2_gain", "ln2_bias", "down_bias")):
-        out[x] = vw[:, :, j].reshape(d)
-    out["up_bias"] = vw[:, :, 3 : 3 + blocks].transpose(0, 2, 1).reshape(ff)
+    vs = gs[:, 4 * per : 4 * per + count].reshape(PIECES, per, 128)
+    for j, x in enumerate(COLUMN_VECTORS):
+        out[x] = vs[:, :, j].reshape(d)
+    first = len(COLUMN_VECTORS)
+    out["up_bias"] = vs[:, :, first : first + blocks].transpose(0, 2, 1).reshape(ff)
     sums = {}
     for x, g in out.items():
         sums[x] = over_rep(lax.psum_scatter(g, "fsdp", scatter_dimension=0, tiled=True))
@@ -1109,20 +1109,15 @@
         for j in range(blocks):
             outs["up_weight"][l, :, j * width : (j + 1) * width] = wide[j * per : (j + 1) * per, :].astype(f32)
         outs["down_weight"][l] = wide[blocks * per : 2 * blocks * per, :].astype(f32)
-        for ref, base, names in (
-            (square, 4 * per, ("ln1_gain", "ln1_bias", "o_bias", "q_bias", "v_bias")),
-            (wide, 2 * blocks * per, ("ln2_gain", "ln2_bias", "down_bias")),
-        ):
-            for m in range(lanes):
-                part = ref[base : base + per // lanes, m * 128 : (m + 1) * 128].astype(f32)
-                cols_ref[pl.ds(m, per // lanes, stride=lanes), :] = part
-            turned = cols_ref[...].T
-            for j, x in enumerate(names):
-                outs[x][l : l + 1, :] = turned[j : j + 1, :]
-            if ref is wide:
-                for c in range(blocks):
-                    row = turned[len(names) + c : len(names) + c + 1, :]
-                    outs["up_bias"][l : l + 1, c * per : (c + 1) * per] = row
+        for m in range(lanes):
+            part = square[4 * per : 4 * per + per // lanes, m * 128 : (m + 1) * 128].astype(f32)
+            cols_ref[pl.ds(m, per // lanes, stride=lanes), :] = part
+        turned = cols_ref[...].T
+        for j, x in enumerate(COLUMN_VECTORS):
+            outs[x][l : l + 1, :] = turned[j : j + 1, :]
+        for c in range(blocks):
+            j = len(COLUMN_VECTORS) + c
+            outs["up_bias"][l : l + 1, c * per : (c + 1) * per] = turned[j : j + 1, :]
     for move in moves:
         move.wait()
 
@@ -1163,23 +1158,23 @@
     g, *saved = attn_forward(hidden, squares[l], vecs[l], segment)
     if not even:
         whole = lambda x: x.reshape((PIECES,) + x.shape[4:])
-        block_out, grad, gw = ff_last(g, wides[l], vecs[l], cotangent, live, ff)
-        grad, gs = attn_backward(hidden, grad, squares[l], vecs[l], saved)
+        block_out, grad, extra, gw = ff_last(g, wides[l], vecs[l], cotangent, live, ff)
+        grad, gs = attn_backward(hidden, grad, squares[l], vecs[l], saved, extra)
         results = [restack(whole(gs), whole(gw), d, ff)]
         for l in reversed(range(layers - 1)):
             hidden, g, saved, more = kept[l]
-            grad, gw = ff_backward(g, wides[l], vecs[l], grad, *more)
-            grad, gs = attn_backward(hidden, grad, squares[l], vecs[l], saved)
+            grad, extra, gw = ff_backward(g, wides[l], vecs[l], grad, *more)
+            grad, gs = attn_backward(hidden, grad, squares[l], vecs[l], saved, extra)
             results.insert(0, restack(whole(gs), whole(gw), d, ff))
     else:
-        block_out, grad, gw = ff_last(g, wides[l], vecs[l], cotangent, live, ff, 1)
-        grad, gs, rw = attn_backward(hidden, grad, squares[l], vecs[l], saved, 2 + 2 * l, (gw, 2), l == 0)
+        block_out, grad, extra, gw = ff_last(g, wides[l], vecs[l], cotangent, live, ff, 1)
+        grad, gs, rw = attn_backward(hidden, grad, squares[l], vecs[l], saved, extra, 2 + 2 * l, (gw, 2), l == 0)
         pairs = []
         for l in reversed(range(layers - 1)):
             hidden, g, saved, more = kept[l]
-            grad, gw, rs = ff_backward(g, wides[l], vecs[l], grad, *more, ident=3 + 2 * l, carry=(gs, 2))
+            grad, extra, gw, rs = ff_backward(g, wides[l], vecs[l], grad, *more, ident=3 + 2 * l, carry=(gs, 2))
             pairs.insert(0, (rs, rw))
-            grad, gs, rw = attn_backward(hidden, grad, squares[l], vecs[l], saved, 2 + 2 * l, (gw, 2), l == 0)
+            grad, gs, rw = attn_backward(hidden, grad, squares[l], vecs[l], saved, extra, 2 + 2 * l, (gw, 2), l == 0)
         pairs.insert(0, (gs, rw))
         return tuple(finish(block_out, grad, pairs, d, ff))
     return (block_out, grad) + tuple(jnp.stack([r[x] for r in results]) for x in NAMES)

time: 500 us -> 498 us (level)
  no operation moved by 1% of the time
where the time goes in v4:
time: 498 us; the launch traced here: 493 us
  Pallas kernels  471 us (95%)
  between operations  14.7 us (3%)
  local copies, waits for them, and re-layouts  5.12 us (1%)
    pallas_call x6, Pallas kernels, call(): pl.pallas_call(body, name=name, in_specs=base_specs, out_specs=out_specs,...  349 us
    pallas_call x1, Pallas kernels, gathered(): pl.pallas_call(gather_kernel, name='gather', in_specs=[full(x.shape)], ou...  91.2 us
    pallas_call x1, Pallas kernels, ff_forward(): pl.pallas_call(functools.partial(ff_forward_kernel, base), name='ff_forwa...  21.5 us
  transfers between devices with their start and end apart: 1, of which 1 were waited for; matrix products, arithmetic and copies ran while one was open for 0% of the time, Pallas kernels for 26%

profile of v4, /device:TPU:0, one launch (start us, length us, event | category | flops | bytes accessed | tf_op | source)
XLA Modules:
  0.0 493.3 jit_solution(5042065192926234861)
XLA Ops:
  7.2 0.0 all-gather.2.cloned.1.call-start
  7.2 2.9 pack.1
  10.2 0.0 all-gather.2.cloned.1.call-update
  10.2 0.0 copy-start.1
  10.2 1.0 copy-done.1
  11.2 91.2 %gather.1 = bf16[2,2,2,2,320,768]{5,4,3,2,1,0:T(8,128)(2,1)S(1)} custom-call(bf16[320,768]{1,0:T(8,128)(2,1)S(1)} %copy-done.1), custom_call_target="tpu_custom_call" | custom-call | bytes 104857600 | tf_op jit(solution)/shard_map/gather/pallas_call | solution.py:341
  102.5 0.0 copy-start
  102.5 3.1 copy-done
  105.6 0.1 reshape.52
  105.7 0.1 reshape.50
  105.8 0.1 reshape.51
  106.0 0.6 slice_bitcast_fusion
  106.6 35.3 %attn_forward.2 = (f32[1024,768]{1,0:T(8,128)}, bf16[768,1024]{1,0:T(8,128)(2,1)}, bf16[16,64,1024]{2,1,0:T(8,128)(2,1)}, bf16[16,64,1024]{2,1,0:T(8,128)(2,1)},...) custom-call(bf16[1024,768]{1,0:T(8,128)(2,1)} %refs_0_.5, ...), custom_call_target="tpu_custom_call" | custom-call | flops 22011707392 | bytes 31457280 | tf_op jit(solution)/shard_map/attn_forward/pallas_call | solution.py:539
  141.9 2.0 all-gather.2.cloned.1.call-done
  143.9 21.5 %ff_forward.1 = (f32[1024,768]{1,0:T(8,128)}, bf16[1024,768]{1,0:T(8,128)(2,1)}, bf16[1024,3072]{1,0:T(8,128)(2,1)}, bf16[1024,3072]{1,0:T(8,128)(2,1)}) custom-call(f32[1024,768]{1,0:T(8,128)} %get-tuple-element.52.g_ref.refs_0_, bf16[16,864,768]{2,1,0:T(8,128)(2,1)} %bitcast.22, f32[12,768]{1,0:T(8,128)} %get-tuple-element.86.refs_3_.vec_ref.refs_2_.refs_4_), custom_call_target="tpu_custom_call" | custom-call | flops 9663676416 | bytes 31457280 | tf_op jit(solution)/shard_map/ff_forward/pallas_call | solution.py:624
  165.5 35.3 %attn_forward.3 = (f32[1024,768]{1,0:T(8,128)}, bf16[768,1024]{1,0:T(8,128)(2,1)}, bf16[16,64,1024]{2,1,0:T(8,128)(2,1)}, bf16[16,64,1024]{2,1,0:T(8,128)(2,1)},...) custom-call(f32[1024,768]{1,0:T(8,128)} %get-tuple-element.54.refs_0_, ...), custom_call_target="tpu_custom_call" | custom-call | flops 22011707392 | bytes 31457280 | tf_op jit(solution)/shard_map/attn_forward/pallas_call | solution.py:539
  200.8 49.3 %ff_last.1 = (bf16[1024,768]{1,0:T(8,128)(2,1)}, f32[1024,768]{1,0:T(8,128)}, f32[768,128]{1,0:T(8,128)}, bf16[2,2,2,384,768]{4,3,2,1,0:T(8,128)(2,1)}) custom-call(f32[1024,768]{1,0:T(8,128)} %get-tuple-element.55.refs_0_, bf16[16,864,768]{2,1,0:T(8,128)(2,1)} %bitcast.24, f32[12,768]{1,0:T(8,128)} %get-tuple-element.85.refs_3_.refs_2_.refs_4_, ...), custom_call_target="tpu_custom_call" | custom-call | flops 28991029248 | bytes 31457280 | tf_op jit(solution)/shard_map/ff_last/pallas_call | solution.py:539
  250.1 72.0 %attn_backward.2 = (f32[1024,768]{1,0:T(8,128)}, bf16[2,2,2,224,768]{4,3,2,1,0:T(8,128)(2,1)}, bf16[384,768]{1,0:T(8,128)(2,1)}) custom-call(f32[1024,768]{1,0:T(8,128)} %get-tuple-element.54.refs_0_, f32[1024,768]{1,0:T(8,128)} %get-tuple-element.57.refs_1_, bf16[16,320,768]{2,1,0:T(8,128)(2,1)} %bitcast.18, bf16[16,864,768]{2,1,0:T(8,128)(2,1)} %bitcast.25, ...), custom_call_target="tpu_custom_call" | custom-call | flops 52613349376 | bytes 41943040 | tf_op jit(solution)/shard_map/attn_backward/pallas_call | solution.py:539
  322.1 51.7 %ff_backward.1 = (f32[1024,768]{1,0:T(8,128)}, f32[768,128]{1,0:T(8,128)}, bf16[2,2,2,384,768]{4,3,2,1,0:T(8,128)(2,1)}, bf16[224,768]{1,0:T(8,128)(2,1)}) custom-call(f32[1024,768]{1,0:T(8,128)} %get-tuple-element.52.g_ref.refs_0_, bf16[16,864,768]{2,1,0:T(8,128)(2,1)} %bitcast.26, f32[12,768]{1,0:T(8,128)} %get-tuple-element.86.refs_3_.vec_ref.refs_2_.refs_4_, ...), custom_call_target="tpu_custom_call" | custom-call | flops 19327352832 | bytes 41943040 | tf_op jit(solution)/shard_map/ff_backward/pallas_call | solution.py:539
  373.8 105.2 %attn_backward.3 = (f32[1024,768]{1,0:T(8,128)}, bf16[224,768]{1,0:T(8,128)(2,1)}, bf16[384,768]{1,0:T(8,128)(2,1)}) custom-call(bf16[1024,768]{1,0:T(8,128)(2,1)} %refs_0_.5, f32[1024,768]{1,0:T(8,128)} %get-tuple-element.71.refs_1_, bf16[16,320,768]{2,1,0:T(8,128)(2,1)} %bitcast.19, bf16[16,320,768]{2,1,0:T(8,128)(2,1)} %bitcast.20, ...), custom_call_target="tpu_custom_call" | custom-call | flops 52613349376 | bytes 41943040 | tf_op jit(solution)/shard_map/attn_backward/pallas_call | solution.py:539
  479.0 6.9 %finish.1 = (bf16[1024,768]{1,0:T(8,128)(2,1)}, f32[1024,768]{1,0:T(8,128)}, f32[2,48]{1,0:T(2,128)}, f32[2,48]{1,0:T(2,128)}, f32[2,48,768]{2,1,0:T(8,128)}, /*...) custom-call(bf16[1024,768]{1,0:T(8,128)(2,1)} %get-tuple-element.56., ...), custom_call_target="tpu_custom_call" | custom-call | tf_op jit(solution)/shard_map/finish/pallas_call | solution.py:1132
  (5 shorter events, 0.1 us)
Async XLA Ops:
  7.2 136.8 %all-gather.2.cloned.1.call-start = ((), (), s32[]{:S(2)}) async-start(), calls=%async_computation | async-start | bytes 22560768 | tf_op jit(solution)/shard_map/all_gather | solution.py:974
  10.2 1.0 copy-start.1
  102.5 3.1 copy-start
Sparse Core Ops, SparseCore 0:
  10.3 133.5 all-gather.1

commit v5 on v4

--- a/solution.py
+++ b/solution.py
@@ -23,7 +23,7 @@
 ATTN_MIDDLE = [(1, 3), (0, 4)]
 ATTN_TILES = {0: [(0, 5)], 1: [(1, 4)]}
 ATTN_END = [(1, 5)]
-FF_TILES = {7: [(0, 1)], 13: [(1, 1), (0, 2)]}
+FF_TILES = {6: [(0, 1)], 14: [(1, 1), (0, 2)]}
 FF_BLOCKS = {1: [(0, 3), (1, 2)], 4: [(0, 4), (1, 3)], 7: [(0, 5), (1, 4)]}
 FF_END = [(1, 5)]
 VMEM_BYTES = 60 * 1024 * 1024
@@ -671,14 +671,14 @@
                 pair.settle(k, where)
 
     def block(j, carry):
-        advance_at(tools.red, 2 * j, FF_BLOCKS)
+        advance_at(tools.red, j, {at // 2: m for at, m in FF_BLOCKS.items() if at % 2 == 0})
         cols = pl.ds(pl.multiple_of(j * width, 128), width)
         (kd, where_d), (ku, where_u) = regions(j)
         dwd = mm_tn(z_ref[:, cols], cm_ref[...]).reshape(2, 2, rows * blocks, width)
         grad_ref[lax.div(j, 2), lax.rem(j, 2), :, :, lower, :] = dwd.astype(bf16)
         if pair is not None:
             pair.send(kd, where_d)
-        advance_at(tools.red, 2 * j + 1, FF_BLOCKS)
+        advance_at(tools.red, j, {at // 2: m for at, m in FF_BLOCKS.items() if at % 2 == 1})
         dwu = mm_tn(b_ref[...], du_ref[:, cols])
         grad_ref[:, :, :, :, where_u[3], :] = dwu.reshape(2, 2, 2, 2, rows, width).astype(bf16)
         if pair is not None:
@@ -796,7 +796,7 @@
         db = jnp.zeros((tile, width), f32)
         for j in range(blocks):
             cols = slice(j * width, (j + 1) * width)
-            advance_at(tools.red, t * blocks + j, FF_TILES)
+            advance_at(tools.red, t, {at // blocks: m for at, m in FF_TILES.items() if at % blocks == j})
             w = weight(w_ref, j, rows)
             wd = down(w_ref, j, rows, blocks)
             du = (s_ref[span, cols].astype(f32) * mm_nt(cm, wd)).astype(bf16)

time: 498 us -> 497 us (level)
  no operation moved by 1% of the time
where the time goes in v5:
time: 497 us; the launch traced here: 492 us
  Pallas kernels  470 us (95%)
  between operations  14.7 us (3%)
  local copies, waits for them, and re-layouts  5.12 us (1%)
    pallas_call x6, Pallas kernels, call(): pl.pallas_call(body, name=name, in_specs=base_specs, out_specs=out_specs,...  348 us
    pallas_call x1, Pallas kernels, gathered(): pl.pallas_call(gather_kernel, name='gather', in_specs=[full(x.shape)], ou...  91.2 us
    pallas_call x1, Pallas kernels, ff_forward(): pl.pallas_call(functools.partial(ff_forward_kernel, base), name='ff_forwa...  21.5 us
  transfers between devices with their start and end apart: 1, of which 1 were waited for; matrix products, arithmetic and copies ran while one was open for 0% of the time, Pallas kernels for 26%

profile of v5, /device:TPU:0, one launch (start us, length us, event | category | flops | bytes accessed | tf_op | source)
XLA Modules:
  0.0 492.2 jit_solution(8715625289125017588)
XLA Ops:
  7.2 0.0 all-gather.2.cloned.1.call-start
  7.2 2.9 pack.1
  10.2 0.0 all-gather.2.cloned.1.call-update
  10.2 0.0 copy-start.1
  10.2 1.0 copy-done.1
  11.2 91.2 %gather.1 = bf16[2,2,2,2,320,768]{5,4,3,2,1,0:T(8,128)(2,1)S(1)} custom-call(bf16[320,768]{1,0:T(8,128)(2,1)S(1)} %copy-done.1), custom_call_target="tpu_custom_call" | custom-call | bytes 104857600 | tf_op jit(solution)/shard_map/gather/pallas_call | solution.py:341
  102.5 0.0 copy-start
  102.5 3.1 copy-done
  105.6 0.1 reshape.52
  105.7 0.1 reshape.50
  105.8 0.1 reshape.51
  106.0 0.6 slice_bitcast_fusion
  106.6 35.3 %attn_forward.2 = (f32[1024,768]{1,0:T(8,128)}, bf16[768,1024]{1,0:T(8,128)(2,1)}, bf16[16,64,1024]{2,1,0:T(8,128)(2,1)}, bf16[16,64,1024]{2,1,0:T(8,128)(2,1)},...) custom-call(bf16[1024,768]{1,0:T(8,128)(2,1)} %refs_0_.5, ...), custom_call_target="tpu_custom_call" | custom-call | flops 22011707392 | bytes 31457280 | tf_op jit(solution)/shard_map/attn_forward/pallas_call | solution.py:539
  141.9 2.0 all-gather.2.cloned.1.call-done
  143.9 21.5 %ff_forward.1 = (f32[1024,768]{1,0:T(8,128)}, bf16[1024,768]{1,0:T(8,128)(2,1)}, bf16[1024,3072]{1,0:T(8,128)(2,1)}, bf16[1024,3072]{1,0:T(8,128)(2,1)}) custom-call(f32[1024,768]{1,0:T(8,128)} %get-tuple-element.52.g_ref.refs_0_, bf16[16,864,768]{2,1,0:T(8,128)(2,1)} %bitcast.22, f32[12,768]{1,0:T(8,128)} %get-tuple-element.86.refs_3_.vec_ref.refs_2_.refs_4_), custom_call_target="tpu_custom_call" | custom-call | flops 9663676416 | bytes 31457280 | tf_op jit(solution)/shard_map/ff_forward/pallas_call | solution.py:624
  165.5 35.3 %attn_forward.3 = (f32[1024,768]{1,0:T(8,128)}, bf16[768,1024]{1,0:T(8,128)(2,1)}, bf16[16,64,1024]{2,1,0:T(8,128)(2,1)}, bf16[16,64,1024]{2,1,0:T(8,128)(2,1)},...) custom-call(f32[1024,768]{1,0:T(8,128)} %get-tuple-element.54.refs_0_, ...), custom_call_target="tpu_custom_call" | custom-call | flops 22011707392 | bytes 31457280 | tf_op jit(solution)/shard_map/attn_forward/pallas_call | solution.py:539
  200.8 49.3 %ff_last.1 = (bf16[1024,768]{1,0:T(8,128)(2,1)}, f32[1024,768]{1,0:T(8,128)}, f32[768,128]{1,0:T(8,128)}, bf16[2,2,2,384,768]{4,3,2,1,0:T(8,128)(2,1)}) custom-call(f32[1024,768]{1,0:T(8,128)} %get-tuple-element.55.refs_0_, bf16[16,864,768]{2,1,0:T(8,128)(2,1)} %bitcast.24, f32[12,768]{1,0:T(8,128)} %get-tuple-element.85.refs_3_.refs_2_.refs_4_, ...), custom_call_target="tpu_custom_call" | custom-call | flops 28991029248 | bytes 31457280 | tf_op jit(solution)/shard_map/ff_last/pallas_call | solution.py:539
  250.1 72.0 %attn_backward.2 = (f32[1024,768]{1,0:T(8,128)}, bf16[2,2,2,224,768]{4,3,2,1,0:T(8,128)(2,1)}, bf16[384,768]{1,0:T(8,128)(2,1)}) custom-call(f32[1024,768]{1,0:T(8,128)} %get-tuple-element.54.refs_0_, f32[1024,768]{1,0:T(8,128)} %get-tuple-element.57.refs_1_, bf16[16,320,768]{2,1,0:T(8,128)(2,1)} %bitcast.18, bf16[16,864,768]{2,1,0:T(8,128)(2,1)} %bitcast.25, ...), custom_call_target="tpu_custom_call" | custom-call | flops 52613349376 | bytes 41943040 | tf_op jit(solution)/shard_map/attn_backward/pallas_call | solution.py:539
  322.1 50.8 %ff_backward.1 = (f32[1024,768]{1,0:T(8,128)}, f32[768,128]{1,0:T(8,128)}, bf16[2,2,2,384,768]{4,3,2,1,0:T(8,128)(2,1)}, bf16[224,768]{1,0:T(8,128)(2,1)}) custom-call(f32[1024,768]{1,0:T(8,128)} %get-tuple-element.52.g_ref.refs_0_, bf16[16,864,768]{2,1,0:T(8,128)(2,1)} %bitcast.26, f32[12,768]{1,0:T(8,128)} %get-tuple-element.86.refs_3_.vec_ref.refs_2_.refs_4_, ...), custom_call_target="tpu_custom_call" | custom-call | flops 19327352832 | bytes 41943040 | tf_op jit(solution)/shard_map/ff_backward/pallas_call | solution.py:539
  372.8 105.1 %attn_backward.3 = (f32[1024,768]{1,0:T(8,128)}, bf16[224,768]{1,0:T(8,128)(2,1)}, bf16[384,768]{1,0:T(8,128)(2,1)}) custom-call(bf16[1024,768]{1,0:T(8,128)(2,1)} %refs_0_.5, f32[1024,768]{1,0:T(8,128)} %get-tuple-element.71.refs_1_, bf16[16,320,768]{2,1,0:T(8,128)(2,1)} %bitcast.19, bf16[16,320,768]{2,1,0:T(8,128)(2,1)} %bitcast.20, ...), custom_call_target="tpu_custom_call" | custom-call | flops 52613349376 | bytes 41943040 | tf_op jit(solution)/shard_map/attn_backward/pallas_call | solution.py:539
  477.9 6.9 %finish.1 = (bf16[1024,768]{1,0:T(8,128)(2,1)}, f32[1024,768]{1,0:T(8,128)}, f32[2,48]{1,0:T(2,128)}, f32[2,48]{1,0:T(2,128)}, f32[2,48,768]{2,1,0:T(8,128)}, /*...) custom-call(bf16[1024,768]{1,0:T(8,128)(2,1)} %get-tuple-element.56., ...), custom_call_target="tpu_custom_call" | custom-call | tf_op jit(solution)/shard_map/finish/pallas_call | solution.py:1132
  (5 shorter events, 0.1 us)
Async XLA Ops:
  7.2 136.8 %all-gather.2.cloned.1.call-start = ((), (), s32[]{:S(2)}) async-start(), calls=%async_computation | async-start | bytes 22560768 | tf_op jit(solution)/shard_map/all_gather | solution.py:974
  10.2 1.0 copy-start.1
  102.5 3.1 copy-start
Sparse Core Ops, SparseCore 0:
  10.3 133.5 all-gather.1
